TPU v7x, 32 devices: a whole 2x2x4 slice. The times are simulated.
32 devices in a mesh: ta: 8 (over y, x, core), site: 4 (over z).
Axes of the slice: x: 2, y: 2, z: 4, core: 2. Of those that a mesh axis runs over, the one named last changes fastest.
Arguments:
- eigenvectors: bfloat16 [16, 192, 3, 4, 256], P('ta', None, None, 'site'), parts along dimension 0, may hold values from -6 to 6
- gauge_links: bfloat16 [16, 3, 3, 3, 4, 256], P('ta', None, None, None, 'site'), parts along dimension 0, may hold values from -2.5 to 2.5
- displacements: int32 [2, 3], replicated, may hold values from 0 to 3, as said below
- block_rows: int32 [4], replicated, may hold values from 0 to 191
Outputs:
- elementals: float32 [16, 4, 192, 384], P('ta', None, 'site'), parts along dimension 0
There are 8 independent parts, one for each index of `ta`. A program takes and returns all parts, laid end to end along the dimension named above; an argument that names none is the same for every part. Nothing has to cross between parts.
Inputs may be any that keep to these rules, and one draw needn't show every extreme that they name: `displacements`: each combination displaces at least one of its three vectors along the third dimension.
All inputs are finite; a program needn't handle non-finite values.
Results may differ from a plain program's by a relative error of at most 0.012.
Values may be sent and summed in bfloat16 or wider, within the bound.
No kernel may reach another device: no remote copies, remote signals or barrier semaphores. Data moves between devices by JAX's collectives and lax.ppermute only.
A program may use at most 64 MiB of HBM per device.

v0:
```python
import functools
import math

import jax
import jax.numpy as jnp
from jax import lax
from jax.experimental import pallas as pl
from jax.experimental.pallas import tpu as pltpu
from jax.sharding import PartitionSpec as P

LX = 16
COLORS = 3
TILE = 16
LANES = 128
SUBLANES = 8


def shifted(block, axis, distance):
    count = lax.axis_size(axis)
    return lax.ppermute(block, axis, [(i, (i + distance) % count) for i in range(count)])


def shift_matrix(direction, sites, width_x):
    source = lax.broadcasted_iota(jnp.int32, (sites, sites), 0)
    target = lax.broadcasted_iota(jnp.int32, (sites, sites), 1)
    column = lax.rem(target, width_x)
    along_x = target - column + lax.rem(column + 1, width_x)
    along_y = lax.rem(target + width_x, sites)
    neighbour = jnp.where(direction == 1, along_x, jnp.where(direction == 2, along_y, target))
    return jnp.where(source == neighbour, 1.0, 0.0).astype(jnp.bfloat16)


def mul(left, right):
    return left[0] * right[0] - left[1] * right[1], left[0] * right[1] + left[1] * right[0]


def add(left, right):
    return left[0] + right[0], left[1] + right[1]


def plane_of(here_ref, next_ref, direction, index):
    return jnp.where(direction == 3, next_ref[index], here_ref[index])


def chosen_link(links_ref, direction):
    which = jnp.maximum(direction - 1, 0)
    resting = direction == 0

    def entry(row, column):
        at = 2 * (COLORS * row + column)
        re = links_ref[which, at : at + 1, :]
        im = links_ref[which, at + 1 : at + 2, :]
        unit = jnp.full_like(re, 1.0 if row == column else 0.0)
        return jnp.where(resting, unit, re), jnp.where(resting, jnp.zeros_like(im), im)

    return [[entry(row, column) for column in range(COLORS)] for row in range(COLORS)]


def site_matrices(combo, moves, rows, here_ref, next_ref, links_ref, matrices_ref, scale, width_x):
    vectors, sites = here_ref.shape[-2:]
    direction = moves[combo, 0]
    picks = matrices_ref.shape[2]
    numbers = lax.broadcasted_iota(jnp.int32, (picks, vectors), 1)
    lane = lax.broadcasted_iota(jnp.int32, (picks, vectors), 0)
    wanted = jnp.full((picks, vectors), -1, jnp.int32)
    for i in range(rows.shape[0]):
        wanted = jnp.where(lane == i, rows[i], wanted)
    select = jnp.where(numbers == wanted, 1.0, 0.0).astype(jnp.bfloat16)
    shift = shift_matrix(direction, sites, width_x)

    def moved(part, color):
        picked = jnp.dot(
            select,
            plane_of(here_ref, next_ref, direction, (part, color)),
            preferred_element_type=jnp.float32,
        ).astype(jnp.bfloat16)
        return jnp.dot(picked, shift, preferred_element_type=jnp.float32)

    fields = [(moved(0, color), moved(1, color)) for color in range(COLORS)]
    first, second, third = (chosen_link(links_ref, moves[combo, slot]) for slot in range(3))

    def total(terms):
        return functools.reduce(add, terms)

    left = [
        total(mul(first[a][b], fields[b]) for b in range(COLORS)) for a in range(COLORS)
    ]
    for column in range(COLORS):
        after = []
        for b in range(COLORS):
            up, down = (b + 1) % COLORS, (b + 2) % COLORS
            plus = mul(third[up][column], left[down])
            minus = mul(third[down][column], left[up])
            after.append((plus[0] - minus[0], plus[1] - minus[1]))
        for row in range(COLORS):
            re, im = total(mul(second[b][row], after[b]) for b in range(COLORS))
            at = 2 * (COLORS * column + row)
            matrices_ref[combo, at] = re * scale
            matrices_ref[combo, at + 1] = im * scale


def right_operand(combo, moves, here_ref, next_ref, right_ref, width_x):
    vectors, sites = here_ref.shape[-2:]
    direction = moves[combo, 2]
    shift = shift_matrix(direction, sites, width_x)
    half = COLORS * sites
    for color in range(COLORS):
        at = color * sites
        re, im = (
            jnp.dot(
                plane_of(here_ref, next_ref, direction, (part, color)),
                shift,
                preferred_element_type=jnp.float32,
            )
            for part in range(2)
        )
        kind = right_ref.dtype
        right_ref[combo, :vectors, at : at + sites] = re.astype(kind)
        right_ref[combo, vectors:, half + at : half + at + sites] = re.astype(kind)
        right_ref[combo, :vectors, half + at : half + at + sites] = (-im).astype(kind)
        right_ref[combo, vectors:, at : at + sites] = im.astype(kind)


def row_block(combo, start, moves, here_ref, next_ref, matrices_ref, right_ref, mid_ref, crossed_ref, out_ref, width_x):
    sites = here_ref.shape[-1]
    picks, count = out_ref.shape[1:3]
    direction = moves[combo, 1]
    shift = shift_matrix(direction, sites, width_x)
    rows = pl.ds(pl.multiple_of(start, TILE), count)
    block = plane_of(here_ref, next_ref, direction, (slice(None), slice(None), rows))
    mid_ref[...] = jnp.dot(
        block.reshape(2 * COLORS * count, sites), shift, preferred_element_type=jnp.float32
    )
    for lanes in range(sites // LANES):
        across = slice(lanes * LANES, (lanes + 1) * LANES)
        for pick in range(picks):
            entries = [
                jnp.broadcast_to(matrices_ref[combo, at, pick : pick + 1, across], (TILE, LANES))
                for at in range(2 * COLORS * COLORS)
            ]
            for tile in range(count // TILE):
                field = [
                    tuple(
                        mid_ref[pl.ds((part * COLORS + color) * count + tile * TILE, TILE), across]
                        for part in range(2)
                    )
                    for color in range(COLORS)
                ]
                for column in range(COLORS):
                    re, im = functools.reduce(
                        add,
                        (
                            mul(
                                (
                                    entries[2 * (COLORS * column + row)],
                                    entries[2 * (COLORS * column + row) + 1],
                                ),
                                field[row],
                            )
                            for row in range(COLORS)
                        ),
                    )
                    down = slice(pick * count + tile * TILE, pick * count + (tile + 1) * TILE)
                    at = column * sites + lanes * LANES
                    crossed_ref[down, at : at + LANES] = re.astype(jnp.bfloat16)
                    at += COLORS * sites
                    crossed_ref[down, at : at + LANES] = im.astype(jnp.bfloat16)
    result = lax.dot_general(
        crossed_ref[...],
        right_ref[combo],
        (((1,), (1,)), ((), ())),
        preferred_element_type=jnp.float32,
    )
    out_ref[combo] = result.reshape(out_ref.shape[1:]).astype(out_ref.dtype)


def first_kernel(scale, width_x, starts, moves, rows, here_ref, next_ref, links_ref, right_ref, matrices_ref, out_ref, mid_ref, crossed_ref):
    def step(combo, carry):
        site_matrices(combo, moves, rows, here_ref, next_ref, links_ref, matrices_ref, scale, width_x)
        right_operand(combo, moves, here_ref, next_ref, right_ref, width_x)
        row_block(combo, starts[0], moves, here_ref, next_ref, matrices_ref, right_ref, mid_ref, crossed_ref, out_ref, width_x)
        return carry

    lax.fori_loop(0, out_ref.shape[0], step, 0)


def later_kernel(width_x, starts, moves, here_ref, next_ref, right_ref, matrices_ref, *rest):
    *outs, mid_ref, crossed_ref = rest

    def step(combo, carry):
        for number, out_ref in enumerate(outs):
            row_block(combo, starts[number], moves, here_ref, next_ref, matrices_ref, right_ref, mid_ref, crossed_ref, out_ref, width_x)
        return carry

    lax.fori_loop(0, outs[0].shape[0], step, 0)


def on_device(eigenvectors, gauge_links, displacements, block_rows):
    parts, vectors, colors, planes, sites = eigenvectors.shape
    ring = lax.axis_size("site")
    me = lax.axis_index("site")
    combos, picks = displacements.shape[0], block_rows.shape[0]
    count = vectors // ring
    sites_all = planes * ring * sites
    scale = 1.0 / math.sqrt(24.0 * sites_all)
    here = jnp.transpose(eigenvectors, (0, 2, 3, 1, 4)).reshape(parts, colors, vectors, sites)
    after = shifted(here, "site", -1)
    links = jnp.transpose(gauge_links, (1, 2, 3, 0, 4, 5)).astype(jnp.float32)
    links = links.reshape(COLORS, colors * colors * parts, sites)

    def chunk(kind):
        return jax.ShapeDtypeStruct((combos, picks, count, 2 * vectors), kind)

    def starts(offsets):
        return jnp.stack([lax.rem(me + offset, ring) * count for offset in offsets]).astype(jnp.int32)

    smem = pl.BlockSpec(memory_space=pltpu.SMEM)
    vmem = pl.BlockSpec(memory_space=pltpu.VMEM)
    scratch = [
        pltpu.VMEM((parts * colors * count, sites), jnp.float32),
        pltpu.VMEM((picks * count, parts * colors * sites), jnp.bfloat16),
    ]
    offsets = [ring // 2] + [o for o in range(1, ring) if o != ring // 2]
    right, matrices, sent = pl.pallas_call(
        functools.partial(first_kernel, scale, LX),
        out_shape=(
            jax.ShapeDtypeStruct((combos, 2 * vectors, parts * colors * sites), jnp.bfloat16),
            jax.ShapeDtypeStruct((combos, 2 * colors * colors, SUBLANES, sites), jnp.float32),
            chunk(jnp.bfloat16),
        ),
        in_specs=[smem, smem, smem, vmem, vmem, vmem],
        out_specs=(vmem, vmem, vmem),
        scratch_shapes=scratch,
        name="first",
    )(starts(offsets[:1]), displacements, block_rows, here, after, links)
    arrived = [shifted(sent, "site", offsets[0])]
    later = pl.pallas_call(
        functools.partial(later_kernel, LX),
        out_shape=tuple(chunk(jnp.bfloat16) for _ in offsets[1:]) + (chunk(jnp.float32),),
        in_specs=[smem, smem, vmem, vmem, vmem, vmem],
        out_specs=(vmem,) * len(offsets),
        scratch_shapes=scratch,
        cost_estimate=pl.CostEstimate(flops=4_000_000_000, bytes_accessed=8_000_000, transcendentals=0),
        name="later",
    )(starts(offsets[1:] + [0]), displacements, here, after, right, matrices)
    arrived += [shifted(block, "site", offset) for block, offset in zip(later[:-1], offsets[1:])]
    return functools.reduce(lambda total, block: total + block.astype(jnp.float32), arrived, later[-1])


def solution(mesh):
    return jax.shard_map(
        on_device,
        mesh=mesh,
        in_specs=(
            P("ta", None, None, "site", None),
            P("ta", None, None, None, "site", None),
            P(),
            P(),
        ),
        out_specs=P("ta", None, "site", None),
        check_vma=False,
    )
```

profile of v0, /device:TPU:0, one launch (start us, length us, event | category | flops | bytes accessed | tf_op | source)
XLA Modules:
  0.0 63.8 jit_solution(16914203468002585151)
XLA Ops:
  0.0 5.1 %collective-permute-start = (bf16[2,3,192,256]{3,2,1,0:T(8,128)(2,1)}, bf16[2,3,192,256]{3,2,1,0:T(8,128)(2,1)S(1)}, u32[]{:S(2)}, u32[]{:S(2)}) collective-permute-start(bf16[2,3,192,256]{3,2,1,0:T(8,128)(2,1)} %bitcast.13), channel_id=1, source_target_pairs={{0,3},{1,0},{2,1},{3,2},{4,7},{5,4},{6,5},{7,6},{8,11},{9,8},{10,9... | collective-permute-start | bytes 1769480 | tf_op jit(solution)/shard_map/ppermute | solution.py:20
  5.1 0.8 %convert_bitcast_fusion = f32[3,3,3,2,1,256]{5,3,4,2,1,0:T(2,128)S(1)} fusion(bf16[2,3,3,3,1,256]{5,0,4,3,2,1:T(2,128)(2,1)} %param.5), kind=kLoop, calls=%fused_computation.1 | loop fusion | flops 13824 | bytes 82944 | tf_op jit(solution)/shard_map/reshape | solution.py:209
  5.8 0.7 %reshape.12.links_ref = f32[3,18,256]{2,1,0:T(8,128)} reshape(f32[3,3,3,2,1,256]{5,3,4,2,1,0:T(2,128)S(1)} %convert_bitcast_fusion) | data formatting | bytes 110592 | tf_op jit(solution)/shard_map/reshape | solution.py:209
  6.5 0.6 pad_add_fusion.starts
  7.1 10.9 %collective-permute-done.next_ref = bf16[2,3,192,256]{3,2,1,0:T(8,128)(2,1)S(1)} collective-permute-done((bf16[2,3,192,256]{3,2,1,0:T(8,128)(2,1)}, bf16[2,3,192,256]{3,2,1,0:T(8,128)(2,1)S(1)}, u32[]{:S(2)}, u32[]{:S(2)}) %collective-permute-start) | collective-permute-done | bytes 589856 | tf_op jit(solution)/shard_map/ppermute | solution.py:20
  18.0 0.0 copy-start
  18.0 0.8 %copy-done = bf16[2,3,192,256]{3,2,1,0:T(8,128)(2,1)} copy-done((bf16[2,3,192,256]{3,2,1,0:T(8,128)(2,1)}, bf16[2,3,192,256]{3,2,1,0:T(8,128)(2,1)S(1)}, u32[]{:S(2)}) %copy-start) | copy-done | bytes 589848
  18.8 5.4 %first.1 = (bf16[2,384,1536]{2,1,0:T(8,128)(2,1)}, f32[2,18,8,256]{3,2,1,0:T(8,128)}, bf16[2,4,48,384]{3,2,1,0:T(8,128)(2,1)}) custom-call(s32[1]{0:T(128)} %bitcast.8.starts, s32[2,3]{1,0:T(2,128)} %moves.3, s32[4]{0:T(128)} %rows.1, bf16[2,3,192,256]{3,2,1,0:T(8,128)(2,1)} %bitcast.14, bf16[2,3,192,256]{3,2,1,0:T(8,128)(2,1)} %copy-done, ...), custom_call_target="tpu_custom_call" | custom-call | tf_op jit(solution)/shard_map/first/pallas_call | solution.py:224
  24.2 0.0 copy-start.1
  24.2 8.1 %later.1 = (bf16[2,4,48,384]{3,2,1,0:T(8,128)(2,1)}, bf16[2,4,48,384]{3,2,1,0:T(8,128)(2,1)}, f32[2,4,48,384]{3,2,1,0:T(8,128)}) custom-call(s32[3]{0:T(128)} %pad_add_fusion.starts, s32[2,3]{1,0:T(2,128)} %moves.3, bf16[2,3,192,256]{3,2,1,0:T(8,128)(2,1)} %bitcast.15, bf16[2,3,192,256]{3,2,1,0:T(8,128)(2,1)} %copy-done, ...), custom_call_target="tpu_custom_call" | custom-call | flops 4000000000 | bytes 8000000 | tf_op jit(solution)/shard_map/later/pallas_call | solution.py:237
  32.3 0.4 collective-permute-start.2
  32.6 3.8 %collective-permute-start.3 = (bf16[2,4,48,384]{3,2,1,0:T(8,128)(2,1)}, bf16[2,4,48,384]{3,2,1,0:T(8,128)(2,1)S(1)}, u32[]{:S(2)}, u32[]{:S(2)}) collective-permute-start(bf16[2,4,48,384]{3,2,1,0:T(8,128)(2,1)} %get-tuple-element.16), channel_id=1, source_target_pairs={{0,3},{1,0},{2,1},{3,2},{4,7},{5,4},{6,5},{7,6},{8,11},{9,8},{10,9... | collective-permute-start | bytes 884744 | tf_op jit(solution)/shard_map/ppermute | solution.py:20
  36.4 0.0 copy-done.1
  36.5 0.6 collective-permute-start.1
  37.0 7.5 %collective-permute-done.2 = bf16[2,4,48,384]{3,2,1,0:T(8,128)(2,1)S(1)} collective-permute-done((bf16[2,4,48,384]{3,2,1,0:T(8,128)(2,1)}, bf16[2,4,48,384]{3,2,1,0:T(8,128)(2,1)S(1)}, u32[]{:S(2)}, u32[]{:S(2)}) %collective-permute-start.2) | collective-permute-done | bytes 294944 | tf_op jit(solution)/shard_map/ppermute | solution.py:20
  44.6 2.2 %collective-permute-done.3 = bf16[2,4,48,384]{3,2,1,0:T(8,128)(2,1)S(1)} collective-permute-done((bf16[2,4,48,384]{3,2,1,0:T(8,128)(2,1)}, bf16[2,4,48,384]{3,2,1,0:T(8,128)(2,1)S(1)}, u32[]{:S(2)}, u32[]{:S(2)}) %collective-permute-start.3) | collective-permute-done | bytes 294944 | tf_op jit(solution)/shard_map/ppermute | solution.py:20
  46.8 15.0 %collective-permute-done.1 = bf16[2,4,48,384]{3,2,1,0:T(8,128)(2,1)S(1)} collective-permute-done((bf16[2,4,48,384]{3,2,1,0:T(8,128)(2,1)S(1)}, bf16[2,4,48,384]{3,2,1,0:T(8,128)(2,1)S(1)}, u32[]{:S(2)}, u32[]{:S(2)}) %collective-permute-start.1) | collective-permute-done | bytes 294944 | tf_op jit(solution)/shard_map/ppermute | solution.py:20
  61.8 2.0 %convert_add_fusion = f32[2,4,48,384]{3,2,1,0:T(8,128)} fusion(bf16[2,4,48,384]{3,2,1,0:T(8,128)(2,1)S(1)} %collective-permute-done.3, bf16[2,4,48,384]{3,2,1,0:T(8,128)(2,1)S(1)} %collective-permute-done.2, f32[2,4,48,384]{3,2,1,0:T(8,128)} %get-tuple-element.13, bf16[2,4,48,384]{3,2,1,0:T(8,128)(2,1)S(1)} %collective-permute-done.1), kind=kLoop, calls=%fused_computation | loop fusion | flops 884736 | bytes 2064384 | tf_op jit(solution)/shard_map/add | solution.py:247
Async XLA Ops:
  0.0 18.0 %collective-permute-start = (bf16[2,3,192,256]{3,2,1,0:T(8,128)(2,1)}, bf16[2,3,192,256]{3,2,1,0:T(8,128)(2,1)S(1)}, u32[]{:S(2)}, u32[]{:S(2)}) collective-permute-start(bf16[2,3,192,256]{3,2,1,0:T(8,128)(2,1)} %bitcast.13), channel_id=1, source_target_pairs={{0,3},{1,0},{2,1},{3,2},{4,7},{5,4},{6,5},{7,6},{8,11},{9,8},{10,9... | collective-permute-start | bytes 1769480 | tf_op jit(solution)/shard_map/ppermute | solution.py:20
  18.0 0.8 %copy-start = (bf16[2,3,192,256]{3,2,1,0:T(8,128)(2,1)}, bf16[2,3,192,256]{3,2,1,0:T(8,128)(2,1)S(1)}, u32[]{:S(2)}) copy-start(bf16[2,3,192,256]{3,2,1,0:T(8,128)(2,1)S(1)} %collective-permute-done.next_ref) | copy-start | bytes 1769476
  24.2 12.2 %copy-start.1 = (bf16[2,4,48,384]{3,2,1,0:T(8,128)(2,1)S(1)}, bf16[2,4,48,384]{3,2,1,0:T(8,128)(2,1)}, u32[]{:S(2)}) copy-start(bf16[2,4,48,384]{3,2,1,0:T(8,128)(2,1)} %get-tuple-element.14) | copy-start | bytes 884740
  32.3 12.3 %collective-permute-start.2 = (bf16[2,4,48,384]{3,2,1,0:T(8,128)(2,1)}, bf16[2,4,48,384]{3,2,1,0:T(8,128)(2,1)S(1)}, u32[]{:S(2)}, u32[]{:S(2)}) collective-permute-start(bf16[2,4,48,384]{3,2,1,0:T(8,128)(2,1)} %get-tuple-element.15), channel_id=1, source_target_pairs={{0,1},{1,2},{2,3},{3,0},{4,5},{5,6},{6,7},{7,4},{8,9},{9,10},{10,1... | collective-permute-start | bytes 884744 | tf_op jit(solution)/shard_map/ppermute | solution.py:20
  32.6 14.1 %collective-permute-start.3 = (bf16[2,4,48,384]{3,2,1,0:T(8,128)(2,1)}, bf16[2,4,48,384]{3,2,1,0:T(8,128)(2,1)S(1)}, u32[]{:S(2)}, u32[]{:S(2)}) collective-permute-start(bf16[2,4,48,384]{3,2,1,0:T(8,128)(2,1)} %get-tuple-element.16), channel_id=1, source_target_pairs={{0,3},{1,0},{2,1},{3,2},{4,7},{5,4},{6,5},{7,6},{8,11},{9,8},{10,9... | collective-permute-start | bytes 884744 | tf_op jit(solution)/shard_map/ppermute | solution.py:20
  36.5 25.3 %collective-permute-start.1 = (bf16[2,4,48,384]{3,2,1,0:T(8,128)(2,1)S(1)}, bf16[2,4,48,384]{3,2,1,0:T(8,128)(2,1)S(1)}, u32[]{:S(2)}, u32[]{:S(2)}) collective-permute-start(bf16[2,4,48,384]{3,2,1,0:T(8,128)(2,1)S(1)} %copy-done.1), channel_id=1, source_target_pairs={{0,2},{1,3},{2,0},{3,1},{4,6},{5,7},{6,4},{7,5},{8,10},{9,11},{10,... | collective-permute-start | bytes 884744 | tf_op jit(solution)/shard_map/ppermute | solution.py:20
where the time goes:
time: 64 us; the launch traced here: 63.8 us
  waiting for transfers between devices  35.6 us (56%)
  Pallas kernels  13.5 us (21%)
  starting transfers between devices  9.81 us (15%)
  other arithmetic  3.34 us (5%)
  local copies, waits for them, and re-layouts  1.48 us (2%)
    ppermute x4, waiting for transfers between devices, shifted(): lax.ppermute(block, axis, [(i, (i + distance) % count) for i in range(cou...  35.6 us
    ppermute x4, starting transfers between devices, shifted(): lax.ppermute(block, axis, [(i, (i + distance) % count) for i in range(cou...  9.81 us
    pallas_call x1, Pallas kernels, on_device(): pl.pallas_call(functools.partial(later_kernel, LX), out_shape=tuple((chun...  8.08 us
    pallas_call x1, Pallas kernels, on_device(): pl.pallas_call(functools.partial(first_kernel, scale, LX), out_shape=(jax...  5.41 us
    add x1, other arithmetic, on_device(): total + block.astype(jnp.float32)  2 us
  transfers between devices with their start and end apart: 4, of which 4 were waited for; matrix products, arithmetic and copies ran while one was open for 3% of the time, Pallas kernels for 0%

commit v1 on v0

v1 whole, which is shorter than its diff:
```python
import functools
import math

import jax
import jax.numpy as jnp
from jax import lax
from jax.experimental import pallas as pl
from jax.experimental.pallas import tpu as pltpu
from jax.sharding import PartitionSpec as P


LX = 16
COLORS = 3
TILE = 16
LANES = 128
SUBLANES = 8
VMEM_BYTES = 24 * 2**20


def shifted(block, axis, distance):
    count = lax.axis_size(axis)
    return lax.ppermute(block, axis, [(i, (i + distance) % count) for i in range(count)])


def shift_matrices(sites, width_x):
    source = lax.broadcasted_iota(jnp.int32, (COLORS, sites, sites), 1)
    target = lax.broadcasted_iota(jnp.int32, (COLORS, sites, sites), 2)
    direction = lax.broadcasted_iota(jnp.int32, (COLORS, sites, sites), 0)
    column = lax.rem(target, width_x)
    along_x = target - column + lax.rem(column + 1, width_x)
    along_y = lax.rem(target + width_x, sites)
    neighbour = jnp.where(direction == 1, along_x, jnp.where(direction == 2, along_y, target))
    return jnp.where(source == neighbour, 1.0, 0.0).astype(jnp.bfloat16)


def in_plane(shifts_ref, direction):
    return shifts_ref[jnp.where(direction == 3, 0, direction)]


def mul(left, right):
    return left[0] * right[0] - left[1] * right[1], left[0] * right[1] + left[1] * right[0]


def add(left, right):
    return left[0] + right[0], left[1] + right[1]


def plane_of(here_ref, next_ref, direction, index):
    return jnp.where(direction == 3, next_ref[index], here_ref[index])


def chosen_link(links_ref, direction):
    which = jnp.maximum(direction - 1, 0)
    resting = direction == 0

    def entry(row, column):
        at = 2 * (COLORS * row + column)
        re = links_ref[which, at : at + 1, :]
        im = links_ref[which, at + 1 : at + 2, :]
        unit = jnp.full_like(re, 1.0 if row == column else 0.0)
        return jnp.where(resting, unit, re), jnp.where(resting, jnp.zeros_like(im), im)

    return [[entry(row, column) for column in range(COLORS)] for row in range(COLORS)]


def site_matrices(combo, moves, rows, here_ref, next_ref, links_ref, shifts_ref, matrices_ref, scale):
    vectors = here_ref.shape[-2]
    direction = moves[combo, 0]
    picks = matrices_ref.shape[2]
    numbers = lax.broadcasted_iota(jnp.int32, (picks, vectors), 1)
    lane = lax.broadcasted_iota(jnp.int32, (picks, vectors), 0)
    wanted = jnp.full((picks, vectors), -1, jnp.int32)
    for i in range(rows.shape[0]):
        wanted = jnp.where(lane == i, rows[i], wanted)
    select = jnp.where(numbers == wanted, 1.0, 0.0).astype(jnp.bfloat16)

    def picked(part, color):
        return jnp.dot(
            select,
            plane_of(here_ref, next_ref, direction, (part, color)),
            preferred_element_type=jnp.float32,
        )

    stacked = jnp.concatenate(
        [picked(part, color) for color in range(COLORS) for part in range(2)], axis=0
    )
    stacked = jnp.dot(
        stacked.astype(jnp.bfloat16), in_plane(shifts_ref, direction), preferred_element_type=jnp.float32
    )
    fields = [
        tuple(stacked[at * picks : (at + 1) * picks] for at in (2 * color, 2 * color + 1))
        for color in range(COLORS)
    ]
    first, second, third = (chosen_link(links_ref, moves[combo, slot]) for slot in range(3))

    def total(terms):
        return functools.reduce(add, terms)

    left = [
        total(mul(first[a][b], fields[b]) for b in range(COLORS)) for a in range(COLORS)
    ]
    left = [(re * scale, im * scale) for re, im in left]
    for column in range(COLORS):
        after = []
        for b in range(COLORS):
            up, down = (b + 1) % COLORS, (b + 2) % COLORS
            plus = mul(third[up][column], left[down])
            minus = mul(third[down][column], left[up])
            after.append((plus[0] - minus[0], plus[1] - minus[1]))
        for row in range(COLORS):
            re, im = total(mul(second[b][row], after[b]) for b in range(COLORS))
            at = COLORS * (COLORS * column + row)
            matrices_ref[combo, at] = re + im
            matrices_ref[combo, at + 1] = re
            matrices_ref[combo, at + 2] = im


def right_operand(combo, moves, here_ref, next_ref, shifts_ref, right_ref):
    vectors, sites = here_ref.shape[-2:]
    direction = moves[combo, 2]
    shift = in_plane(shifts_ref, direction)
    kind = right_ref.dtype
    for color in range(COLORS):
        re, im = (
            jnp.dot(
                plane_of(here_ref, next_ref, direction, (part, color)),
                shift,
                preferred_element_type=jnp.float32,
            )
            for part in range(2)
        )
        of_re = slice(2 * color * sites, (2 * color + 1) * sites)
        of_im = slice((2 * color + 1) * sites, (2 * color + 2) * sites)
        right_ref[combo, :vectors, of_re] = re.astype(kind)
        right_ref[combo, vectors:, of_im] = re.astype(kind)
        right_ref[combo, :vectors, of_im] = (-im).astype(kind)
        right_ref[combo, vectors:, of_re] = im.astype(kind)


def row_block(combo, start, moves, here_ref, next_ref, shifts_ref, matrices_ref, right_ref, mid_ref, crossed_ref, out_ref):
    sites = here_ref.shape[-1]
    picks, count = out_ref.shape[1:3]
    direction = moves[combo, 1]
    rows = pl.ds(pl.multiple_of(start, TILE), count)
    block = plane_of(here_ref, next_ref, direction, (slice(None), slice(None), rows))
    half = COLORS * count
    both = jnp.dot(
        block.reshape(2 * half, sites), in_plane(shifts_ref, direction), preferred_element_type=jnp.float32
    )
    re, im = both[:half], both[half:]
    mid_ref[:half] = re
    mid_ref[half : 2 * half] = im - re
    mid_ref[2 * half :] = re + im
    result = None
    for column in range(COLORS):
        for lanes in range(sites // LANES):
            across = slice(lanes * LANES, (lanes + 1) * LANES)
            for tile in range(count // TILE):
                field = [
                    [
                        mid_ref[pl.ds(kind * half + row * count + tile * TILE, TILE), across]
                        for kind in range(3)
                    ]
                    for row in range(COLORS)
                ]
                for pick in range(picks):
                    sums = [None] * 3
                    for row in range(COLORS):
                        at = COLORS * (COLORS * column + row)
                        for kind in range(3):
                            entry = jnp.broadcast_to(
                                matrices_ref[combo, at + kind, pick : pick + 1, across], (TILE, LANES)
                            )
                            term = entry * field[row][kind]
                            sums[kind] = term if row == 0 else sums[kind] + term
                    down = slice(pick * count + tile * TILE, pick * count + (tile + 1) * TILE)
                    at = 2 * column * sites + lanes * LANES
                    crossed_ref[down, at : at + LANES] = (sums[0] - sums[2]).astype(jnp.bfloat16)
                    at += sites
                    crossed_ref[down, at : at + LANES] = (sums[0] + sums[1]).astype(jnp.bfloat16)
        deep = slice(2 * column * sites, 2 * (column + 1) * sites)
        part = lax.dot_general(
            crossed_ref[:, deep],
            right_ref[combo, :, deep],
            (((1,), (1,)), ((), ())),
            preferred_element_type=jnp.float32,
        )
        result = part if result is None else result + part
    out_ref[combo] = result.reshape(out_ref.shape[1:]).astype(out_ref.dtype)


def first_kernel(scale, starts, moves, rows, here_ref, next_ref, links_ref, shifts_ref, right_ref, matrices_ref, out_ref, mid_ref, crossed_ref):
    combos = range(out_ref.shape[0])
    for combo in combos:
        site_matrices(combo, moves, rows, here_ref, next_ref, links_ref, shifts_ref, matrices_ref, scale)
    for combo in combos:
        right_operand(combo, moves, here_ref, next_ref, shifts_ref, right_ref)
        row_block(combo, starts[0], moves, here_ref, next_ref, shifts_ref, matrices_ref, right_ref, mid_ref.at[combo], crossed_ref.at[combo], out_ref)


def later_kernel(starts, moves, here_ref, next_ref, shifts_ref, right_ref, matrices_ref, *rest):
    *outs, mid_ref, crossed_ref = rest

    def step(combo, carry):
        for number, out_ref in enumerate(outs):
            row_block(combo, starts[number], moves, here_ref, next_ref, shifts_ref, matrices_ref, right_ref, mid_ref.at[number], crossed_ref.at[number], out_ref)
        return carry

    lax.fori_loop(0, outs[0].shape[0], step, 0)


def local_work(eigenvectors, gauge_links, displacements, block_rows):
    parts, vectors, colors, planes, sites = eigenvectors.shape
    ring = lax.axis_size("site")
    me = lax.axis_index("site")
    combos, picks = displacements.shape[0], block_rows.shape[0]
    count = vectors // ring
    scale = 1.0 / math.sqrt(24.0 * planes * ring * sites)
    here = jnp.transpose(eigenvectors, (0, 2, 3, 1, 4)).reshape(parts, colors, vectors, sites)
    after = shifted(here, "site", -1)
    links = jnp.transpose(gauge_links, (1, 2, 3, 0, 4, 5)).astype(jnp.float32)
    links = links.reshape(COLORS, colors * colors * parts, sites)
    shifts = shift_matrices(sites, LX)

    def chunk(kind):
        return jax.ShapeDtypeStruct((combos, picks, count, 2 * vectors), kind)

    def starts(owners):
        return jnp.stack([owner * count for owner in owners]).astype(jnp.int32)

    smem = pl.BlockSpec(memory_space=pltpu.SMEM)
    vmem = pl.BlockSpec(memory_space=pltpu.VMEM)

    def scratch(blocks):
        return [
            pltpu.VMEM((blocks, 3 * colors * count, sites), jnp.float32),
            pltpu.VMEM((blocks, picks * count, parts * colors * sites), jnp.bfloat16),
        ]

    folded = ring == 4
    if folded:
        owners = [ring - 1 - me, lax.rem(me + 2, ring), me + 1 - 2 * lax.rem(me, 2), me]
    else:
        owners = [lax.rem(me + offset, ring) for offset in range(1, ring + 1)]
    right, matrices, sent = pl.pallas_call(
        functools.partial(first_kernel, scale),
        out_shape=(
            jax.ShapeDtypeStruct((combos, 2 * vectors, parts * colors * sites), jnp.bfloat16),
            jax.ShapeDtypeStruct((combos, 3 * colors * colors, SUBLANES, sites), jnp.float32),
            chunk(jnp.bfloat16),
        ),
        in_specs=[smem, smem, smem, vmem, vmem, vmem, vmem],
        out_specs=(vmem, vmem, vmem),
        scratch_shapes=scratch(combos),
        compiler_params=pltpu.CompilerParams(vmem_limit_bytes=VMEM_BYTES),
        name="first",
    )(starts(owners[:1]), displacements, block_rows, here, after, links, shifts)
    others = pl.pallas_call(
        later_kernel,
        out_shape=tuple(chunk(jnp.bfloat16) for _ in owners[1:-1]) + (chunk(jnp.float32),),
        in_specs=[smem, smem, vmem, vmem, vmem, vmem, vmem],
        out_specs=(vmem,) * (ring - 1),
        scratch_shapes=scratch(ring - 1),
        compiler_params=pltpu.CompilerParams(vmem_limit_bytes=VMEM_BYTES),
        cost_estimate=pl.CostEstimate(flops=3_000_000_000, bytes_accessed=8_000_000, transcendentals=0),
        name="later",
    )(starts(owners[1:]), displacements, here, after, shifts, right, matrices)
    if not folded:
        blocks = [sent, *others[:-1]]
        arrived = [shifted(block, "site", offset + 1) for offset, block in enumerate(blocks)]
        return functools.reduce(lambda total, block: total + block.astype(jnp.float32), arrived, others[-1])
    last = ring - 1
    passed = lax.ppermute(sent, "site", [(0, 1), (last, last - 1)])
    near = lax.ppermute(sent, "site", [(1, 2), (2, 1)])
    paired = lax.ppermute(others[1], "site", [(0, 1), (1, 0), (2, 3), (3, 2)])
    far = shifted(others[0] + passed, "site", 2)
    held = others[2] + near.astype(jnp.float32) + paired.astype(jnp.float32)
    held = lax.optimization_barrier(held)
    return held + far.astype(jnp.float32)


def solution(mesh):
    return jax.shard_map(
        local_work,
        mesh=mesh,
        in_specs=(
            P("ta", None, None, "site", None),
            P("ta", None, None, None, "site", None),
            P(),
            P(),
        ),
        out_specs=P("ta", None, "site", None),
        check_vma=False,
    )
```

time: 64 us -> 58.2 us (0.909)
  waiting for transfers between devices: 35.6 us -> 30 us
  Pallas kernels: 13.5 us -> 8.37 us
  starting transfers between devices: 9.81 us -> 13.1 us
  local copies, waits for them, and re-layouts: 1.48 us -> 4.17 us
  other arithmetic: 3.34 us -> 2.13 us
    ppermute x4 -> x2, waiting for transfers between devices: 35.6 us -> 28.2 us  [shifted(): lax.ppermute(block, axis, [(i, (i + distance) % count) for i in range(cou...]
    pallas_call x2, Pallas kernels: 13.5 us -> 8.37 us  [the longest x1 5.33 us: local_work(): pl.pallas_call(later_kernel, out_shape=tuple((chunk(jnp.bfloat16) for _ i...]
    unnamed x4 -> x10, local copies, waits for them, and re-layouts: 0.82 us -> 4.13 us
    ppermute x0 -> x3, starting transfers between devices: none -> 3.02 us  [the longest x1 2.27 us: local_work(): passed = lax.ppermute(sent, 'site', [(0, 1), (last, last - 1)])]
    ppermute x0 -> x3, waiting for transfers between devices: none -> 1.78 us  [the longest x1 1.77 us: local_work(): paired = lax.ppermute(others[1], 'site', [(0, 1), (1, 0), (2, 3), (3, 2)])]
    add x1 -> x4, other arithmetic: 2 us -> 1.08 us  [the longest x1 0.88 us: local_work(): return held + far.astype(jnp.float32)]
    ppermute x4 -> x2, starting transfers between devices: 9.81 us -> 10.1 us  [shifted(): lax.ppermute(block, axis, [(i, (i + distance) % count) for i in range(cou...]
  transfers between devices with their start and end apart: 4 -> 5, of which waited for: 4 -> 3; matrix products, arithmetic and copies ran while one was open for 3% -> 2% of each run, Pallas kernels for 0% -> 9%
where the time goes in v1:
time: 58.2 us; the launch traced here: 57.9 us
  waiting for transfers between devices  30 us (52%)
  starting transfers between devices  13.1 us (23%)
  Pallas kernels  8.37 us (14%)
  local copies, waits for them, and re-layouts  4.17 us (7%)
  other arithmetic  2.13 us (4%)
    ppermute x2, waiting for transfers between devices, shifted(): lax.ppermute(block, axis, [(i, (i + distance) % count) for i in range(cou...  28.2 us
    ppermute x2, starting transfers between devices, shifted(): lax.ppermute(block, axis, [(i, (i + distance) % count) for i in range(cou...  10.1 us
    pallas_call x1, Pallas kernels, local_work(): pl.pallas_call(later_kernel, out_shape=tuple((chunk(jnp.bfloat16) for _ i...  5.33 us
    unnamed x10, local copies, waits for them, and re-layouts  4.13 us
    pallas_call x1, Pallas kernels, local_work(): pl.pallas_call(functools.partial(first_kernel, scale), out_shape=(jax.Sha...  3.03 us
    ppermute x1, starting transfers between devices, local_work(): passed = lax.ppermute(sent, 'site', [(0, 1), (last, last - 1)])  2.27 us
    ppermute x1, waiting for transfers between devices, local_work(): paired = lax.ppermute(others[1], 'site', [(0, 1), (1, 0), (2, 3), (3, 2)])  1.77 us
  transfers between devices with their start and end apart: 5, of which 3 were waited for; matrix products, arithmetic and copies ran while one was open for 2% of the time, Pallas kernels for 9%

profile of v1, /device:TPU:0, one launch (start us, length us, event | category | flops | bytes accessed | tf_op | source)
XLA Modules:
  0.0 57.9 jit_solution(1467341982821352701)
XLA Ops:
  0.0 5.1 %collective-permute-start = (bf16[2,3,192,256]{3,2,1,0:T(8,128)(2,1)}, bf16[2,3,192,256]{3,2,1,0:T(8,128)(2,1)S(1)}, u32[]{:S(2)}, u32[]{:S(2)}) collective-permute-start(bf16[2,3,192,256]{3,2,1,0:T(8,128)(2,1)} %bitcast.13), channel_id=1, source_target_pairs={{0,3},{1,0},{2,1},{3,2},{4,7},{5,4},{6,5},{7,6},{8,11},{9,8},{10,9... | collective-permute-start | bytes 1769480 | tf_op jit(solution)/shard_map/ppermute | solution.py:22
  5.1 0.8 %convert_bitcast_fusion = f32[3,3,3,2,1,256]{5,3,4,2,1,0:T(2,128)S(1)} fusion(bf16[2,3,3,3,1,256]{5,0,4,3,2,1:T(2,128)(2,1)} %param.5), kind=kLoop, calls=%fused_computation.7 | loop fusion | flops 13824 | bytes 82944 | tf_op jit(solution)/shard_map/reshape | solution.py:222
  5.8 0.1 pad_add_fusion.starts
  6.0 0.2 select_convert_fusion.shifts_ref
  6.2 11.8 %collective-permute-done.next_ref = bf16[2,3,192,256]{3,2,1,0:T(8,128)(2,1)S(1)} collective-permute-done((bf16[2,3,192,256]{3,2,1,0:T(8,128)(2,1)}, bf16[2,3,192,256]{3,2,1,0:T(8,128)(2,1)S(1)}, u32[]{:S(2)}, u32[]{:S(2)}) %collective-permute-start) | collective-permute-done | bytes 589856 | tf_op jit(solution)/shard_map/ppermute | solution.py:22
  18.0 0.0 copy-start
  18.0 1.1 %copy-done = bf16[2,192,3,1,256]{4,1,3,2,0:T(8,128)(2,1)S(1)} copy-done((bf16[2,192,3,1,256]{4,1,3,2,0:T(8,128)(2,1)S(1)}, bf16[2,192,3,1,256]{4,1,3,2,0:T(8,128)(2,1)}, u32[]{:S(2)}) %copy-start) | copy-done | bytes 589848
  19.0 0.0 copy-start.2
  19.0 0.7 %copy-done.2 = s32[2,3]{1,0:T(2,128)S(1)} copy-done((s32[2,3]{1,0:T(2,128)S(1)}, s32[2,3]{1,0:T(2,128)}, u32[]{:S(2)}) %copy-start.2) | copy-done | bytes 48
  19.7 0.0 copy-start.4
  19.7 0.7 %copy-done.4 = s32[4]{0:T(128)S(1)} copy-done((s32[4]{0:T(128)S(1)}, s32[4]{0:T(128)}, u32[]{:S(2)}) %copy-start.4) | copy-done | bytes 40
  20.4 3.0 %first.1 = (bf16[2,384,1536]{2,1,0:T(8,128)(2,1)S(1)}, f32[2,27,8,256]{3,2,1,0:T(8,128)S(1)}, bf16[2,4,48,384]{3,2,1,0:T(8,128)(2,1)S(1)}) custom-call(s32[1]{0:T(128)} %bitcast.8.starts, s32[2,3]{1,0:T(2,128)S(1)} %copy-done.2, s32[4]{0:T(128)S(1)} %copy-done.4, bf16[2,3,192,256]{3,2,1,0:T(8,128)(2,1)S(1)} %bitcast.14, ...), custom_call_target="tpu_custom_call" | custom-call | tf_op jit(solution)/shard_map/first/pallas_call | solution.py:245
  23.4 2.3 %collective-permute-start.3 = (bf16[2,4,48,384]{3,2,1,0:T(8,128)(2,1)S(1)}, bf16[2,4,48,384]{3,2,1,0:T(8,128)(2,1)S(1)}, u32[]{:S(2)}, u32[]{:S(2)}) collective-permute-start(bf16[2,4,48,384]{3,2,1,0:T(8,128)(2,1)S(1)} %get-tuple-element.14), channel_id=1, source_target_pairs={{0,1},{3,2},{4,5},{7,6},{8,9},{11,10},{12,13},{15,14},{16,17},{19,... | collective-permute-start | bytes 884744 | tf_op jit(solution)/shard_map/ppermute | solution.py:273
  25.7 0.0 copy-start.1
  25.7 1.1 %copy-done.1 = bf16[2,192,3,1,256]{4,1,3,2,0:T(8,128)(2,1)S(1)} copy-done((bf16[2,192,3,1,256]{4,1,3,2,0:T(8,128)(2,1)S(1)}, bf16[2,192,3,1,256]{4,1,3,2,0:T(8,128)(2,1)}, u32[]{:S(2)}) %copy-start.1) | copy-done | bytes 589848
  26.8 0.0 copy-start.3
  26.8 0.7 %copy-done.3 = s32[2,3]{1,0:T(2,128)S(1)} copy-done((s32[2,3]{1,0:T(2,128)S(1)}, s32[2,3]{1,0:T(2,128)}, u32[]{:S(2)}) %copy-start.3) | copy-done | bytes 48
  27.4 5.3 %later.1 = (bf16[2,4,48,384]{3,2,1,0:T(8,128)(2,1)S(1)}, bf16[2,4,48,384]{3,2,1,0:T(8,128)(2,1)S(1)}, f32[2,4,48,384]{3,2,1,0:T(8,128)S(1)}) custom-call(s32[3]{0:T(128)S(1)} %pad_add_fusion.starts, s32[2,3]{1,0:T(2,128)S(1)} %copy-done.3, bf16[2,3,192,256]{3,2,1,0:T(8,128)(2,1)S(1)} %bitcast.15, bf16[2,3,192,256]{3,2,1,0:T(8,128)(2,1)S(1)} %collective-permute-done.next_ref, ...), custom_call_target="tpu_custom_call" | custom-call | flops 3000000000 | bytes 8000000 | tf_op jit(solution)/shard_map/later/pallas_call | solution.py:258
  32.8 0.1 collective-permute-start.2
  32.9 0.7 %collective-permute-start.1 = (bf16[2,4,48,384]{3,2,1,0:T(8,128)(2,1)S(1)}, bf16[2,4,48,384]{3,2,1,0:T(8,128)(2,1)S(1)}, u32[]{:S(2)}, u32[]{:S(2)}) collective-permute-start(bf16[2,4,48,384]{3,2,1,0:T(8,128)(2,1)S(1)} %get-tuple-element.14), channel_id=1, source_target_pairs={{1,2},{2,1},{5,6},{6,5},{9,10},{10,9},{13,14},{14,13},{17,18},{18,... | collective-permute-start | bytes 884744 | tf_op jit(solution)/shard_map/ppermute | solution.py:274
  33.6 0.0 collective-permute-done.3
  33.6 0.1 add.42
  33.6 5.0 %collective-permute-start.4 = (bf16[2,4,48,384]{3,2,1,0:T(8,128)(2,1)S(1)}, bf16[2,4,48,384]{3,2,1,0:T(8,128)(2,1)S(1)}, u32[]{:S(2)}, u32[]{:S(2)}) collective-permute-start(bf16[2,4,48,384]{3,2,1,0:T(8,128)(2,1)S(1)} %add.42), channel_id=1, source_target_pairs={{0,2},{1,3},{2,0},{3,1},{4,6},{5,7},{6,4},{7,5},{8,10},{9,11},{10,... | collective-permute-start | bytes 884744 | tf_op jit(solution)/shard_map/ppermute | solution.py:22
  38.7 1.8 %collective-permute-done.2 = bf16[2,4,48,384]{3,2,1,0:T(8,128)(2,1)S(1)} collective-permute-done((bf16[2,4,48,384]{3,2,1,0:T(8,128)(2,1)S(1)}, bf16[2,4,48,384]{3,2,1,0:T(8,128)(2,1)S(1)}, u32[]{:S(2)}, u32[]{:S(2)}) %collective-permute-start.2) | collective-permute-done | bytes 294944 | tf_op jit(solution)/shard_map/ppermute | solution.py:275
  40.5 0.0 collective-permute-done.1
  40.5 0.1 convert_add_fusion.1
  40.6 16.4 %collective-permute-done.4 = bf16[2,4,48,384]{3,2,1,0:T(8,128)(2,1)S(1)} collective-permute-done((bf16[2,4,48,384]{3,2,1,0:T(8,128)(2,1)S(1)}, bf16[2,4,48,384]{3,2,1,0:T(8,128)(2,1)S(1)}, u32[]{:S(2)}, u32[]{:S(2)}) %collective-permute-start.4) | collective-permute-done | bytes 294944 | tf_op jit(solution)/shard_map/ppermute | solution.py:22
  57.0 0.9 %convert_add_fusion = f32[2,4,48,384]{3,2,1,0:T(8,128)} fusion(f32[2,4,48,384]{3,2,1,0:T(8,128)S(1)} %convert_add_fusion.1, bf16[2,4,48,384]{3,2,1,0:T(8,128)(2,1)S(1)} %collective-permute-done.4), kind=kLoop, calls=%fused_computation.5 | loop fusion | flops 294912 | bytes 1474560 | tf_op jit(solution)/shard_map/add | solution.py:279
  (5 shorter events, 0.1 us)
Async XLA Ops:
  0.0 18.0 %collective-permute-start = (bf16[2,3,192,256]{3,2,1,0:T(8,128)(2,1)}, bf16[2,3,192,256]{3,2,1,0:T(8,128)(2,1)S(1)}, u32[]{:S(2)}, u32[]{:S(2)}) collective-permute-start(bf16[2,3,192,256]{3,2,1,0:T(8,128)(2,1)} %bitcast.13), channel_id=1, source_target_pairs={{0,3},{1,0},{2,1},{3,2},{4,7},{5,4},{6,5},{7,6},{8,11},{9,8},{10,9... | collective-permute-start | bytes 1769480 | tf_op jit(solution)/shard_map/ppermute | solution.py:22
  18.0 1.1 %copy-start = (bf16[2,192,3,1,256]{4,1,3,2,0:T(8,128)(2,1)S(1)}, bf16[2,192,3,1,256]{4,1,3,2,0:T(8,128)(2,1)}, u32[]{:S(2)}) copy-start(bf16[2,192,3,1,256]{4,1,3,2,0:T(8,128)(2,1)} %param.4) | copy-start | bytes 1769476
  19.0 0.7 %copy-start.2 = (s32[2,3]{1,0:T(2,128)S(1)}, s32[2,3]{1,0:T(2,128)}, u32[]{:S(2)}) copy-start(s32[2,3]{1,0:T(2,128)} %moves.3) | copy-start | bytes 76
  19.7 0.7 %copy-start.4 = (s32[4]{0:T(128)S(1)}, s32[4]{0:T(128)}, u32[]{:S(2)}) copy-start(s32[4]{0:T(128)} %rows.1) | copy-start | bytes 52
  23.4 10.1 %collective-permute-start.3 = (bf16[2,4,48,384]{3,2,1,0:T(8,128)(2,1)S(1)}, bf16[2,4,48,384]{3,2,1,0:T(8,128)(2,1)S(1)}, u32[]{:S(2)}, u32[]{:S(2)}) collective-permute-start(bf16[2,4,48,384]{3,2,1,0:T(8,128)(2,1)S(1)} %get-tuple-element.14), channel_id=1, source_target_pairs={{0,1},{3,2},{4,5},{7,6},{8,9},{11,10},{12,13},{15,14},{16,17},{19,... | collective-permute-start | bytes 884744 | tf_op jit(solution)/shard_map/ppermute | solution.py:273
  25.7 1.1 %copy-start.1 = (bf16[2,192,3,1,256]{4,1,3,2,0:T(8,128)(2,1)S(1)}, bf16[2,192,3,1,256]{4,1,3,2,0:T(8,128)(2,1)}, u32[]{:S(2)}) copy-start(bf16[2,192,3,1,256]{4,1,3,2,0:T(8,128)(2,1)} %param.4) | copy-start | bytes 1769476
  26.8 0.7 %copy-start.3 = (s32[2,3]{1,0:T(2,128)S(1)}, s32[2,3]{1,0:T(2,128)}, u32[]{:S(2)}) copy-start(s32[2,3]{1,0:T(2,128)} %moves.3) | copy-start | bytes 76
  32.8 7.7 %collective-permute-start.2 = (bf16[2,4,48,384]{3,2,1,0:T(8,128)(2,1)S(1)}, bf16[2,4,48,384]{3,2,1,0:T(8,128)(2,1)S(1)}, u32[]{:S(2)}, u32[]{:S(2)}) collective-permute-start(bf16[2,4,48,384]{3,2,1,0:T(8,128)(2,1)S(1)} %get-tuple-element.15), channel_id=1, source_target_pairs={{0,1},{1,0},{2,3},{3,2},{4,5},{5,4},{6,7},{7,6},{8,9},{9,8},{10,11... | collective-permute-start | bytes 884744 | tf_op jit(solution)/shard_map/ppermute | solution.py:275
  32.9 7.6 %collective-permute-start.1 = (bf16[2,4,48,384]{3,2,1,0:T(8,128)(2,1)S(1)}, bf16[2,4,48,384]{3,2,1,0:T(8,128)(2,1)S(1)}, u32[]{:S(2)}, u32[]{:S(2)}) collective-permute-start(bf16[2,4,48,384]{3,2,1,0:T(8,128)(2,1)S(1)} %get-tuple-element.14), channel_id=1, source_target_pairs={{1,2},{2,1},{5,6},{6,5},{9,10},{10,9},{13,14},{14,13},{17,18},{18,... | collective-permute-start | bytes 884744 | tf_op jit(solution)/shard_map/ppermute | solution.py:274
  33.6 23.4 %collective-permute-start.4 = (bf16[2,4,48,384]{3,2,1,0:T(8,128)(2,1)S(1)}, bf16[2,4,48,384]{3,2,1,0:T(8,128)(2,1)S(1)}, u32[]{:S(2)}, u32[]{:S(2)}) collective-permute-start(bf16[2,4,48,384]{3,2,1,0:T(8,128)(2,1)S(1)} %add.42), channel_id=1, source_target_pairs={{0,2},{1,3},{2,0},{3,1},{4,6},{5,7},{6,4},{7,5},{8,10},{9,11},{10,... | collective-permute-start | bytes 884744 | tf_op jit(solution)/shard_map/ppermute | solution.py:22

commit v2 on v1

--- a/solution.py
+++ b/solution.py
@@ -14,7 +14,7 @@
 TILE = 16
 LANES = 128
 SUBLANES = 8
-VMEM_BYTES = 24 * 2**20
+VMEM_BYTES = 16 * 2**20
 
 
 def shifted(block, axis, distance):
@@ -66,7 +66,7 @@
 def site_matrices(combo, moves, rows, here_ref, next_ref, links_ref, shifts_ref, matrices_ref, scale):
     vectors = here_ref.shape[-2]
     direction = moves[combo, 0]
-    picks = matrices_ref.shape[2]
+    kept, picks = matrices_ref.shape[2], SUBLANES
     numbers = lax.broadcasted_iota(jnp.int32, (picks, vectors), 1)
     lane = lax.broadcasted_iota(jnp.int32, (picks, vectors), 0)
     wanted = jnp.full((picks, vectors), -1, jnp.int32)
@@ -110,34 +110,35 @@
         for row in range(COLORS):
             re, im = total(mul(second[b][row], after[b]) for b in range(COLORS))
             at = COLORS * (COLORS * column + row)
-            matrices_ref[combo, at] = re + im
-            matrices_ref[combo, at + 1] = re
-            matrices_ref[combo, at + 2] = im
+            matrices_ref[combo, at] = (re + im)[:kept]
+            matrices_ref[combo, at + 1] = re[:kept]
+            matrices_ref[combo, at + 2] = im[:kept]
 
 
 def right_operand(combo, moves, here_ref, next_ref, shifts_ref, right_ref):
     vectors, sites = here_ref.shape[-2:]
     direction = moves[combo, 2]
     shift = in_plane(shifts_ref, direction)
-    kind = right_ref.dtype
     for color in range(COLORS):
-        re, im = (
-            jnp.dot(
+        for part in range(2):
+            field = jnp.dot(
                 plane_of(here_ref, next_ref, direction, (part, color)),
                 shift,
                 preferred_element_type=jnp.float32,
             )
-            for part in range(2)
-        )
-        of_re = slice(2 * color * sites, (2 * color + 1) * sites)
-        of_im = slice((2 * color + 1) * sites, (2 * color + 2) * sites)
-        right_ref[combo, :vectors, of_re] = re.astype(kind)
-        right_ref[combo, vectors:, of_im] = re.astype(kind)
-        right_ref[combo, :vectors, of_im] = (-im).astype(kind)
-        right_ref[combo, vectors:, of_re] = im.astype(kind)
-
-
-def row_block(combo, start, moves, here_ref, next_ref, shifts_ref, matrices_ref, right_ref, mid_ref, crossed_ref, out_ref):
+            right_ref[
+                combo, part * vectors : (part + 1) * vectors, color * sites : (color + 1) * sites
+            ] = field.astype(right_ref.dtype)
+
+
+def turn(right_ref, turned_ref):
+    vectors = right_ref.shape[1] // 2
+    for combo in range(right_ref.shape[0]):
+        turned_ref[combo, :vectors] = -right_ref[combo, vectors:]
+        turned_ref[combo, vectors:] = right_ref[combo, :vectors]
+
+
+def row_block(combo, start, moves, here_ref, next_ref, shifts_ref, matrices_ref, right_ref, turned_ref, mid_ref, crossed_ref, out_ref):
     sites = here_ref.shape[-1]
     picks, count = out_ref.shape[1:3]
     direction = moves[combo, 1]
@@ -179,9 +180,10 @@
                     at += sites
                     crossed_ref[down, at : at + LANES] = (sums[0] + sums[1]).astype(jnp.bfloat16)
         deep = slice(2 * column * sites, 2 * (column + 1) * sites)
+        wide = slice(column * sites, (column + 1) * sites)
         part = lax.dot_general(
             crossed_ref[:, deep],
-            right_ref[combo, :, deep],
+            jnp.concatenate([right_ref[combo, :, wide], turned_ref[combo, :, wide]], axis=1),
             (((1,), (1,)), ((), ())),
             preferred_element_type=jnp.float32,
         )
@@ -189,24 +191,54 @@
     out_ref[combo] = result.reshape(out_ref.shape[1:]).astype(out_ref.dtype)
 
 
-def first_kernel(scale, starts, moves, rows, here_ref, next_ref, links_ref, shifts_ref, right_ref, matrices_ref, out_ref, mid_ref, crossed_ref):
-    combos = range(out_ref.shape[0])
-    for combo in combos:
-        site_matrices(combo, moves, rows, here_ref, next_ref, links_ref, shifts_ref, matrices_ref, scale)
-    for combo in combos:
-        right_operand(combo, moves, here_ref, next_ref, shifts_ref, right_ref)
-        row_block(combo, starts[0], moves, here_ref, next_ref, shifts_ref, matrices_ref, right_ref, mid_ref.at[combo], crossed_ref.at[combo], out_ref)
-
-
-def later_kernel(starts, moves, here_ref, next_ref, shifts_ref, right_ref, matrices_ref, *rest):
-    *outs, mid_ref, crossed_ref = rest
-
-    def step(combo, carry):
-        for number, out_ref in enumerate(outs):
-            row_block(combo, starts[number], moves, here_ref, next_ref, shifts_ref, matrices_ref, right_ref, mid_ref.at[number], crossed_ref.at[number], out_ref)
-        return carry
-
-    lax.fori_loop(0, outs[0].shape[0], step, 0)
+def moves_of(meta, layout):
+    ring, combos = layout
+
+    class Moves:
+        def __getitem__(self, key):
+            combo, slot = key
+            return meta[ring + 3 * combo + slot]
+
+    class Rows:
+        shape = (meta.shape[0] - ring - 3 * combos,)
+
+        def __getitem__(self, i):
+            return meta[ring + 3 * combos + i]
+
+    return Moves(), Rows()
+
+
+def prepare(of_next, layout, scale, meta, here_ref, next_ref, links_ref, shifts_ref, right_ref, matrices_ref):
+    moves, rows = moves_of(meta, layout)
+    for combo in range(layout[1]):
+
+        @pl.when((moves[combo, 0] == 3) == of_next)
+        def _(combo=combo):
+            site_matrices(combo, moves, rows, here_ref, next_ref, links_ref, shifts_ref, matrices_ref, scale)
+
+        @pl.when((moves[combo, 2] == 3) == of_next)
+        def _(combo=combo):
+            right_operand(combo, moves, here_ref, next_ref, shifts_ref, right_ref)
+
+
+def early_kernel(layout, scale, meta, here_ref, links_ref, shifts_ref, right_ref, matrices_ref, copy_ref):
+    copy_ref[...] = here_ref[...]
+    prepare(False, layout, scale, meta, here_ref, here_ref, links_ref, shifts_ref, right_ref, matrices_ref)
+
+
+def first_kernel(layout, scale, meta, here_ref, next_ref, links_ref, shifts_ref, right_in, matrices_in, right_ref, matrices_ref, out_ref, turned_ref, mid_ref, crossed_ref):
+    prepare(True, layout, scale, meta, here_ref, next_ref, links_ref, shifts_ref, right_ref, matrices_ref)
+    turn(right_ref, turned_ref)
+    moves, _ = moves_of(meta, layout)
+    for combo in range(layout[1]):
+        row_block(combo, meta[0], moves, here_ref, next_ref, shifts_ref, matrices_ref, right_ref, turned_ref, mid_ref.at[combo], crossed_ref.at[combo], out_ref)
+
+
+def block_kernel(number, layout, meta, here_ref, next_ref, shifts_ref, right_ref, matrices_ref, out_ref, turned_ref, mid_ref, crossed_ref):
+    turn(right_ref, turned_ref)
+    moves, _ = moves_of(meta, layout)
+    for combo in range(layout[1]):
+        row_block(combo, meta[number], moves, here_ref, next_ref, shifts_ref, matrices_ref, right_ref, turned_ref, mid_ref.at[combo], crossed_ref.at[combo], out_ref)
 
 
 def local_work(eigenvectors, gauge_links, displacements, block_rows):
@@ -214,6 +246,7 @@
     ring = lax.axis_size("site")
     me = lax.axis_index("site")
     combos, picks = displacements.shape[0], block_rows.shape[0]
+    layout = (ring, combos)
     count = vectors // ring
     scale = 1.0 / math.sqrt(24.0 * planes * ring * sites)
     here = jnp.transpose(eigenvectors, (0, 2, 3, 1, 4)).reshape(parts, colors, vectors, sites)
@@ -221,66 +254,84 @@
     links = jnp.transpose(gauge_links, (1, 2, 3, 0, 4, 5)).astype(jnp.float32)
     links = links.reshape(COLORS, colors * colors * parts, sites)
     shifts = shift_matrices(sites, LX)
+    last = ring - 1
+    folded = ring == 4
+    if folded:
+        odd = lax.rem(me, 2)
+        owners = [last * (1 - odd), 1 + odd, lax.rem(me + 2, ring), me]
+    else:
+        owners = [lax.rem(me + offset, ring) for offset in range(1, ring + 1)]
+    meta = jnp.concatenate(
+        [jnp.stack(owners) * count, displacements.reshape(-1), block_rows]
+    ).astype(jnp.int32)
+
+    smem = pl.BlockSpec(memory_space=pltpu.SMEM)
+    vmem = pl.BlockSpec(memory_space=pltpu.VMEM)
+    right = jax.ShapeDtypeStruct((combos, parts * vectors, colors * sites), jnp.bfloat16)
+    matrices = jax.ShapeDtypeStruct((combos, 3 * colors * colors, picks, sites), jnp.float32)
+    scratch = [
+        pltpu.VMEM(right.shape, right.dtype),
+        pltpu.VMEM((combos, 3 * colors * count, sites), jnp.float32),
+        pltpu.VMEM((combos, picks * count, parts * colors * sites), jnp.bfloat16),
+    ]
+    params = pltpu.CompilerParams(vmem_limit_bytes=VMEM_BYTES)
 
     def chunk(kind):
         return jax.ShapeDtypeStruct((combos, picks, count, 2 * vectors), kind)
 
-    def starts(owners):
-        return jnp.stack([owner * count for owner in owners]).astype(jnp.int32)
-
-    smem = pl.BlockSpec(memory_space=pltpu.SMEM)
-    vmem = pl.BlockSpec(memory_space=pltpu.VMEM)
-
-    def scratch(blocks):
-        return [
-            pltpu.VMEM((blocks, 3 * colors * count, sites), jnp.float32),
-            pltpu.VMEM((blocks, picks * count, parts * colors * sites), jnp.bfloat16),
-        ]
-
-    folded = ring == 4
-    if folded:
-        owners = [ring - 1 - me, lax.rem(me + 2, ring), me + 1 - 2 * lax.rem(me, 2), me]
-    else:
-        owners = [lax.rem(me + offset, ring) for offset in range(1, ring + 1)]
+    right, matrices, here = pl.pallas_call(
+        functools.partial(early_kernel, layout, scale),
+        out_shape=(right, matrices, jax.ShapeDtypeStruct(here.shape, here.dtype)),
+        in_specs=[smem, vmem, vmem, vmem],
+        out_specs=(vmem, vmem, vmem),
+        compiler_params=params,
+        cost_estimate=pl.CostEstimate(flops=500_000_000, bytes_accessed=4_000_000, transcendentals=0),
+        name="early",
+    )(meta, here, links, shifts)
     right, matrices, sent = pl.pallas_call(
-        functools.partial(first_kernel, scale),
+        functools.partial(first_kernel, layout, scale),
         out_shape=(
-            jax.ShapeDtypeStruct((combos, 2 * vectors, parts * colors * sites), jnp.bfloat16),
-            jax.ShapeDtypeStruct((combos, 3 * colors * colors, SUBLANES, sites), jnp.float32),
+            jax.ShapeDtypeStruct(right.shape, right.dtype),
+            jax.ShapeDtypeStruct(matrices.shape, matrices.dtype),
             chunk(jnp.bfloat16),
         ),
-        in_specs=[smem, smem, smem, vmem, vmem, vmem, vmem],
+        in_specs=[smem, vmem, vmem, vmem, vmem, vmem, vmem],
         out_specs=(vmem, vmem, vmem),
-        scratch_shapes=scratch(combos),
-        compiler_params=pltpu.CompilerParams(vmem_limit_bytes=VMEM_BYTES),
+        input_output_aliases={5: 0, 6: 1},
+        scratch_shapes=scratch,
+        compiler_params=params,
         name="first",
-    )(starts(owners[:1]), displacements, block_rows, here, after, links, shifts)
-    others = pl.pallas_call(
-        later_kernel,
-        out_shape=tuple(chunk(jnp.bfloat16) for _ in owners[1:-1]) + (chunk(jnp.float32),),
-        in_specs=[smem, smem, vmem, vmem, vmem, vmem, vmem],
-        out_specs=(vmem,) * (ring - 1),
-        scratch_shapes=scratch(ring - 1),
-        compiler_params=pltpu.CompilerParams(vmem_limit_bytes=VMEM_BYTES),
-        cost_estimate=pl.CostEstimate(flops=3_000_000_000, bytes_accessed=8_000_000, transcendentals=0),
-        name="later",
-    )(starts(owners[1:]), displacements, here, after, shifts, right, matrices)
+    )(meta, here, after, links, shifts, right, matrices)
+    blocks = [sent]
+    for number in range(1, ring):
+        blocks.append(
+            pl.pallas_call(
+                functools.partial(block_kernel, number, layout),
+                out_shape=chunk(jnp.float32 if number == last else jnp.bfloat16),
+                in_specs=[smem, vmem, vmem, vmem, vmem, vmem],
+                out_specs=vmem,
+                scratch_shapes=scratch,
+                compiler_params=params,
+                cost_estimate=pl.CostEstimate(flops=1_000_000_000, bytes_accessed=4_000_000, transcendentals=0),
+            )(meta, here, after, shifts, right, matrices)
+        )
+    own = blocks.pop()
     if not folded:
-        blocks = [sent, *others[:-1]]
         arrived = [shifted(block, "site", offset + 1) for offset, block in enumerate(blocks)]
-        return functools.reduce(lambda total, block: total + block.astype(jnp.float32), arrived, others[-1])
-    last = ring - 1
-    passed = lax.ppermute(sent, "site", [(0, 1), (last, last - 1)])
-    near = lax.ppermute(sent, "site", [(1, 2), (2, 1)])
-    paired = lax.ppermute(others[1], "site", [(0, 1), (1, 0), (2, 3), (3, 2)])
-    far = shifted(others[0] + passed, "site", 2)
-    held = others[2] + near.astype(jnp.float32) + paired.astype(jnp.float32)
+        return functools.reduce(lambda total, block: total + block.astype(jnp.float32), arrived, own)
+    paired = lax.ppermute(blocks[0], "site", [(0, 1), (1, 0), (2, 3), (3, 2)])
+    near = lax.ppermute(blocks[1], "site", [(1, 2), (2, 1)])
+    inner = (me > 0) & (me < last)
+    far = shifted(blocks[2] + jnp.where(inner, paired, jnp.zeros_like(paired)), "site", 2)
+    inward = lax.ppermute(blocks[1], "site", [(0, 1), (3, 2)])
+    held = own + near.astype(jnp.float32) + inward.astype(jnp.float32)
+    held = held + jnp.where(inner, jnp.zeros_like(paired), paired).astype(jnp.float32)
     held = lax.optimization_barrier(held)
     return held + far.astype(jnp.float32)
 
 
 def solution(mesh):
-    return jax.shard_map(
+    step = jax.shard_map(
         local_work,
         mesh=mesh,
         in_specs=(
@@ -292,3 +343,6 @@
         out_specs=P("ta", None, "site", None),
         check_vma=False,
     )
+    if mesh.shape["site"] != 4:
+        return step
+    return step

time: 58.2 us -> 50.1 us (0.86)
  waiting for transfers between devices: 30 us -> 18.9 us
  Pallas kernels: 8.37 us -> 11 us
  local copies, waits for them, and re-layouts: 4.17 us -> 1.86 us
  other arithmetic: 2.13 us -> 3.86 us
  starting transfers between devices: 13.1 us -> 14.1 us
    ppermute x2, waiting for transfers between devices: 28.2 us -> 18.9 us  [shifted(): lax.ppermute(block, axis, [(i, (i + distance) % count) for i in range(cou...]
    unnamed x10 -> x2, local copies, waits for them, and re-layouts: 4.13 us -> 1.06 us
    pallas_call x2 -> x5, Pallas kernels: 8.37 us -> 11 us  [the longest x3 6.62 us: local_work(): pl.pallas_call(functools.partial(block_kernel, number, layout), out_shape...]
    ppermute x3, waiting for transfers between devices: 1.78 us -> 0.01 us  [the longest x1 0.01 us: local_work(): inward = lax.ppermute(blocks[1], 'site', [(0, 1), (3, 2)])]
    ppermute x3, starting transfers between devices: 3.02 us -> 4.69 us  [the longest x1 3.59 us: local_work(): inward = lax.ppermute(blocks[1], 'site', [(0, 1), (3, 2)])]
    add x2, other arithmetic: 0.19 us -> 1.19 us  [the longest x1 1.12 us: local_work(): held + jnp.where(inner, jnp.zeros_like(paired), paired).astype(jnp.float32)]
    reshape x0 -> x1, local copies, waits for them, and re-layouts: none -> 0.76 us  [local_work(): displacements.reshape(-1)]
    concatenate x0 -> x1, other arithmetic: none -> 0.73 us  [local_work(): jnp.concatenate([jnp.stack(owners) * count, displacements.reshape(-1), bl...]
  transfers between devices with their start and end apart: 5 -> 5, of which waited for: 3 -> 2; matrix products, arithmetic and copies ran while one was open for 2% -> 8% of each run, Pallas kernels for 9% -> 18%
where the time goes in v2:
time: 50.1 us; the launch traced here: 49.8 us
  waiting for transfers between devices  18.9 us (38%)
  starting transfers between devices  14.1 us (28%)
  Pallas kernels  11 us (22%)
  other arithmetic  3.86 us (8%)
  local copies, waits for them, and re-layouts  1.86 us (4%)
    ppermute x2, waiting for transfers between devices, shifted(): lax.ppermute(block, axis, [(i, (i + distance) % count) for i in range(cou...  18.9 us
    ppermute x2, starting transfers between devices, shifted(): lax.ppermute(block, axis, [(i, (i + distance) % count) for i in range(cou...  9.42 us
    pallas_call x3, Pallas kernels, local_work(): pl.pallas_call(functools.partial(block_kernel, number, layout), out_shape...  6.62 us
    ppermute x1, starting transfers between devices, local_work(): inward = lax.ppermute(blocks[1], 'site', [(0, 1), (3, 2)])  3.59 us
    pallas_call x1, Pallas kernels, local_work(): pl.pallas_call(functools.partial(first_kernel, layout, scale), out_shape=...  2.24 us
    pallas_call x1, Pallas kernels, local_work(): pl.pallas_call(functools.partial(early_kernel, layout, scale), out_shape=...  2.14 us
    add x1, other arithmetic, local_work(): held + jnp.where(inner, jnp.zeros_like(paired), paired).astype(jnp.float32)  1.12 us
    unnamed x2, local copies, waits for them, and re-layouts  1.06 us
  transfers between devices with their start and end apart: 5, of which 2 were waited for; matrix products, arithmetic and copies ran while one was open for 8% of the time, Pallas kernels for 18%

profile of v2, /device:TPU:0, one launch (start us, length us, event | category | flops | bytes accessed | tf_op | source)
XLA Modules:
  0.0 49.8 jit_solution(9378504720665494904)
XLA Ops:
  0.0 5.1 %collective-permute-start = (bf16[2,3,192,256]{3,2,1,0:T(8,128)(2,1)}, bf16[2,3,192,256]{3,2,1,0:T(8,128)(2,1)S(1)}, u32[]{:S(2)}, u32[]{:S(2)}) collective-permute-start(bf16[2,3,192,256]{3,2,1,0:T(8,128)(2,1)} %bitcast.13), channel_id=1, source_target_pairs={{0,3},{1,0},{2,1},{3,2},{4,7},{5,4},{6,5},{7,6},{8,11},{9,8},{10,9... | collective-permute-start | bytes 1769480 | tf_op jit(solution)/shard_map/ppermute | solution.py:22
  5.1 0.8 %reshape.11 = s32[6]{0:T(128)S(1)} reshape(s32[2,3]{1,0:T(2,128)} %param.6) | data formatting | bytes 48 | tf_op jit(solution)/shard_map/reshape | solution.py:265
  5.8 0.8 %convert_bitcast_fusion = f32[3,3,3,2,1,256]{5,3,4,2,1,0:T(2,128)S(1)} fusion(bf16[2,3,3,3,1,256]{5,0,4,3,2,1:T(2,128)(2,1)} %param.5), kind=kLoop, calls=%fused_computation.8 | loop fusion | flops 13824 | bytes 82944 | tf_op jit(solution)/shard_map/reshape | solution.py:255
  6.7 0.1 add_multiply_fusion
  6.7 0.7 %pad_add_fusion.meta = s32[14]{0:T(128)S(1)} fusion(s32[4]{0:T(128)} %param.7, s32[6]{0:T(128)S(1)} %reshape.11, s32[4]{0:T(128)S(1)} %add_multiply_fusion), kind=kLoop, calls=%fused_computation.20 | loop fusion | flops 28 | bytes 112 | tf_op jit(solution)/shard_map/concatenate | solution.py:264
  7.5 0.2 select_convert_fusion.shifts_ref
  7.7 0.0 copy-start
  7.7 1.1 %copy-done = bf16[2,192,3,1,256]{4,1,3,2,0:T(8,128)(2,1)S(1)} copy-done((bf16[2,192,3,1,256]{4,1,3,2,0:T(8,128)(2,1)S(1)}, bf16[2,192,3,1,256]{4,1,3,2,0:T(8,128)(2,1)}, u32[]{:S(2)}) %copy-start) | copy-done | bytes 589848
  8.8 2.1 %early.1 = (bf16[2,384,768]{2,1,0:T(8,128)(2,1)S(1)}, f32[2,27,4,256]{3,2,1,0:T(4,128)S(1)}, bf16[2,3,192,256]{3,2,1,0:T(8,128)(2,1)S(1)}) custom-call(s32[14]{0:T(128)S(1)} %pad_add_fusion.meta, bf16[2,3,192,256]{3,2,1,0:T(8,128)(2,1)S(1)} %bitcast.14, f32[3,18,256]{2,1,0:T(8,128)S(1)} %reshape.16.links_ref, ...), custom_call_target="tpu_custom_call" | custom-call | flops 500000000 | bytes 4000000 | tf_op jit(solution)/shard_map/early/pallas_call | solution.py:282
  10.9 7.1 %collective-permute-done.next_ref = bf16[2,3,192,256]{3,2,1,0:T(8,128)(2,1)S(1)} collective-permute-done((bf16[2,3,192,256]{3,2,1,0:T(8,128)(2,1)}, bf16[2,3,192,256]{3,2,1,0:T(8,128)(2,1)S(1)}, u32[]{:S(2)}, u32[]{:S(2)}) %collective-permute-start) | collective-permute-done | bytes 589856 | tf_op jit(solution)/shard_map/ppermute | solution.py:22
  18.0 2.2 %first.1 = (bf16[2,384,768]{2,1,0:T(8,128)(2,1)S(1)}, f32[2,27,4,256]{3,2,1,0:T(4,128)S(1)}, bf16[2,4,48,384]{3,2,1,0:T(8,128)(2,1)S(1)}) custom-call(s32[14]{0:T(128)S(1)} %pad_add_fusion.meta, bf16[2,3,192,256]{3,2,1,0:T(8,128)(2,1)S(1)} %get-tuple-element.11.here_ref, ...), custom_call_target="tpu_custom_call", output_to_operand_aliasing={{0}: (5, {}), {1}: (6, {})} | custom-call | tf_op jit(solution)/shard_map/first/pallas_call | solution.py:291
  20.2 0.4 collective-permute-start.3
  20.6 2.2 %shard_map.47 = bf16[2,4,48,384]{3,2,1,0:T(8,128)(2,1)S(1)} custom-call(s32[14]{0:T(128)S(1)} %pad_add_fusion.meta, bf16[2,3,192,256]{3,2,1,0:T(8,128)(2,1)S(1)} %get-tuple-element.11.here_ref, bf16[2,3,192,256]{3,2,1,0:T(8,128)(2,1)S(1)} %collective-permute-done.next_ref, bf16[3,256,256]{2,1,0:T(8,128)(2,1)S(1)} %select_convert_fusion.shifts_ref, ...), custom_call_target="tpu_custom_call" | custom-call | flops 1000000000 | bytes 4000000 | tf_op jit(solution)/shard_map/pallas_call | solution.py:308
  22.9 3.6 %collective-permute-start.2 = (bf16[2,4,48,384]{3,2,1,0:T(8,128)(2,1)S(1)}, bf16[2,4,48,384]{3,2,1,0:T(8,128)(2,1)S(1)}, u32[]{:S(2)}, u32[]{:S(2)}) collective-permute-start(bf16[2,4,48,384]{3,2,1,0:T(8,128)(2,1)S(1)} %shard_map.47), channel_id=1, source_target_pairs={{0,1},{3,2},{4,5},{7,6},{8,9},{11,10},{12,13},{15,14},{16,17},{19,... | collective-permute-start | bytes 884744 | tf_op jit(solution)/shard_map/ppermute | solution.py:326
  26.5 0.7 %collective-permute-start.1 = (bf16[2,4,48,384]{3,2,1,0:T(8,128)(2,1)S(1)}, bf16[2,4,48,384]{3,2,1,0:T(8,128)(2,1)S(1)}, u32[]{:S(2)}, u32[]{:S(2)}) collective-permute-start(bf16[2,4,48,384]{3,2,1,0:T(8,128)(2,1)S(1)} %shard_map.47), channel_id=1, source_target_pairs={{1,2},{2,1},{5,6},{6,5},{9,10},{10,9},{13,14},{14,13},{17,18},{18,... | collective-permute-start | bytes 884744 | tf_op jit(solution)/shard_map/ppermute | solution.py:323
  27.2 2.2 %shard_map.48 = bf16[2,4,48,384]{3,2,1,0:T(8,128)(2,1)S(1)} custom-call(s32[14]{0:T(128)S(1)} %pad_add_fusion.meta, bf16[2,3,192,256]{3,2,1,0:T(8,128)(2,1)S(1)} %get-tuple-element.11.here_ref, bf16[2,3,192,256]{3,2,1,0:T(8,128)(2,1)S(1)} %collective-permute-done.next_ref, bf16[3,256,256]{2,1,0:T(8,128)(2,1)S(1)} %select_convert_fusion.shifts_ref, ...), custom_call_target="tpu_custom_call" | custom-call | flops 1000000000 | bytes 4000000 | tf_op jit(solution)/shard_map/pallas_call | solution.py:308
  29.4 0.0 collective-permute-done.3
  29.4 0.1 select_add_fusion
  29.5 4.3 %collective-permute-start.4 = (bf16[2,4,48,384]{3,2,1,0:T(8,128)(2,1)S(1)}, bf16[2,4,48,384]{3,2,1,0:T(8,128)(2,1)S(1)}, u32[]{:S(2)}, u32[]{:S(2)}) collective-permute-start(bf16[2,4,48,384]{3,2,1,0:T(8,128)(2,1)S(1)} %select_add_fusion), channel_id=1, source_target_pairs={{0,2},{1,3},{2,0},{3,1},{4,6},{5,7},{6,4},{7,5},{8,10},{9,11},{10,... | collective-permute-start | bytes 884744 | tf_op jit(solution)/shard_map/ppermute | solution.py:22
  33.8 2.2 %shard_map.46 = f32[2,4,48,384]{3,2,1,0:T(8,128)S(1)} custom-call(s32[14]{0:T(128)S(1)} %pad_add_fusion.meta, bf16[2,3,192,256]{3,2,1,0:T(8,128)(2,1)S(1)} %get-tuple-element.11.here_ref, bf16[2,3,192,256]{3,2,1,0:T(8,128)(2,1)S(1)} %collective-permute-done.next_ref, bf16[3,256,256]{2,1,0:T(8,128)(2,1)S(1)} %select_convert_fusion.shifts_ref, ...), custom_call_target="tpu_custom_call" | custom-call | flops 1000000000 | bytes 4000000 | tf_op jit(solution)/shard_map/pallas_call | solution.py:308
  36.0 0.0 collective-permute-done.2
  36.0 0.0 collective-permute-done.1
  36.0 1.1 %convert_add_fusion.1 = f32[2,4,48,384]{3,2,1,0:T(8,128)S(1)} fusion(bf16[2,4,48,384]{3,2,1,0:T(8,128)(2,1)S(1)} %collective-permute-done.2, f32[2,4,48,384]{3,2,1,0:T(8,128)S(1)} %shard_map.46, bf16[2,4,48,384]{3,2,1,0:T(8,128)(2,1)S(1)} %collective-permute-done.1, bf16[2,4,48,384]{3,2,1,0:T(8,128)(2,1)} %collective-permute-done.3, pred[]{:T(512)S(6)} %and.11), kind=kLoop, calls=%fused_computation.6 | loop fusion | flops 1032192 | bytes 2064385 | tf_op jit(solution)/shard_map/add | solution.py:328
  37.2 11.8 %collective-permute-done.4 = bf16[2,4,48,384]{3,2,1,0:T(8,128)(2,1)S(1)} collective-permute-done((bf16[2,4,48,384]{3,2,1,0:T(8,128)(2,1)S(1)}, bf16[2,4,48,384]{3,2,1,0:T(8,128)(2,1)S(1)}, u32[]{:S(2)}, u32[]{:S(2)}) %collective-permute-start.4) | collective-permute-done | bytes 294944 | tf_op jit(solution)/shard_map/ppermute | solution.py:22
  49.0 0.9 %convert_add_fusion = f32[2,4,48,384]{3,2,1,0:T(8,128)} fusion(f32[2,4,48,384]{3,2,1,0:T(8,128)S(1)} %convert_add_fusion.1, bf16[2,4,48,384]{3,2,1,0:T(8,128)(2,1)S(1)} %collective-permute-done.4), kind=kLoop, calls=%fused_computation.5 | loop fusion | flops 294912 | bytes 1474560 | tf_op jit(solution)/shard_map/add | solution.py:330
  (5 shorter events, 0.1 us)
Async XLA Ops:
  0.0 18.0 %collective-permute-start = (bf16[2,3,192,256]{3,2,1,0:T(8,128)(2,1)}, bf16[2,3,192,256]{3,2,1,0:T(8,128)(2,1)S(1)}, u32[]{:S(2)}, u32[]{:S(2)}) collective-permute-start(bf16[2,3,192,256]{3,2,1,0:T(8,128)(2,1)} %bitcast.13), channel_id=1, source_target_pairs={{0,3},{1,0},{2,1},{3,2},{4,7},{5,4},{6,5},{7,6},{8,11},{9,8},{10,9... | collective-permute-start | bytes 1769480 | tf_op jit(solution)/shard_map/ppermute | solution.py:22
  7.7 1.1 %copy-start = (bf16[2,192,3,1,256]{4,1,3,2,0:T(8,128)(2,1)S(1)}, bf16[2,192,3,1,256]{4,1,3,2,0:T(8,128)(2,1)}, u32[]{:S(2)}) copy-start(bf16[2,192,3,1,256]{4,1,3,2,0:T(8,128)(2,1)} %param.4) | copy-start | bytes 1769476
  20.2 9.1 %collective-permute-start.3 = (bf16[2,4,48,384]{3,2,1,0:T(8,128)(2,1)S(1)}, bf16[2,4,48,384]{3,2,1,0:T(8,128)(2,1)}, u32[]{:S(2)}, u32[]{:S(2)}) collective-permute-start(bf16[2,4,48,384]{3,2,1,0:T(8,128)(2,1)S(1)} %get-tuple-element.16), channel_id=1, source_target_pairs={{0,1},{1,0},{2,3},{3,2},{4,5},{5,4},{6,7},{7,6},{8,9},{9,8},{10,11... | collective-permute-start | bytes 884744 | tf_op jit(solution)/shard_map/ppermute | solution.py:322
  22.9 13.2 %collective-permute-start.2 = (bf16[2,4,48,384]{3,2,1,0:T(8,128)(2,1)S(1)}, bf16[2,4,48,384]{3,2,1,0:T(8,128)(2,1)S(1)}, u32[]{:S(2)}, u32[]{:S(2)}) collective-permute-start(bf16[2,4,48,384]{3,2,1,0:T(8,128)(2,1)S(1)} %shard_map.47), channel_id=1, source_target_pairs={{0,1},{3,2},{4,5},{7,6},{8,9},{11,10},{12,13},{15,14},{16,17},{19,... | collective-permute-start | bytes 884744 | tf_op jit(solution)/shard_map/ppermute | solution.py:326
  26.5 9.6 %collective-permute-start.1 = (bf16[2,4,48,384]{3,2,1,0:T(8,128)(2,1)S(1)}, bf16[2,4,48,384]{3,2,1,0:T(8,128)(2,1)S(1)}, u32[]{:S(2)}, u32[]{:S(2)}) collective-permute-start(bf16[2,4,48,384]{3,2,1,0:T(8,128)(2,1)S(1)} %shard_map.47), channel_id=1, source_target_pairs={{1,2},{2,1},{5,6},{6,5},{9,10},{10,9},{13,14},{14,13},{17,18},{18,... | collective-permute-start | bytes 884744 | tf_op jit(solution)/shard_map/ppermute | solution.py:323
  29.5 19.5 %collective-permute-start.4 = (bf16[2,4,48,384]{3,2,1,0:T(8,128)(2,1)S(1)}, bf16[2,4,48,384]{3,2,1,0:T(8,128)(2,1)S(1)}, u32[]{:S(2)}, u32[]{:S(2)}) collective-permute-start(bf16[2,4,48,384]{3,2,1,0:T(8,128)(2,1)S(1)} %select_add_fusion), channel_id=1, source_target_pairs={{0,2},{1,3},{2,0},{3,1},{4,6},{5,7},{6,4},{7,5},{8,10},{9,11},{10,... | collective-permute-start | bytes 884744 | tf_op jit(solution)/shard_map/ppermute | solution.py:22

commit v3 on v2

--- a/solution.py
+++ b/solution.py
@@ -257,8 +257,7 @@
     last = ring - 1
     folded = ring == 4
     if folded:
-        odd = lax.rem(me, 2)
-        owners = [last * (1 - odd), 1 + odd, lax.rem(me + 2, ring), me]
+        owners = [last - me, lax.rem(me + 2, ring), me + 1 - 2 * lax.rem(me, 2), me]
     else:
         owners = [lax.rem(me + offset, ring) for offset in range(1, ring + 1)]
     meta = jnp.concatenate(
@@ -319,13 +318,11 @@
     if not folded:
         arrived = [shifted(block, "site", offset + 1) for offset, block in enumerate(blocks)]
         return functools.reduce(lambda total, block: total + block.astype(jnp.float32), arrived, own)
-    paired = lax.ppermute(blocks[0], "site", [(0, 1), (1, 0), (2, 3), (3, 2)])
-    near = lax.ppermute(blocks[1], "site", [(1, 2), (2, 1)])
-    inner = (me > 0) & (me < last)
-    far = shifted(blocks[2] + jnp.where(inner, paired, jnp.zeros_like(paired)), "site", 2)
-    inward = lax.ppermute(blocks[1], "site", [(0, 1), (3, 2)])
-    held = own + near.astype(jnp.float32) + inward.astype(jnp.float32)
-    held = held + jnp.where(inner, jnp.zeros_like(paired), paired).astype(jnp.float32)
+    near = lax.ppermute(blocks[0], "site", [(1, 2), (2, 1)])
+    passed = lax.ppermute(blocks[0], "site", [(0, 1), (3, 2)])
+    far = shifted(blocks[1] + passed, "site", 2)
+    paired = lax.ppermute(blocks[2], "site", [(0, 1), (1, 0), (2, 3), (3, 2)])
+    held = own + near.astype(jnp.float32) + paired.astype(jnp.float32)
     held = lax.optimization_barrier(held)
     return held + far.astype(jnp.float32)
 

time: 50.1 us -> 50.2 us (level)
  waiting for transfers between devices: 18.9 us -> 21.5 us
  starting transfers between devices: 14.1 us -> 12.4 us
  other arithmetic: 3.86 us -> 2.86 us
    ppermute x3, waiting for transfers between devices: 0.01 us -> 2.06 us  [the longest x1 2.06 us: local_work(): passed = lax.ppermute(blocks[0], 'site', [(0, 1), (3, 2)])]
    ppermute x3, starting transfers between devices: 4.69 us -> 3.01 us  [the longest x1 2.26 us: local_work(): passed = lax.ppermute(blocks[0], 'site', [(0, 1), (3, 2)])]
    add x2, other arithmetic: 1.19 us -> 0.19 us  [the longest x1 0.11 us: local_work(): held = own + near.astype(jnp.float32) + paired.astype(jnp.float32)]
    ppermute x2, waiting for transfers between devices: 18.9 us -> 19.5 us  [shifted(): lax.ppermute(block, axis, [(i, (i + distance) % count) for i in range(cou...]
  transfers between devices with their start and end apart: 5 -> 5, of which waited for: 2 -> 3; matrix products, arithmetic and copies ran while one was open for 8% -> 6% of each run, Pallas kernels for 18% -> 18%
where the time goes in v3:
time: 50.2 us; the launch traced here: 50 us
  waiting for transfers between devices  21.5 us (43%)
  starting transfers between devices  12.4 us (25%)
  Pallas kernels  11.2 us (22%)
  other arithmetic  2.86 us (6%)
  local copies, waits for them, and re-layouts  1.86 us (4%)
    ppermute x2, waiting for transfers between devices, shifted(): lax.ppermute(block, axis, [(i, (i + distance) % count) for i in range(cou...  19.5 us
    ppermute x2, starting transfers between devices, shifted(): lax.ppermute(block, axis, [(i, (i + distance) % count) for i in range(cou...  9.37 us
    pallas_call x3, Pallas kernels, local_work(): pl.pallas_call(functools.partial(block_kernel, number, layout), out_shape...  6.78 us
    pallas_call x1, Pallas kernels, local_work(): pl.pallas_call(functools.partial(first_kernel, layout, scale), out_shape=...  2.3 us
    ppermute x1, starting transfers between devices, local_work(): passed = lax.ppermute(blocks[0], 'site', [(0, 1), (3, 2)])  2.26 us
    pallas_call x1, Pallas kernels, local_work(): pl.pallas_call(functools.partial(early_kernel, layout, scale), out_shape=...  2.14 us
    ppermute x1, waiting for transfers between devices, local_work(): passed = lax.ppermute(blocks[0], 'site', [(0, 1), (3, 2)])  2.06 us
    unnamed x2, local copies, waits for them, and re-layouts  1.06 us
  transfers between devices with their start and end apart: 5, of which 3 were waited for; matrix products, arithmetic and copies ran while one was open for 6% of the time, Pallas kernels for 18%

profile of v3, /device:TPU:0, one launch (start us, length us, event | category | flops | bytes accessed | tf_op | source)
XLA Modules:
  0.0 50.0 jit_solution(6053096661001853323)
XLA Ops:
  0.0 5.1 %collective-permute-start = (bf16[2,3,192,256]{3,2,1,0:T(8,128)(2,1)}, bf16[2,3,192,256]{3,2,1,0:T(8,128)(2,1)S(1)}, u32[]{:S(2)}, u32[]{:S(2)}) collective-permute-start(bf16[2,3,192,256]{3,2,1,0:T(8,128)(2,1)} %bitcast.13), channel_id=1, source_target_pairs={{0,3},{1,0},{2,1},{3,2},{4,7},{5,4},{6,5},{7,6},{8,11},{9,8},{10,9... | collective-permute-start | bytes 1769480 | tf_op jit(solution)/shard_map/ppermute | solution.py:22
  5.1 0.8 %reshape.11 = s32[6]{0:T(128)S(1)} reshape(s32[2,3]{1,0:T(2,128)} %param.6) | data formatting | bytes 48 | tf_op jit(solution)/shard_map/reshape | solution.py:264
  5.8 0.8 %convert_bitcast_fusion = f32[3,3,3,2,1,256]{5,3,4,2,1,0:T(2,128)S(1)} fusion(bf16[2,3,3,3,1,256]{5,0,4,3,2,1:T(2,128)(2,1)} %param.5), kind=kLoop, calls=%fused_computation.7 | loop fusion | flops 13824 | bytes 82944 | tf_op jit(solution)/shard_map/reshape | solution.py:255
  6.7 0.1 add_multiply_fusion
  6.7 0.7 %pad_add_fusion.meta = s32[14]{0:T(128)S(1)} fusion(s32[4]{0:T(128)} %param.7, s32[6]{0:T(128)S(1)} %reshape.11, s32[4]{0:T(128)S(1)} %add_multiply_fusion), kind=kLoop, calls=%fused_computation.19 | loop fusion | flops 28 | bytes 112 | tf_op jit(solution)/shard_map/concatenate | solution.py:263
  7.5 0.2 select_convert_fusion.shifts_ref
  7.7 0.0 copy-start
  7.7 1.1 %copy-done = bf16[2,192,3,1,256]{4,1,3,2,0:T(8,128)(2,1)S(1)} copy-done((bf16[2,192,3,1,256]{4,1,3,2,0:T(8,128)(2,1)S(1)}, bf16[2,192,3,1,256]{4,1,3,2,0:T(8,128)(2,1)}, u32[]{:S(2)}) %copy-start) | copy-done | bytes 589848
  8.8 2.1 %early.1 = (bf16[2,384,768]{2,1,0:T(8,128)(2,1)S(1)}, f32[2,27,4,256]{3,2,1,0:T(4,128)S(1)}, bf16[2,3,192,256]{3,2,1,0:T(8,128)(2,1)S(1)}) custom-call(s32[14]{0:T(128)S(1)} %pad_add_fusion.meta, bf16[2,3,192,256]{3,2,1,0:T(8,128)(2,1)S(1)} %bitcast.14, f32[3,18,256]{2,1,0:T(8,128)S(1)} %reshape.16.links_ref, ...), custom_call_target="tpu_custom_call" | custom-call | flops 500000000 | bytes 4000000 | tf_op jit(solution)/shard_map/early/pallas_call | solution.py:281
  10.9 7.1 %collective-permute-done.next_ref = bf16[2,3,192,256]{3,2,1,0:T(8,128)(2,1)S(1)} collective-permute-done((bf16[2,3,192,256]{3,2,1,0:T(8,128)(2,1)}, bf16[2,3,192,256]{3,2,1,0:T(8,128)(2,1)S(1)}, u32[]{:S(2)}, u32[]{:S(2)}) %collective-permute-start) | collective-permute-done | bytes 589856 | tf_op jit(solution)/shard_map/ppermute | solution.py:22
  18.0 2.3 %first.1 = (bf16[2,384,768]{2,1,0:T(8,128)(2,1)S(1)}, f32[2,27,4,256]{3,2,1,0:T(4,128)S(1)}, bf16[2,4,48,384]{3,2,1,0:T(8,128)(2,1)S(1)}) custom-call(s32[14]{0:T(128)S(1)} %pad_add_fusion.meta, bf16[2,3,192,256]{3,2,1,0:T(8,128)(2,1)S(1)} %get-tuple-element.11.here_ref, ...), custom_call_target="tpu_custom_call", output_to_operand_aliasing={{0}: (5, {}), {1}: (6, {})} | custom-call | tf_op jit(solution)/shard_map/first/pallas_call | solution.py:290
  20.3 2.3 %collective-permute-start.3 = (bf16[2,4,48,384]{3,2,1,0:T(8,128)(2,1)S(1)}, bf16[2,4,48,384]{3,2,1,0:T(8,128)(2,1)S(1)}, u32[]{:S(2)}, u32[]{:S(2)}) collective-permute-start(bf16[2,4,48,384]{3,2,1,0:T(8,128)(2,1)S(1)} %get-tuple-element.16), channel_id=1, source_target_pairs={{0,1},{3,2},{4,5},{7,6},{8,9},{11,10},{12,13},{15,14},{16,17},{19,... | collective-permute-start | bytes 884744 | tf_op jit(solution)/shard_map/ppermute | solution.py:322
  22.6 2.3 %shard_map.47 = bf16[2,4,48,384]{3,2,1,0:T(8,128)(2,1)S(1)} custom-call(s32[14]{0:T(128)S(1)} %pad_add_fusion.meta, bf16[2,3,192,256]{3,2,1,0:T(8,128)(2,1)S(1)} %get-tuple-element.11.here_ref, bf16[2,3,192,256]{3,2,1,0:T(8,128)(2,1)S(1)} %collective-permute-done.next_ref, bf16[3,256,256]{2,1,0:T(8,128)(2,1)S(1)} %select_convert_fusion.shifts_ref, ...), custom_call_target="tpu_custom_call" | custom-call | flops 1000000000 | bytes 4000000 | tf_op jit(solution)/shard_map/pallas_call | solution.py:307
  24.8 0.1 collective-permute-start.2
  24.9 0.7 %collective-permute-start.1 = (bf16[2,4,48,384]{3,2,1,0:T(8,128)(2,1)S(1)}, bf16[2,4,48,384]{3,2,1,0:T(8,128)(2,1)S(1)}, u32[]{:S(2)}, u32[]{:S(2)}) collective-permute-start(bf16[2,4,48,384]{3,2,1,0:T(8,128)(2,1)S(1)} %get-tuple-element.16), channel_id=1, source_target_pairs={{1,2},{2,1},{5,6},{6,5},{9,10},{10,9},{13,14},{14,13},{17,18},{18,... | collective-permute-start | bytes 884744 | tf_op jit(solution)/shard_map/ppermute | solution.py:321
  25.6 2.3 %shard_map.48 = bf16[2,4,48,384]{3,2,1,0:T(8,128)(2,1)S(1)} custom-call(s32[14]{0:T(128)S(1)} %pad_add_fusion.meta, bf16[2,3,192,256]{3,2,1,0:T(8,128)(2,1)S(1)} %get-tuple-element.11.here_ref, bf16[2,3,192,256]{3,2,1,0:T(8,128)(2,1)S(1)} %collective-permute-done.next_ref, bf16[3,256,256]{2,1,0:T(8,128)(2,1)S(1)} %select_convert_fusion.shifts_ref, ...), custom_call_target="tpu_custom_call" | custom-call | flops 1000000000 | bytes 4000000 | tf_op jit(solution)/shard_map/pallas_call | solution.py:307
  27.9 2.1 %collective-permute-done.3 = bf16[2,4,48,384]{3,2,1,0:T(8,128)(2,1)S(1)} collective-permute-done((bf16[2,4,48,384]{3,2,1,0:T(8,128)(2,1)S(1)}, bf16[2,4,48,384]{3,2,1,0:T(8,128)(2,1)S(1)}, u32[]{:S(2)}, u32[]{:S(2)}) %collective-permute-start.3) | collective-permute-done | bytes 294944 | tf_op jit(solution)/shard_map/ppermute | solution.py:322
  29.9 0.1 add.60
  30.0 4.3 %collective-permute-start.4 = (bf16[2,4,48,384]{3,2,1,0:T(8,128)(2,1)S(1)}, bf16[2,4,48,384]{3,2,1,0:T(8,128)(2,1)S(1)}, u32[]{:S(2)}, u32[]{:S(2)}) collective-permute-start(bf16[2,4,48,384]{3,2,1,0:T(8,128)(2,1)S(1)} %add.60), channel_id=1, source_target_pairs={{0,2},{1,3},{2,0},{3,1},{4,6},{5,7},{6,4},{7,5},{8,10},{9,11},{10,... | collective-permute-start | bytes 884744 | tf_op jit(solution)/shard_map/ppermute | solution.py:22
  34.3 2.3 %shard_map.46 = f32[2,4,48,384]{3,2,1,0:T(8,128)S(1)} custom-call(s32[14]{0:T(128)S(1)} %pad_add_fusion.meta, bf16[2,3,192,256]{3,2,1,0:T(8,128)(2,1)S(1)} %get-tuple-element.11.here_ref, bf16[2,3,192,256]{3,2,1,0:T(8,128)(2,1)S(1)} %collective-permute-done.next_ref, bf16[3,256,256]{2,1,0:T(8,128)(2,1)S(1)} %select_convert_fusion.shifts_ref, ...), custom_call_target="tpu_custom_call" | custom-call | flops 1000000000 | bytes 4000000 | tf_op jit(solution)/shard_map/pallas_call | solution.py:307
  36.6 0.0 collective-permute-done.2
  36.6 0.0 collective-permute-done.1
  36.6 0.1 convert_add_fusion.1
  36.7 12.4 %collective-permute-done.4 = bf16[2,4,48,384]{3,2,1,0:T(8,128)(2,1)S(1)} collective-permute-done((bf16[2,4,48,384]{3,2,1,0:T(8,128)(2,1)S(1)}, bf16[2,4,48,384]{3,2,1,0:T(8,128)(2,1)S(1)}, u32[]{:S(2)}, u32[]{:S(2)}) %collective-permute-start.4) | collective-permute-done | bytes 294944 | tf_op jit(solution)/shard_map/ppermute | solution.py:22
  49.1 0.9 %convert_add_fusion = f32[2,4,48,384]{3,2,1,0:T(8,128)} fusion(f32[2,4,48,384]{3,2,1,0:T(8,128)S(1)} %convert_add_fusion.1, bf16[2,4,48,384]{3,2,1,0:T(8,128)(2,1)S(1)} %collective-permute-done.4), kind=kLoop, calls=%fused_computation.5 | loop fusion | flops 294912 | bytes 1474560 | tf_op jit(solution)/shard_map/add | solution.py:327
  (5 shorter events, 0.1 us)
Async XLA Ops:
  0.0 18.0 %collective-permute-start = (bf16[2,3,192,256]{3,2,1,0:T(8,128)(2,1)}, bf16[2,3,192,256]{3,2,1,0:T(8,128)(2,1)S(1)}, u32[]{:S(2)}, u32[]{:S(2)}) collective-permute-start(bf16[2,3,192,256]{3,2,1,0:T(8,128)(2,1)} %bitcast.13), channel_id=1, source_target_pairs={{0,3},{1,0},{2,1},{3,2},{4,7},{5,4},{6,5},{7,6},{8,11},{9,8},{10,9... | collective-permute-start | bytes 1769480 | tf_op jit(solution)/shard_map/ppermute | solution.py:22
  7.7 1.1 %copy-start = (bf16[2,192,3,1,256]{4,1,3,2,0:T(8,128)(2,1)S(1)}, bf16[2,192,3,1,256]{4,1,3,2,0:T(8,128)(2,1)}, u32[]{:S(2)}) copy-start(bf16[2,192,3,1,256]{4,1,3,2,0:T(8,128)(2,1)} %param.4) | copy-start | bytes 1769476
  20.3 9.6 %collective-permute-start.3 = (bf16[2,4,48,384]{3,2,1,0:T(8,128)(2,1)S(1)}, bf16[2,4,48,384]{3,2,1,0:T(8,128)(2,1)S(1)}, u32[]{:S(2)}, u32[]{:S(2)}) collective-permute-start(bf16[2,4,48,384]{3,2,1,0:T(8,128)(2,1)S(1)} %get-tuple-element.16), channel_id=1, source_target_pairs={{0,1},{3,2},{4,5},{7,6},{8,9},{11,10},{12,13},{15,14},{16,17},{19,... | collective-permute-start | bytes 884744 | tf_op jit(solution)/shard_map/ppermute | solution.py:322
  24.8 11.7 %collective-permute-start.2 = (bf16[2,4,48,384]{3,2,1,0:T(8,128)(2,1)S(1)}, bf16[2,4,48,384]{3,2,1,0:T(8,128)(2,1)S(1)}, u32[]{:S(2)}, u32[]{:S(2)}) collective-permute-start(bf16[2,4,48,384]{3,2,1,0:T(8,128)(2,1)S(1)} %shard_map.47), channel_id=1, source_target_pairs={{0,1},{1,0},{2,3},{3,2},{4,5},{5,4},{6,7},{7,6},{8,9},{9,8},{10,11... | collective-permute-start | bytes 884744 | tf_op jit(solution)/shard_map/ppermute | solution.py:324
  24.9 11.7 %collective-permute-start.1 = (bf16[2,4,48,384]{3,2,1,0:T(8,128)(2,1)S(1)}, bf16[2,4,48,384]{3,2,1,0:T(8,128)(2,1)S(1)}, u32[]{:S(2)}, u32[]{:S(2)}) collective-permute-start(bf16[2,4,48,384]{3,2,1,0:T(8,128)(2,1)S(1)} %get-tuple-element.16), channel_id=1, source_target_pairs={{1,2},{2,1},{5,6},{6,5},{9,10},{10,9},{13,14},{14,13},{17,18},{18,... | collective-permute-start | bytes 884744 | tf_op jit(solution)/shard_map/ppermute | solution.py:321
  30.0 19.1 %collective-permute-start.4 = (bf16[2,4,48,384]{3,2,1,0:T(8,128)(2,1)S(1)}, bf16[2,4,48,384]{3,2,1,0:T(8,128)(2,1)S(1)}, u32[]{:S(2)}, u32[]{:S(2)}) collective-permute-start(bf16[2,4,48,384]{3,2,1,0:T(8,128)(2,1)S(1)} %add.60), channel_id=1, source_target_pairs={{0,2},{1,3},{2,0},{3,1},{4,6},{5,7},{6,4},{7,5},{8,10},{9,11},{10,... | collective-permute-start | bytes 884744 | tf_op jit(solution)/shard_map/ppermute | solution.py:22

commit v4 on v3

--- a/solution.py
+++ b/solution.py
@@ -320,9 +320,10 @@
         return functools.reduce(lambda total, block: total + block.astype(jnp.float32), arrived, own)
     near = lax.ppermute(blocks[0], "site", [(1, 2), (2, 1)])
     passed = lax.ppermute(blocks[0], "site", [(0, 1), (3, 2)])
-    far = shifted(blocks[1] + passed, "site", 2)
+    inward = lax.ppermute(blocks[1], "site", [(0, 2), (3, 1)])
     paired = lax.ppermute(blocks[2], "site", [(0, 1), (1, 0), (2, 3), (3, 2)])
-    held = own + near.astype(jnp.float32) + paired.astype(jnp.float32)
+    far = lax.ppermute(blocks[1] + passed, "site", [(1, 3), (2, 0)])
+    held = own + near.astype(jnp.float32) + inward.astype(jnp.float32) + paired.astype(jnp.float32)
     held = lax.optimization_barrier(held)
     return held + far.astype(jnp.float32)
 

time: 50.2 us -> 53.9 us (1.074)
  starting transfers between devices: 12.4 us -> 15.1 us
  waiting for transfers between devices: 21.5 us -> 22.4 us
    ppermute x0 -> x2, waiting for transfers between devices: none -> 15.3 us  [the longest x1 11.9 us: local_work(): far = lax.ppermute(blocks[1] + passed, 'site', [(1, 3), (2, 0)])]
    ppermute x2 -> x1, waiting for transfers between devices: 19.5 us -> 7.08 us  [shifted(): lax.ppermute(block, axis, [(i, (i + distance) % count) for i in range(cou...]
    ppermute x0 -> x2, starting transfers between devices: none -> 6.96 us  [the longest x1 5.67 us: local_work(): inward = lax.ppermute(blocks[1], 'site', [(0, 2), (3, 1)])]
    ppermute x2 -> x1, starting transfers between devices: 9.37 us -> 5.08 us  [shifted(): lax.ppermute(block, axis, [(i, (i + distance) % count) for i in range(cou...]
    ppermute x1, waiting for transfers between devices: 2.06 us -> 0.01 us  [local_work(): passed = lax.ppermute(blocks[0], 'site', [(0, 1), (3, 2)])]
  transfers between devices with their start and end apart: 5 -> 6, of which waited for: 3 -> 3; matrix products, arithmetic and copies ran while one was open for 6% -> 5% of each run, Pallas kernels for 18% -> 17%
where the time goes in v4:
time: 53.9 us; the launch traced here: 53.5 us
  waiting for transfers between devices  22.4 us (42%)
  starting transfers between devices  15.1 us (28%)
  Pallas kernels  11.2 us (21%)
  other arithmetic  2.91 us (5%)
  local copies, waits for them, and re-layouts  1.86 us (3%)
    ppermute x1, waiting for transfers between devices, local_work(): far = lax.ppermute(blocks[1] + passed, 'site', [(1, 3), (2, 0)])  11.9 us
    ppermute x1, waiting for transfers between devices, shifted(): lax.ppermute(block, axis, [(i, (i + distance) % count) for i in range(cou...  7.08 us
    pallas_call x3, Pallas kernels, local_work(): pl.pallas_call(functools.partial(block_kernel, number, layout), out_shape...  6.79 us
    ppermute x1, starting transfers between devices, local_work(): inward = lax.ppermute(blocks[1], 'site', [(0, 2), (3, 1)])  5.67 us
    ppermute x1, starting transfers between devices, shifted(): lax.ppermute(block, axis, [(i, (i + distance) % count) for i in range(cou...  5.08 us
    ppermute x1, waiting for transfers between devices, local_work(): inward = lax.ppermute(blocks[1], 'site', [(0, 2), (3, 1)])  3.4 us
    pallas_call x1, Pallas kernels, local_work(): pl.pallas_call(functools.partial(first_kernel, layout, scale), out_shape=...  2.3 us
    ppermute x1, starting transfers between devices, local_work(): passed = lax.ppermute(blocks[0], 'site', [(0, 1), (3, 2)])  2.26 us
  transfers between devices with their start and end apart: 6, of which 3 were waited for; matrix products, arithmetic and copies ran while one was open for 5% of the time, Pallas kernels for 17%

profile of v4, /device:TPU:0, one launch (start us, length us, event | category | flops | bytes accessed | tf_op | source)
XLA Modules:
  0.0 53.5 jit_solution(3004448288251148630)
XLA Ops:
  0.0 5.1 %collective-permute-start = (bf16[2,3,192,256]{3,2,1,0:T(8,128)(2,1)}, bf16[2,3,192,256]{3,2,1,0:T(8,128)(2,1)S(1)}, u32[]{:S(2)}, u32[]{:S(2)}) collective-permute-start(bf16[2,3,192,256]{3,2,1,0:T(8,128)(2,1)} %bitcast.13), channel_id=1, source_target_pairs={{0,3},{1,0},{2,1},{3,2},{4,7},{5,4},{6,5},{7,6},{8,11},{9,8},{10,9... | collective-permute-start | bytes 1769480 | tf_op jit(solution)/shard_map/ppermute | solution.py:22
  5.1 0.8 %reshape.11 = s32[6]{0:T(128)S(1)} reshape(s32[2,3]{1,0:T(2,128)} %param.6) | data formatting | bytes 48 | tf_op jit(solution)/shard_map/reshape | solution.py:264
  5.8 0.8 %convert_bitcast_fusion = f32[3,3,3,2,1,256]{5,3,4,2,1,0:T(2,128)S(1)} fusion(bf16[2,3,3,3,1,256]{5,0,4,3,2,1:T(2,128)(2,1)} %param.5), kind=kLoop, calls=%fused_computation.7 | loop fusion | flops 13824 | bytes 82944 | tf_op jit(solution)/shard_map/reshape | solution.py:255
  6.7 0.1 add_multiply_fusion
  6.7 0.7 %pad_add_fusion.meta = s32[14]{0:T(128)S(1)} fusion(s32[4]{0:T(128)} %param.7, s32[6]{0:T(128)S(1)} %reshape.11, s32[4]{0:T(128)S(1)} %add_multiply_fusion), kind=kLoop, calls=%fused_computation.19 | loop fusion | flops 28 | bytes 112 | tf_op jit(solution)/shard_map/concatenate | solution.py:263
  7.5 0.2 select_convert_fusion.shifts_ref
  7.7 0.0 copy-start
  7.7 1.1 %copy-done = bf16[2,192,3,1,256]{4,1,3,2,0:T(8,128)(2,1)S(1)} copy-done((bf16[2,192,3,1,256]{4,1,3,2,0:T(8,128)(2,1)S(1)}, bf16[2,192,3,1,256]{4,1,3,2,0:T(8,128)(2,1)}, u32[]{:S(2)}) %copy-start) | copy-done | bytes 589848
  8.8 2.1 %early.1 = (bf16[2,384,768]{2,1,0:T(8,128)(2,1)S(1)}, f32[2,27,4,256]{3,2,1,0:T(4,128)S(1)}, bf16[2,3,192,256]{3,2,1,0:T(8,128)(2,1)S(1)}) custom-call(s32[14]{0:T(128)S(1)} %pad_add_fusion.meta, bf16[2,3,192,256]{3,2,1,0:T(8,128)(2,1)S(1)} %bitcast.14, f32[3,18,256]{2,1,0:T(8,128)S(1)} %reshape.16.links_ref, ...), custom_call_target="tpu_custom_call" | custom-call | flops 500000000 | bytes 4000000 | tf_op jit(solution)/shard_map/early/pallas_call | solution.py:281
  10.9 7.1 %collective-permute-done.next_ref = bf16[2,3,192,256]{3,2,1,0:T(8,128)(2,1)S(1)} collective-permute-done((bf16[2,3,192,256]{3,2,1,0:T(8,128)(2,1)}, bf16[2,3,192,256]{3,2,1,0:T(8,128)(2,1)S(1)}, u32[]{:S(2)}, u32[]{:S(2)}) %collective-permute-start) | collective-permute-done | bytes 589856 | tf_op jit(solution)/shard_map/ppermute | solution.py:22
  18.0 2.3 %first.1 = (bf16[2,384,768]{2,1,0:T(8,128)(2,1)S(1)}, f32[2,27,4,256]{3,2,1,0:T(4,128)S(1)}, bf16[2,4,48,384]{3,2,1,0:T(8,128)(2,1)S(1)}) custom-call(s32[14]{0:T(128)S(1)} %pad_add_fusion.meta, bf16[2,3,192,256]{3,2,1,0:T(8,128)(2,1)S(1)} %get-tuple-element.11.here_ref, ...), custom_call_target="tpu_custom_call", output_to_operand_aliasing={{0}: (5, {}), {1}: (6, {})} | custom-call | tf_op jit(solution)/shard_map/first/pallas_call | solution.py:290
  20.3 2.3 %collective-permute-start.4 = (bf16[2,4,48,384]{3,2,1,0:T(8,128)(2,1)S(1)}, bf16[2,4,48,384]{3,2,1,0:T(8,128)(2,1)S(1)}, u32[]{:S(2)}, u32[]{:S(2)}) collective-permute-start(bf16[2,4,48,384]{3,2,1,0:T(8,128)(2,1)S(1)} %get-tuple-element.16), channel_id=1, source_target_pairs={{0,1},{3,2},{4,5},{7,6},{8,9},{11,10},{12,13},{15,14},{16,17},{19,... | collective-permute-start | bytes 884744 | tf_op jit(solution)/shard_map/ppermute | solution.py:322
  22.6 2.3 %shard_map.48 = bf16[2,4,48,384]{3,2,1,0:T(8,128)(2,1)S(1)} custom-call(s32[14]{0:T(128)S(1)} %pad_add_fusion.meta, bf16[2,3,192,256]{3,2,1,0:T(8,128)(2,1)S(1)} %get-tuple-element.11.here_ref, bf16[2,3,192,256]{3,2,1,0:T(8,128)(2,1)S(1)} %collective-permute-done.next_ref, bf16[3,256,256]{2,1,0:T(8,128)(2,1)S(1)} %select_convert_fusion.shifts_ref, ...), custom_call_target="tpu_custom_call" | custom-call | flops 1000000000 | bytes 4000000 | tf_op jit(solution)/shard_map/pallas_call | solution.py:307
  24.8 0.1 collective-permute-start.3
  24.9 2.3 %shard_map.47 = bf16[2,4,48,384]{3,2,1,0:T(8,128)(2,1)S(1)} custom-call(s32[14]{0:T(128)S(1)} %pad_add_fusion.meta, bf16[2,3,192,256]{3,2,1,0:T(8,128)(2,1)S(1)} %get-tuple-element.11.here_ref, bf16[2,3,192,256]{3,2,1,0:T(8,128)(2,1)S(1)} %collective-permute-done.next_ref, bf16[3,256,256]{2,1,0:T(8,128)(2,1)S(1)} %select_convert_fusion.shifts_ref, ...), custom_call_target="tpu_custom_call" | custom-call | flops 1000000000 | bytes 4000000 | tf_op jit(solution)/shard_map/pallas_call | solution.py:307
  27.2 5.7 %collective-permute-start.2 = (bf16[2,4,48,384]{3,2,1,0:T(8,128)(2,1)S(1)}, bf16[2,4,48,384]{3,2,1,0:T(8,128)(2,1)S(1)}, u32[]{:S(2)}, u32[]{:S(2)}) collective-permute-start(bf16[2,4,48,384]{3,2,1,0:T(8,128)(2,1)S(1)} %shard_map.47), channel_id=1, source_target_pairs={{0,2},{3,1},{4,6},{7,5},{8,10},{11,9},{12,14},{15,13},{16,18},{19,... | collective-permute-start | bytes 884744 | tf_op jit(solution)/shard_map/ppermute | solution.py:323
  32.9 0.7 %collective-permute-start.1 = (bf16[2,4,48,384]{3,2,1,0:T(8,128)(2,1)S(1)}, bf16[2,4,48,384]{3,2,1,0:T(8,128)(2,1)S(1)}, u32[]{:S(2)}, u32[]{:S(2)}) collective-permute-start(bf16[2,4,48,384]{3,2,1,0:T(8,128)(2,1)S(1)} %get-tuple-element.16), channel_id=1, source_target_pairs={{1,2},{2,1},{5,6},{6,5},{9,10},{10,9},{13,14},{14,13},{17,18},{18,... | collective-permute-start | bytes 884744 | tf_op jit(solution)/shard_map/ppermute | solution.py:321
  33.5 0.0 collective-permute-done.4
  33.6 0.1 add.64
  33.6 1.3 %collective-permute-start.5 = (bf16[2,4,48,384]{3,2,1,0:T(8,128)(2,1)S(1)}, bf16[2,4,48,384]{3,2,1,0:T(8,128)(2,1)S(1)}, u32[]{:S(2)}, u32[]{:S(2)}) collective-permute-start(bf16[2,4,48,384]{3,2,1,0:T(8,128)(2,1)S(1)} %add.64), channel_id=1, source_target_pairs={{1,3},{2,0},{5,7},{6,4},{9,11},{10,8},{13,15},{14,12},{17,19},{18,... | collective-permute-start | bytes 884744 | tf_op jit(solution)/shard_map/ppermute | solution.py:325
  34.9 2.3 %shard_map.46 = f32[2,4,48,384]{3,2,1,0:T(8,128)S(1)} custom-call(s32[14]{0:T(128)S(1)} %pad_add_fusion.meta, bf16[2,3,192,256]{3,2,1,0:T(8,128)(2,1)S(1)} %get-tuple-element.11.here_ref, bf16[2,3,192,256]{3,2,1,0:T(8,128)(2,1)S(1)} %collective-permute-done.next_ref, bf16[3,256,256]{2,1,0:T(8,128)(2,1)S(1)} %select_convert_fusion.shifts_ref, ...), custom_call_target="tpu_custom_call" | custom-call | flops 1000000000 | bytes 4000000 | tf_op jit(solution)/shard_map/pallas_call | solution.py:307
  37.2 0.0 collective-permute-done.3
  37.2 3.4 %collective-permute-done.2 = bf16[2,4,48,384]{3,2,1,0:T(8,128)(2,1)S(1)} collective-permute-done((bf16[2,4,48,384]{3,2,1,0:T(8,128)(2,1)S(1)}, bf16[2,4,48,384]{3,2,1,0:T(8,128)(2,1)S(1)}, u32[]{:S(2)}, u32[]{:S(2)}) %collective-permute-start.2) | collective-permute-done | bytes 294944 | tf_op jit(solution)/shard_map/ppermute | solution.py:323
  40.6 0.0 collective-permute-done.1
  40.6 0.2 convert_add_fusion.1
  40.8 11.9 %collective-permute-done.5 = bf16[2,4,48,384]{3,2,1,0:T(8,128)(2,1)S(1)} collective-permute-done((bf16[2,4,48,384]{3,2,1,0:T(8,128)(2,1)S(1)}, bf16[2,4,48,384]{3,2,1,0:T(8,128)(2,1)S(1)}, u32[]{:S(2)}, u32[]{:S(2)}) %collective-permute-start.5) | collective-permute-done | bytes 294944 | tf_op jit(solution)/shard_map/ppermute | solution.py:325
  52.7 0.9 %convert_add_fusion = f32[2,4,48,384]{3,2,1,0:T(8,128)} fusion(f32[2,4,48,384]{3,2,1,0:T(8,128)S(1)} %convert_add_fusion.1, bf16[2,4,48,384]{3,2,1,0:T(8,128)(2,1)S(1)} %collective-permute-done.5), kind=kLoop, calls=%fused_computation.5 | loop fusion | flops 294912 | bytes 1474560 | tf_op jit(solution)/shard_map/add | solution.py:328
  (5 shorter events, 0.1 us)
Async XLA Ops:
  0.0 18.0 %collective-permute-start = (bf16[2,3,192,256]{3,2,1,0:T(8,128)(2,1)}, bf16[2,3,192,256]{3,2,1,0:T(8,128)(2,1)S(1)}, u32[]{:S(2)}, u32[]{:S(2)}) collective-permute-start(bf16[2,3,192,256]{3,2,1,0:T(8,128)(2,1)} %bitcast.13), channel_id=1, source_target_pairs={{0,3},{1,0},{2,1},{3,2},{4,7},{5,4},{6,5},{7,6},{8,11},{9,8},{10,9... | collective-permute-start | bytes 1769480 | tf_op jit(solution)/shard_map/ppermute | solution.py:22
  7.7 1.1 %copy-start = (bf16[2,192,3,1,256]{4,1,3,2,0:T(8,128)(2,1)S(1)}, bf16[2,192,3,1,256]{4,1,3,2,0:T(8,128)(2,1)}, u32[]{:S(2)}) copy-start(bf16[2,192,3,1,256]{4,1,3,2,0:T(8,128)(2,1)} %param.4) | copy-start | bytes 1769476
  20.3 13.3 %collective-permute-start.4 = (bf16[2,4,48,384]{3,2,1,0:T(8,128)(2,1)S(1)}, bf16[2,4,48,384]{3,2,1,0:T(8,128)(2,1)S(1)}, u32[]{:S(2)}, u32[]{:S(2)}) collective-permute-start(bf16[2,4,48,384]{3,2,1,0:T(8,128)(2,1)S(1)} %get-tuple-element.16), channel_id=1, source_target_pairs={{0,1},{3,2},{4,5},{7,6},{8,9},{11,10},{12,13},{15,14},{16,17},{19,... | collective-permute-start | bytes 884744 | tf_op jit(solution)/shard_map/ppermute | solution.py:322
  24.8 12.4 %collective-permute-start.3 = (bf16[2,4,48,384]{3,2,1,0:T(8,128)(2,1)S(1)}, bf16[2,4,48,384]{3,2,1,0:T(8,128)(2,1)S(1)}, u32[]{:S(2)}, u32[]{:S(2)}) collective-permute-start(bf16[2,4,48,384]{3,2,1,0:T(8,128)(2,1)S(1)} %shard_map.48), channel_id=1, source_target_pairs={{0,1},{1,0},{2,3},{3,2},{4,5},{5,4},{6,7},{7,6},{8,9},{9,8},{10,11... | collective-permute-start | bytes 884744 | tf_op jit(solution)/shard_map/ppermute | solution.py:324
  27.2 13.4 %collective-permute-start.2 = (bf16[2,4,48,384]{3,2,1,0:T(8,128)(2,1)S(1)}, bf16[2,4,48,384]{3,2,1,0:T(8,128)(2,1)S(1)}, u32[]{:S(2)}, u32[]{:S(2)}) collective-permute-start(bf16[2,4,48,384]{3,2,1,0:T(8,128)(2,1)S(1)} %shard_map.47), channel_id=1, source_target_pairs={{0,2},{3,1},{4,6},{7,5},{8,10},{11,9},{12,14},{15,13},{16,18},{19,... | collective-permute-start | bytes 884744 | tf_op jit(solution)/shard_map/ppermute | solution.py:323
  32.9 7.8 %collective-permute-start.1 = (bf16[2,4,48,384]{3,2,1,0:T(8,128)(2,1)S(1)}, bf16[2,4,48,384]{3,2,1,0:T(8,128)(2,1)S(1)}, u32[]{:S(2)}, u32[]{:S(2)}) collective-permute-start(bf16[2,4,48,384]{3,2,1,0:T(8,128)(2,1)S(1)} %get-tuple-element.16), channel_id=1, source_target_pairs={{1,2},{2,1},{5,6},{6,5},{9,10},{10,9},{13,14},{14,13},{17,18},{18,... | collective-permute-start | bytes 884744 | tf_op jit(solution)/shard_map/ppermute | solution.py:321
  33.6 19.0 %collective-permute-start.5 = (bf16[2,4,48,384]{3,2,1,0:T(8,128)(2,1)S(1)}, bf16[2,4,48,384]{3,2,1,0:T(8,128)(2,1)S(1)}, u32[]{:S(2)}, u32[]{:S(2)}) collective-permute-start(bf16[2,4,48,384]{3,2,1,0:T(8,128)(2,1)S(1)} %add.64), channel_id=1, source_target_pairs={{1,3},{2,0},{5,7},{6,4},{9,11},{10,8},{13,15},{14,12},{17,19},{18,... | collective-permute-start | bytes 884744 | tf_op jit(solution)/shard_map/ppermute | solution.py:325

commit v5 on v3

--- a/solution.py
+++ b/solution.py
@@ -318,11 +318,10 @@
     if not folded:
         arrived = [shifted(block, "site", offset + 1) for offset, block in enumerate(blocks)]
         return functools.reduce(lambda total, block: total + block.astype(jnp.float32), arrived, own)
-    near = lax.ppermute(blocks[0], "site", [(1, 2), (2, 1)])
-    passed = lax.ppermute(blocks[0], "site", [(0, 1), (3, 2)])
-    far = shifted(blocks[1] + passed, "site", 2)
+    mirrored = lax.ppermute(blocks[0], "site", [(i, last - i) for i in range(ring)])
+    far = shifted(blocks[1], "site", 2)
     paired = lax.ppermute(blocks[2], "site", [(0, 1), (1, 0), (2, 3), (3, 2)])
-    held = own + near.astype(jnp.float32) + paired.astype(jnp.float32)
+    held = own + mirrored.astype(jnp.float32) + paired.astype(jnp.float32)
     held = lax.optimization_barrier(held)
     return held + far.astype(jnp.float32)
 

time: 50.2 us -> 53.3 us (1.062)
  waiting for transfers between devices: 21.5 us -> 27.2 us
  starting transfers between devices: 12.4 us -> 9.94 us
    ppermute x2 -> x1, waiting for transfers between devices: 2.06 us -> 9.1 us  [local_work(): lax.ppermute(blocks[0], 'site', [(i, last - i) for i in range(ring)])]
    ppermute x2, starting transfers between devices: 9.37 us -> 5.63 us  [shifted(): lax.ppermute(block, axis, [(i, (i + distance) % count) for i in range(cou...]
    ppermute x2, waiting for transfers between devices: 19.5 us -> 18.1 us  [shifted(): lax.ppermute(block, axis, [(i, (i + distance) % count) for i in range(cou...]
    ppermute x2 -> x1, starting transfers between devices: 2.94 us -> 3.91 us  [local_work(): lax.ppermute(blocks[0], 'site', [(i, last - i) for i in range(ring)])]
  transfers between devices with their start and end apart: 5 -> 4, of which waited for: 3 -> 3; matrix products, arithmetic and copies ran while one was open for 6% -> 5% of each run, Pallas kernels for 18% -> 13%
where the time goes in v5:
time: 53.3 us; the launch traced here: 53.1 us
  waiting for transfers between devices  27.2 us (51%)
  Pallas kernels  11.2 us (21%)
  starting transfers between devices  9.94 us (19%)
  other arithmetic  2.79 us (5%)
  local copies, waits for them, and re-layouts  1.86 us (3%)
    ppermute x2, waiting for transfers between devices, shifted(): lax.ppermute(block, axis, [(i, (i + distance) % count) for i in range(cou...  18.1 us
    ppermute x1, waiting for transfers between devices, local_work(): lax.ppermute(blocks[0], 'site', [(i, last - i) for i in range(ring)])  9.1 us
    pallas_call x3, Pallas kernels, local_work(): pl.pallas_call(functools.partial(block_kernel, number, layout), out_shape...  6.78 us
    ppermute x2, starting transfers between devices, shifted(): lax.ppermute(block, axis, [(i, (i + distance) % count) for i in range(cou...  5.63 us
    ppermute x1, starting transfers between devices, local_work(): lax.ppermute(blocks[0], 'site', [(i, last - i) for i in range(ring)])  3.91 us
    pallas_call x1, Pallas kernels, local_work(): pl.pallas_call(functools.partial(first_kernel, layout, scale), out_shape=...  2.3 us
    pallas_call x1, Pallas kernels, local_work(): pl.pallas_call(functools.partial(early_kernel, layout, scale), out_shape=...  2.14 us
  transfers between devices with their start and end apart: 4, of which 3 were waited for; matrix products, arithmetic and copies ran while one was open for 5% of the time, Pallas kernels for 13%

profile of v5, /device:TPU:0, one launch (start us, length us, event | category | flops | bytes accessed | tf_op | source)
XLA Modules:
  0.0 53.1 jit_solution(6484568591609450228)
XLA Ops:
  0.0 5.1 %collective-permute-start = (bf16[2,3,192,256]{3,2,1,0:T(8,128)(2,1)}, bf16[2,3,192,256]{3,2,1,0:T(8,128)(2,1)S(1)}, u32[]{:S(2)}, u32[]{:S(2)}) collective-permute-start(bf16[2,3,192,256]{3,2,1,0:T(8,128)(2,1)} %bitcast.13), channel_id=1, source_target_pairs={{0,3},{1,0},{2,1},{3,2},{4,7},{5,4},{6,5},{7,6},{8,11},{9,8},{10,9... | collective-permute-start | bytes 1769480 | tf_op jit(solution)/shard_map/ppermute | solution.py:22
  5.1 0.8 %reshape.11 = s32[6]{0:T(128)S(1)} reshape(s32[2,3]{1,0:T(2,128)} %param.6) | data formatting | bytes 48 | tf_op jit(solution)/shard_map/reshape | solution.py:264
  5.8 0.8 %convert_bitcast_fusion = f32[3,3,3,2,1,256]{5,3,4,2,1,0:T(2,128)S(1)} fusion(bf16[2,3,3,3,1,256]{5,0,4,3,2,1:T(2,128)(2,1)} %param.5), kind=kLoop, calls=%fused_computation.7 | loop fusion | flops 13824 | bytes 82944 | tf_op jit(solution)/shard_map/reshape | solution.py:255
  6.7 0.1 add_multiply_fusion
  6.7 0.7 %pad_add_fusion.meta = s32[14]{0:T(128)S(1)} fusion(s32[4]{0:T(128)} %param.7, s32[6]{0:T(128)S(1)} %reshape.11, s32[4]{0:T(128)S(1)} %add_multiply_fusion), kind=kLoop, calls=%fused_computation.19 | loop fusion | flops 28 | bytes 112 | tf_op jit(solution)/shard_map/concatenate | solution.py:263
  7.5 0.2 select_convert_fusion.shifts_ref
  7.7 0.0 copy-start
  7.7 1.1 %copy-done = bf16[2,192,3,1,256]{4,1,3,2,0:T(8,128)(2,1)S(1)} copy-done((bf16[2,192,3,1,256]{4,1,3,2,0:T(8,128)(2,1)S(1)}, bf16[2,192,3,1,256]{4,1,3,2,0:T(8,128)(2,1)}, u32[]{:S(2)}) %copy-start) | copy-done | bytes 589848
  8.8 2.1 %early.1 = (bf16[2,384,768]{2,1,0:T(8,128)(2,1)S(1)}, f32[2,27,4,256]{3,2,1,0:T(4,128)S(1)}, bf16[2,3,192,256]{3,2,1,0:T(8,128)(2,1)S(1)}) custom-call(s32[14]{0:T(128)S(1)} %pad_add_fusion.meta, bf16[2,3,192,256]{3,2,1,0:T(8,128)(2,1)S(1)} %bitcast.14, f32[3,18,256]{2,1,0:T(8,128)S(1)} %reshape.16.links_ref, ...), custom_call_target="tpu_custom_call" | custom-call | flops 500000000 | bytes 4000000 | tf_op jit(solution)/shard_map/early/pallas_call | solution.py:281
  10.9 7.1 %collective-permute-done.next_ref = bf16[2,3,192,256]{3,2,1,0:T(8,128)(2,1)S(1)} collective-permute-done((bf16[2,3,192,256]{3,2,1,0:T(8,128)(2,1)}, bf16[2,3,192,256]{3,2,1,0:T(8,128)(2,1)S(1)}, u32[]{:S(2)}, u32[]{:S(2)}) %collective-permute-start) | collective-permute-done | bytes 589856 | tf_op jit(solution)/shard_map/ppermute | solution.py:22
  18.0 2.3 %first.1 = (bf16[2,384,768]{2,1,0:T(8,128)(2,1)S(1)}, f32[2,27,4,256]{3,2,1,0:T(4,128)S(1)}, bf16[2,4,48,384]{3,2,1,0:T(8,128)(2,1)S(1)}) custom-call(s32[14]{0:T(128)S(1)} %pad_add_fusion.meta, bf16[2,3,192,256]{3,2,1,0:T(8,128)(2,1)S(1)} %get-tuple-element.11.here_ref, ...), custom_call_target="tpu_custom_call", output_to_operand_aliasing={{0}: (5, {}), {1}: (6, {})} | custom-call | tf_op jit(solution)/shard_map/first/pallas_call | solution.py:290
  20.3 2.3 %shard_map.47 = bf16[2,4,48,384]{3,2,1,0:T(8,128)(2,1)S(1)} custom-call(s32[14]{0:T(128)S(1)} %pad_add_fusion.meta, bf16[2,3,192,256]{3,2,1,0:T(8,128)(2,1)S(1)} %get-tuple-element.11.here_ref, bf16[2,3,192,256]{3,2,1,0:T(8,128)(2,1)S(1)} %collective-permute-done.next_ref, bf16[3,256,256]{2,1,0:T(8,128)(2,1)S(1)} %select_convert_fusion.shifts_ref, ...), custom_call_target="tpu_custom_call" | custom-call | flops 1000000000 | bytes 4000000 | tf_op jit(solution)/shard_map/pallas_call | solution.py:307
  22.6 0.4 collective-permute-start.2
  23.0 3.9 %collective-permute-start.1 = (bf16[2,4,48,384]{3,2,1,0:T(8,128)(2,1)S(1)}, bf16[2,4,48,384]{3,2,1,0:T(8,128)(2,1)S(1)}, u32[]{:S(2)}, u32[]{:S(2)}) collective-permute-start(bf16[2,4,48,384]{3,2,1,0:T(8,128)(2,1)S(1)} %get-tuple-element.16), channel_id=1, source_target_pairs={{0,3},{1,2},{2,1},{3,0},{4,7},{5,6},{6,5},{7,4},{8,11},{9,10},{10,... | collective-permute-start | bytes 884744 | tf_op jit(solution)/shard_map/ppermute | solution.py:321
  26.9 2.3 %shard_map.48 = bf16[2,4,48,384]{3,2,1,0:T(8,128)(2,1)S(1)} custom-call(s32[14]{0:T(128)S(1)} %pad_add_fusion.meta, bf16[2,3,192,256]{3,2,1,0:T(8,128)(2,1)S(1)} %get-tuple-element.11.here_ref, bf16[2,3,192,256]{3,2,1,0:T(8,128)(2,1)S(1)} %collective-permute-done.next_ref, bf16[3,256,256]{2,1,0:T(8,128)(2,1)S(1)} %select_convert_fusion.shifts_ref, ...), custom_call_target="tpu_custom_call" | custom-call | flops 1000000000 | bytes 4000000 | tf_op jit(solution)/shard_map/pallas_call | solution.py:307
  29.1 0.6 %collective-permute-start.3 = (bf16[2,4,48,384]{3,2,1,0:T(8,128)(2,1)S(1)}, bf16[2,4,48,384]{3,2,1,0:T(8,128)(2,1)S(1)}, u32[]{:S(2)}, u32[]{:S(2)}) collective-permute-start(bf16[2,4,48,384]{3,2,1,0:T(8,128)(2,1)S(1)} %shard_map.48), channel_id=1, source_target_pairs={{0,2},{1,3},{2,0},{3,1},{4,6},{5,7},{6,4},{7,5},{8,10},{9,11},{10,... | collective-permute-start | bytes 884744 | tf_op jit(solution)/shard_map/ppermute | solution.py:22
  29.7 2.3 %shard_map.46 = f32[2,4,48,384]{3,2,1,0:T(8,128)S(1)} custom-call(s32[14]{0:T(128)S(1)} %pad_add_fusion.meta, bf16[2,3,192,256]{3,2,1,0:T(8,128)(2,1)S(1)} %get-tuple-element.11.here_ref, bf16[2,3,192,256]{3,2,1,0:T(8,128)(2,1)S(1)} %collective-permute-done.next_ref, bf16[3,256,256]{2,1,0:T(8,128)(2,1)S(1)} %select_convert_fusion.shifts_ref, ...), custom_call_target="tpu_custom_call" | custom-call | flops 1000000000 | bytes 4000000 | tf_op jit(solution)/shard_map/pallas_call | solution.py:307
  32.0 0.0 collective-permute-done.2
  32.0 9.1 %collective-permute-done.1 = bf16[2,4,48,384]{3,2,1,0:T(8,128)(2,1)S(1)} collective-permute-done((bf16[2,4,48,384]{3,2,1,0:T(8,128)(2,1)S(1)}, bf16[2,4,48,384]{3,2,1,0:T(8,128)(2,1)S(1)}, u32[]{:S(2)}, u32[]{:S(2)}) %collective-permute-start.1) | collective-permute-done | bytes 294944 | tf_op jit(solution)/shard_map/ppermute | solution.py:321
  41.1 0.1 convert_add_fusion.1
  41.2 11.0 %collective-permute-done.3 = bf16[2,4,48,384]{3,2,1,0:T(8,128)(2,1)S(1)} collective-permute-done((bf16[2,4,48,384]{3,2,1,0:T(8,128)(2,1)S(1)}, bf16[2,4,48,384]{3,2,1,0:T(8,128)(2,1)S(1)}, u32[]{:S(2)}, u32[]{:S(2)}) %collective-permute-start.3) | collective-permute-done | bytes 294944 | tf_op jit(solution)/shard_map/ppermute | solution.py:22
  52.2 0.9 %convert_add_fusion = f32[2,4,48,384]{3,2,1,0:T(8,128)} fusion(f32[2,4,48,384]{3,2,1,0:T(8,128)S(1)} %convert_add_fusion.1, bf16[2,4,48,384]{3,2,1,0:T(8,128)(2,1)S(1)} %collective-permute-done.3), kind=kLoop, calls=%fused_computation.5 | loop fusion | flops 294912 | bytes 1474560 | tf_op jit(solution)/shard_map/add | solution.py:326
  (5 shorter events, 0.1 us)
Async XLA Ops:
  0.0 18.0 %collective-permute-start = (bf16[2,3,192,256]{3,2,1,0:T(8,128)(2,1)}, bf16[2,3,192,256]{3,2,1,0:T(8,128)(2,1)S(1)}, u32[]{:S(2)}, u32[]{:S(2)}) collective-permute-start(bf16[2,3,192,256]{3,2,1,0:T(8,128)(2,1)} %bitcast.13), channel_id=1, source_target_pairs={{0,3},{1,0},{2,1},{3,2},{4,7},{5,4},{6,5},{7,6},{8,11},{9,8},{10,9... | collective-permute-start | bytes 1769480 | tf_op jit(solution)/shard_map/ppermute | solution.py:22
  7.7 1.1 %copy-start = (bf16[2,192,3,1,256]{4,1,3,2,0:T(8,128)(2,1)S(1)}, bf16[2,192,3,1,256]{4,1,3,2,0:T(8,128)(2,1)}, u32[]{:S(2)}) copy-start(bf16[2,192,3,1,256]{4,1,3,2,0:T(8,128)(2,1)} %param.4) | copy-start | bytes 1769476
  22.6 9.4 %collective-permute-start.2 = (bf16[2,4,48,384]{3,2,1,0:T(8,128)(2,1)S(1)}, bf16[2,4,48,384]{3,2,1,0:T(8,128)(2,1)S(1)}, u32[]{:S(2)}, u32[]{:S(2)}) collective-permute-start(bf16[2,4,48,384]{3,2,1,0:T(8,128)(2,1)S(1)} %shard_map.47), channel_id=1, source_target_pairs={{0,1},{1,0},{2,3},{3,2},{4,5},{5,4},{6,7},{7,6},{8,9},{9,8},{10,11... | collective-permute-start | bytes 884744 | tf_op jit(solution)/shard_map/ppermute | solution.py:323
  23.0 18.1 %collective-permute-start.1 = (bf16[2,4,48,384]{3,2,1,0:T(8,128)(2,1)S(1)}, bf16[2,4,48,384]{3,2,1,0:T(8,128)(2,1)S(1)}, u32[]{:S(2)}, u32[]{:S(2)}) collective-permute-start(bf16[2,4,48,384]{3,2,1,0:T(8,128)(2,1)S(1)} %get-tuple-element.16), channel_id=1, source_target_pairs={{0,3},{1,2},{2,1},{3,0},{4,7},{5,6},{6,5},{7,4},{8,11},{9,10},{10,... | collective-permute-start | bytes 884744 | tf_op jit(solution)/shard_map/ppermute | solution.py:321
  29.1 23.0 %collective-permute-start.3 = (bf16[2,4,48,384]{3,2,1,0:T(8,128)(2,1)S(1)}, bf16[2,4,48,384]{3,2,1,0:T(8,128)(2,1)S(1)}, u32[]{:S(2)}, u32[]{:S(2)}) collective-permute-start(bf16[2,4,48,384]{3,2,1,0:T(8,128)(2,1)S(1)} %shard_map.48), channel_id=1, source_target_pairs={{0,2},{1,3},{2,0},{3,1},{4,6},{5,7},{6,4},{7,5},{8,10},{9,11},{10,... | collective-permute-start | bytes 884744 | tf_op jit(solution)/shard_map/ppermute | solution.py:22

commit v6 on v3

--- a/solution.py
+++ b/solution.py
@@ -63,9 +63,26 @@
     return [[entry(row, column) for column in range(COLORS)] for row in range(COLORS)]
 
 
-def site_matrices(combo, moves, rows, here_ref, next_ref, links_ref, shifts_ref, matrices_ref, scale):
-    vectors = here_ref.shape[-2]
-    direction = moves[combo, 0]
+def join_links(combo, moves, links_ref, joins_ref, scale):
+    first, second, third = (chosen_link(links_ref, moves[combo, slot]) for slot in range(3))
+    for a in range(COLORS):
+        for b in range(COLORS):
+            for part in range(2):
+                at = 2 * (COLORS * a + b) + part
+                joins_ref[combo, at : at + 1, :] = first[a][b][part] * scale
+    for a in range(COLORS):
+        up, down = (a + 1) % COLORS, (a + 2) % COLORS
+        for column in range(COLORS):
+            for row in range(COLORS):
+                plus = mul(second[up][row], third[down][column])
+                minus = mul(second[down][row], third[up][column])
+                at = 2 * (COLORS * COLORS * (1 + a) + COLORS * column + row)
+                for part in range(2):
+                    joins_ref[combo, at + part : at + part + 1, :] = plus[part] - minus[part]
+
+
+def site_matrices(combo, rows, plane_ref, shift, joins_ref, matrices_ref):
+    vectors = plane_ref.shape[-2]
     kept, picks = matrices_ref.shape[2], SUBLANES
     numbers = lax.broadcasted_iota(jnp.int32, (picks, vectors), 1)
     lane = lax.broadcasted_iota(jnp.int32, (picks, vectors), 0)
@@ -73,59 +90,47 @@
     for i in range(rows.shape[0]):
         wanted = jnp.where(lane == i, rows[i], wanted)
     select = jnp.where(numbers == wanted, 1.0, 0.0).astype(jnp.bfloat16)
-
-    def picked(part, color):
-        return jnp.dot(
-            select,
-            plane_of(here_ref, next_ref, direction, (part, color)),
-            preferred_element_type=jnp.float32,
-        )
-
     stacked = jnp.concatenate(
-        [picked(part, color) for color in range(COLORS) for part in range(2)], axis=0
+        [
+            jnp.dot(select, plane_ref[part, color], preferred_element_type=jnp.float32)
+            for color in range(COLORS)
+            for part in range(2)
+        ],
+        axis=0,
     )
-    stacked = jnp.dot(
-        stacked.astype(jnp.bfloat16), in_plane(shifts_ref, direction), preferred_element_type=jnp.float32
-    )
+    if shift is not None:
+        stacked = jnp.dot(stacked.astype(jnp.bfloat16), shift, preferred_element_type=jnp.float32)
     fields = [
         tuple(stacked[at * picks : (at + 1) * picks] for at in (2 * color, 2 * color + 1))
         for color in range(COLORS)
     ]
-    first, second, third = (chosen_link(links_ref, moves[combo, slot]) for slot in range(3))
+
+    def joined(at):
+        return tuple(joins_ref[combo, 2 * at + part : 2 * at + part + 1, :] for part in range(2))
 
     def total(terms):
         return functools.reduce(add, terms)
 
     left = [
-        total(mul(first[a][b], fields[b]) for b in range(COLORS)) for a in range(COLORS)
+        total(mul(joined(COLORS * a + b), fields[b]) for b in range(COLORS)) for a in range(COLORS)
     ]
-    left = [(re * scale, im * scale) for re, im in left]
-    for column in range(COLORS):
-        after = []
-        for b in range(COLORS):
-            up, down = (b + 1) % COLORS, (b + 2) % COLORS
-            plus = mul(third[up][column], left[down])
-            minus = mul(third[down][column], left[up])
-            after.append((plus[0] - minus[0], plus[1] - minus[1]))
-        for row in range(COLORS):
-            re, im = total(mul(second[b][row], after[b]) for b in range(COLORS))
-            at = COLORS * (COLORS * column + row)
-            matrices_ref[combo, at] = (re + im)[:kept]
-            matrices_ref[combo, at + 1] = re[:kept]
-            matrices_ref[combo, at + 2] = im[:kept]
-
-
-def right_operand(combo, moves, here_ref, next_ref, shifts_ref, right_ref):
-    vectors, sites = here_ref.shape[-2:]
-    direction = moves[combo, 2]
-    shift = in_plane(shifts_ref, direction)
+    for place in range(COLORS * COLORS):
+        re, im = total(
+            mul(joined(COLORS * COLORS * (1 + a) + place), left[a]) for a in range(COLORS)
+        )
+        at = COLORS * place
+        matrices_ref[combo, at] = (re + im)[:kept]
+        matrices_ref[combo, at + 1] = re[:kept]
+        matrices_ref[combo, at + 2] = im[:kept]
+
+
+def right_operand(combo, plane_ref, shift, right_ref):
+    vectors, sites = plane_ref.shape[-2:]
     for color in range(COLORS):
         for part in range(2):
-            field = jnp.dot(
-                plane_of(here_ref, next_ref, direction, (part, color)),
-                shift,
-                preferred_element_type=jnp.float32,
-            )
+            field = plane_ref[part, color]
+            if shift is not None:
+                field = jnp.dot(field, shift, preferred_element_type=jnp.float32)
             right_ref[
                 combo, part * vectors : (part + 1) * vectors, color * sites : (color + 1) * sites
             ] = field.astype(right_ref.dtype)
@@ -208,26 +213,31 @@
     return Moves(), Rows()
 
 
-def prepare(of_next, layout, scale, meta, here_ref, next_ref, links_ref, shifts_ref, right_ref, matrices_ref):
+def prepare(of_next, layout, meta, plane_ref, shifts_ref, joins_ref, right_ref, matrices_ref):
     moves, rows = moves_of(meta, layout)
     for combo in range(layout[1]):
 
         @pl.when((moves[combo, 0] == 3) == of_next)
         def _(combo=combo):
-            site_matrices(combo, moves, rows, here_ref, next_ref, links_ref, shifts_ref, matrices_ref, scale)
+            shift = None if of_next else in_plane(shifts_ref, moves[combo, 0])
+            site_matrices(combo, rows, plane_ref, shift, joins_ref, matrices_ref)
 
         @pl.when((moves[combo, 2] == 3) == of_next)
         def _(combo=combo):
-            right_operand(combo, moves, here_ref, next_ref, shifts_ref, right_ref)
-
-
-def early_kernel(layout, scale, meta, here_ref, links_ref, shifts_ref, right_ref, matrices_ref, copy_ref):
+            shift = None if of_next else in_plane(shifts_ref, moves[combo, 2])
+            right_operand(combo, plane_ref, shift, right_ref)
+
+
+def early_kernel(layout, scale, meta, here_ref, links_ref, shifts_ref, right_ref, matrices_ref, copy_ref, joins_ref):
     copy_ref[...] = here_ref[...]
-    prepare(False, layout, scale, meta, here_ref, here_ref, links_ref, shifts_ref, right_ref, matrices_ref)
-
-
-def first_kernel(layout, scale, meta, here_ref, next_ref, links_ref, shifts_ref, right_in, matrices_in, right_ref, matrices_ref, out_ref, turned_ref, mid_ref, crossed_ref):
-    prepare(True, layout, scale, meta, here_ref, next_ref, links_ref, shifts_ref, right_ref, matrices_ref)
+    moves, _ = moves_of(meta, layout)
+    for combo in range(layout[1]):
+        join_links(combo, moves, links_ref, joins_ref, scale)
+    prepare(False, layout, meta, here_ref, shifts_ref, joins_ref, right_ref, matrices_ref)
+
+
+def first_kernel(layout, meta, here_ref, next_ref, joins_ref, shifts_ref, right_in, matrices_in, right_ref, matrices_ref, out_ref, turned_ref, mid_ref, crossed_ref):
+    prepare(True, layout, meta, next_ref, shifts_ref, joins_ref, right_ref, matrices_ref)
     turn(right_ref, turned_ref)
     moves, _ = moves_of(meta, layout)
     for combo in range(layout[1]):
@@ -268,6 +278,7 @@
     vmem = pl.BlockSpec(memory_space=pltpu.VMEM)
     right = jax.ShapeDtypeStruct((combos, parts * vectors, colors * sites), jnp.bfloat16)
     matrices = jax.ShapeDtypeStruct((combos, 3 * colors * colors, picks, sites), jnp.float32)
+    joins = jax.ShapeDtypeStruct((combos, 2 * (1 + colors) * colors * colors, sites), jnp.float32)
     scratch = [
         pltpu.VMEM(right.shape, right.dtype),
         pltpu.VMEM((combos, 3 * colors * count, sites), jnp.float32),
@@ -278,17 +289,17 @@
     def chunk(kind):
         return jax.ShapeDtypeStruct((combos, picks, count, 2 * vectors), kind)
 
-    right, matrices, here = pl.pallas_call(
+    right, matrices, here, joins = pl.pallas_call(
         functools.partial(early_kernel, layout, scale),
-        out_shape=(right, matrices, jax.ShapeDtypeStruct(here.shape, here.dtype)),
+        out_shape=(right, matrices, jax.ShapeDtypeStruct(here.shape, here.dtype), joins),
         in_specs=[smem, vmem, vmem, vmem],
-        out_specs=(vmem, vmem, vmem),
+        out_specs=(vmem, vmem, vmem, vmem),
         compiler_params=params,
         cost_estimate=pl.CostEstimate(flops=500_000_000, bytes_accessed=4_000_000, transcendentals=0),
         name="early",
     )(meta, here, links, shifts)
     right, matrices, sent = pl.pallas_call(
-        functools.partial(first_kernel, layout, scale),
+        functools.partial(first_kernel, layout),
         out_shape=(
             jax.ShapeDtypeStruct(right.shape, right.dtype),
             jax.ShapeDtypeStruct(matrices.shape, matrices.dtype),
@@ -300,7 +311,7 @@
         scratch_shapes=scratch,
         compiler_params=params,
         name="first",
-    )(meta, here, after, links, shifts, right, matrices)
+    )(meta, here, after, joins, shifts, right, matrices)
     blocks = [sent]
     for number in range(1, ring):
         blocks.append(

time: 50.2 us -> 50.2 us (level)
  no operation moved by 1% of the time
where the time goes in v6:
time: 50.2 us; the launch traced here: 49.9 us
  waiting for transfers between devices  21.5 us (43%)
  starting transfers between devices  12.4 us (25%)
  Pallas kernels  11.2 us (22%)
  other arithmetic  2.83 us (6%)
  local copies, waits for them, and re-layouts  1.86 us (4%)
    ppermute x2, waiting for transfers between devices, shifted(): lax.ppermute(block, axis, [(i, (i + distance) % count) for i in range(cou...  19.4 us
    ppermute x2, starting transfers between devices, shifted(): lax.ppermute(block, axis, [(i, (i + distance) % count) for i in range(cou...  9.36 us
    pallas_call x3, Pallas kernels, local_work(): pl.pallas_call(functools.partial(block_kernel, number, layout), out_shape...  6.75 us
    pallas_call x1, Pallas kernels, local_work(): pl.pallas_call(functools.partial(first_kernel, layout), out_shape=(jax.Sh...  2.28 us
    ppermute x1, starting transfers between devices, local_work(): passed = lax.ppermute(blocks[0], 'site', [(0, 1), (3, 2)])  2.28 us
    pallas_call x1, Pallas kernels, local_work(): pl.pallas_call(functools.partial(early_kernel, layout, scale), out_shape=...  2.17 us
    ppermute x1, waiting for transfers between devices, local_work(): passed = lax.ppermute(blocks[0], 'site', [(0, 1), (3, 2)])  2.08 us
    unnamed x2, local copies, waits for them, and re-layouts  1.06 us
  transfers between devices with their start and end apart: 5, of which 3 were waited for; matrix products, arithmetic and copies ran while one was open for 6% of the time, Pallas kernels for 18%

profile of v6, /device:TPU:0, one launch (start us, length us, event | category | flops | bytes accessed | tf_op | source)
XLA Modules:
  0.0 49.9 jit_solution(12618732070839479366)
XLA Ops:
  0.0 5.1 %collective-permute-start = (bf16[2,3,192,256]{3,2,1,0:T(8,128)(2,1)}, bf16[2,3,192,256]{3,2,1,0:T(8,128)(2,1)S(1)}, u32[]{:S(2)}, u32[]{:S(2)}) collective-permute-start(bf16[2,3,192,256]{3,2,1,0:T(8,128)(2,1)} %bitcast.13), channel_id=1, source_target_pairs={{0,3},{1,0},{2,1},{3,2},{4,7},{5,4},{6,5},{7,6},{8,11},{9,8},{10,9... | collective-permute-start | bytes 1769480 | tf_op jit(solution)/shard_map/ppermute | solution.py:22
  5.1 0.8 %reshape.11 = s32[6]{0:T(128)S(1)} reshape(s32[2,3]{1,0:T(2,128)} %param.6) | data formatting | bytes 48 | tf_op jit(solution)/shard_map/reshape | solution.py:274
  5.8 0.8 %convert_bitcast_fusion = f32[3,3,3,2,1,256]{5,3,4,2,1,0:T(2,128)S(1)} fusion(bf16[2,3,3,3,1,256]{5,0,4,3,2,1:T(2,128)(2,1)} %param.5), kind=kLoop, calls=%fused_computation.7 | loop fusion | flops 13824 | bytes 82944 | tf_op jit(solution)/shard_map/reshape | solution.py:265
  6.7 0.1 add_multiply_fusion
  6.7 0.7 %pad_add_fusion.meta = s32[14]{0:T(128)S(1)} fusion(s32[4]{0:T(128)} %param.7, s32[6]{0:T(128)S(1)} %reshape.11, s32[4]{0:T(128)S(1)} %add_multiply_fusion), kind=kLoop, calls=%fused_computation.19 | loop fusion | flops 28 | bytes 112 | tf_op jit(solution)/shard_map/concatenate | solution.py:273
  7.5 0.2 select_convert_fusion.shifts_ref
  7.7 0.0 copy-start
  7.7 1.1 %copy-done = bf16[2,192,3,1,256]{4,1,3,2,0:T(8,128)(2,1)S(1)} copy-done((bf16[2,192,3,1,256]{4,1,3,2,0:T(8,128)(2,1)S(1)}, bf16[2,192,3,1,256]{4,1,3,2,0:T(8,128)(2,1)}, u32[]{:S(2)}) %copy-start) | copy-done | bytes 589848
  8.8 2.2 %early.1 = (bf16[2,384,768]{2,1,0:T(8,128)(2,1)S(1)}, f32[2,27,4,256]{3,2,1,0:T(4,128)S(1)}, bf16[2,3,192,256]{3,2,1,0:T(8,128)(2,1)S(1)}, f32[2,72,256]{2,1,0:T(8,128)S(1)}) custom-call(s32[14]{0:T(128)S(1)} %pad_add_fusion.meta, bf16[2,3,192,256]{3,2,1,0:T(8,128)(2,1)S(1)} %bitcast.14, f32[3,18,256]{2,1,0:T(8,128)S(1)} %reshape.16.links_ref, ...), custom_call_target="tpu_custom_call" | custom-call | flops 500000000 | bytes 4000000 | tf_op jit(solution)/shard_map/early/pallas_call | solution.py:292
  10.9 7.0 %collective-permute-done.next_ref = bf16[2,3,192,256]{3,2,1,0:T(8,128)(2,1)S(1)} collective-permute-done((bf16[2,3,192,256]{3,2,1,0:T(8,128)(2,1)}, bf16[2,3,192,256]{3,2,1,0:T(8,128)(2,1)S(1)}, u32[]{:S(2)}, u32[]{:S(2)}) %collective-permute-start) | collective-permute-done | bytes 589856 | tf_op jit(solution)/shard_map/ppermute | solution.py:22
  18.0 2.3 %first.1 = (bf16[2,384,768]{2,1,0:T(8,128)(2,1)S(1)}, f32[2,27,4,256]{3,2,1,0:T(4,128)S(1)}, bf16[2,4,48,384]{3,2,1,0:T(8,128)(2,1)S(1)}) custom-call(s32[14]{0:T(128)S(1)} %pad_add_fusion.meta, bf16[2,3,192,256]{3,2,1,0:T(8,128)(2,1)S(1)} %get-tuple-element.12.here_ref, ...), custom_call_target="tpu_custom_call", output_to_operand_aliasing={{0}: (5, {}), {1}: (6, {})} | custom-call | tf_op jit(solution)/shard_map/first/pallas_call | solution.py:301
  20.3 2.3 %collective-permute-start.3 = (bf16[2,4,48,384]{3,2,1,0:T(8,128)(2,1)S(1)}, bf16[2,4,48,384]{3,2,1,0:T(8,128)(2,1)S(1)}, u32[]{:S(2)}, u32[]{:S(2)}) collective-permute-start(bf16[2,4,48,384]{3,2,1,0:T(8,128)(2,1)S(1)} %get-tuple-element.18), channel_id=1, source_target_pairs={{0,1},{3,2},{4,5},{7,6},{8,9},{11,10},{12,13},{15,14},{16,17},{19,... | collective-permute-start | bytes 884744 | tf_op jit(solution)/shard_map/ppermute | solution.py:333
  22.6 2.3 %shard_map.47 = bf16[2,4,48,384]{3,2,1,0:T(8,128)(2,1)S(1)} custom-call(s32[14]{0:T(128)S(1)} %pad_add_fusion.meta, bf16[2,3,192,256]{3,2,1,0:T(8,128)(2,1)S(1)} %get-tuple-element.12.here_ref, bf16[2,3,192,256]{3,2,1,0:T(8,128)(2,1)S(1)} %collective-permute-done.next_ref, bf16[3,256,256]{2,1,0:T(8,128)(2,1)S(1)} %select_convert_fusion.shifts_ref, ...), custom_call_target="tpu_custom_call" | custom-call | flops 1000000000 | bytes 4000000 | tf_op jit(solution)/shard_map/pallas_call | solution.py:318
  24.8 0.1 collective-permute-start.2
  24.9 0.7 %collective-permute-start.1 = (bf16[2,4,48,384]{3,2,1,0:T(8,128)(2,1)S(1)}, bf16[2,4,48,384]{3,2,1,0:T(8,128)(2,1)S(1)}, u32[]{:S(2)}, u32[]{:S(2)}) collective-permute-start(bf16[2,4,48,384]{3,2,1,0:T(8,128)(2,1)S(1)} %get-tuple-element.18), channel_id=1, source_target_pairs={{1,2},{2,1},{5,6},{6,5},{9,10},{10,9},{13,14},{14,13},{17,18},{18,... | collective-permute-start | bytes 884744 | tf_op jit(solution)/shard_map/ppermute | solution.py:332
  25.6 2.2 %shard_map.48 = bf16[2,4,48,384]{3,2,1,0:T(8,128)(2,1)S(1)} custom-call(s32[14]{0:T(128)S(1)} %pad_add_fusion.meta, bf16[2,3,192,256]{3,2,1,0:T(8,128)(2,1)S(1)} %get-tuple-element.12.here_ref, bf16[2,3,192,256]{3,2,1,0:T(8,128)(2,1)S(1)} %collective-permute-done.next_ref, bf16[3,256,256]{2,1,0:T(8,128)(2,1)S(1)} %select_convert_fusion.shifts_ref, ...), custom_call_target="tpu_custom_call" | custom-call | flops 1000000000 | bytes 4000000 | tf_op jit(solution)/shard_map/pallas_call | solution.py:318
  27.8 2.1 %collective-permute-done.3 = bf16[2,4,48,384]{3,2,1,0:T(8,128)(2,1)S(1)} collective-permute-done((bf16[2,4,48,384]{3,2,1,0:T(8,128)(2,1)S(1)}, bf16[2,4,48,384]{3,2,1,0:T(8,128)(2,1)S(1)}, u32[]{:S(2)}, u32[]{:S(2)}) %collective-permute-start.3) | collective-permute-done | bytes 294944 | tf_op jit(solution)/shard_map/ppermute | solution.py:333
  29.9 0.1 add.60
  30.0 4.3 %collective-permute-start.4 = (bf16[2,4,48,384]{3,2,1,0:T(8,128)(2,1)S(1)}, bf16[2,4,48,384]{3,2,1,0:T(8,128)(2,1)S(1)}, u32[]{:S(2)}, u32[]{:S(2)}) collective-permute-start(bf16[2,4,48,384]{3,2,1,0:T(8,128)(2,1)S(1)} %add.60), channel_id=1, source_target_pairs={{0,2},{1,3},{2,0},{3,1},{4,6},{5,7},{6,4},{7,5},{8,10},{9,11},{10,... | collective-permute-start | bytes 884744 | tf_op jit(solution)/shard_map/ppermute | solution.py:22
  34.3 2.2 %shard_map.46 = f32[2,4,48,384]{3,2,1,0:T(8,128)S(1)} custom-call(s32[14]{0:T(128)S(1)} %pad_add_fusion.meta, bf16[2,3,192,256]{3,2,1,0:T(8,128)(2,1)S(1)} %get-tuple-element.12.here_ref, bf16[2,3,192,256]{3,2,1,0:T(8,128)(2,1)S(1)} %collective-permute-done.next_ref, bf16[3,256,256]{2,1,0:T(8,128)(2,1)S(1)} %select_convert_fusion.shifts_ref, ...), custom_call_target="tpu_custom_call" | custom-call | flops 1000000000 | bytes 4000000 | tf_op jit(solution)/shard_map/pallas_call | solution.py:318
  36.5 0.0 collective-permute-done.2
  36.5 0.0 collective-permute-done.1
  36.6 0.1 convert_add_fusion.1
  36.6 12.4 %collective-permute-done.4 = bf16[2,4,48,384]{3,2,1,0:T(8,128)(2,1)S(1)} collective-permute-done((bf16[2,4,48,384]{3,2,1,0:T(8,128)(2,1)S(1)}, bf16[2,4,48,384]{3,2,1,0:T(8,128)(2,1)S(1)}, u32[]{:S(2)}, u32[]{:S(2)}) %collective-permute-start.4) | collective-permute-done | bytes 294944 | tf_op jit(solution)/shard_map/ppermute | solution.py:22
  49.0 0.9 %convert_add_fusion = f32[2,4,48,384]{3,2,1,0:T(8,128)} fusion(f32[2,4,48,384]{3,2,1,0:T(8,128)S(1)} %convert_add_fusion.1, bf16[2,4,48,384]{3,2,1,0:T(8,128)(2,1)S(1)} %collective-permute-done.4), kind=kLoop, calls=%fused_computation.5 | loop fusion | flops 294912 | bytes 1474560 | tf_op jit(solution)/shard_map/add | solution.py:338
  (5 shorter events, 0.1 us)
Async XLA Ops:
  0.0 18.0 %collective-permute-start = (bf16[2,3,192,256]{3,2,1,0:T(8,128)(2,1)}, bf16[2,3,192,256]{3,2,1,0:T(8,128)(2,1)S(1)}, u32[]{:S(2)}, u32[]{:S(2)}) collective-permute-start(bf16[2,3,192,256]{3,2,1,0:T(8,128)(2,1)} %bitcast.13), channel_id=1, source_target_pairs={{0,3},{1,0},{2,1},{3,2},{4,7},{5,4},{6,5},{7,6},{8,11},{9,8},{10,9... | collective-permute-start | bytes 1769480 | tf_op jit(solution)/shard_map/ppermute | solution.py:22
  7.7 1.1 %copy-start = (bf16[2,192,3,1,256]{4,1,3,2,0:T(8,128)(2,1)S(1)}, bf16[2,192,3,1,256]{4,1,3,2,0:T(8,128)(2,1)}, u32[]{:S(2)}) copy-start(bf16[2,192,3,1,256]{4,1,3,2,0:T(8,128)(2,1)} %param.4) | copy-start | bytes 1769476
  20.3 9.6 %collective-permute-start.3 = (bf16[2,4,48,384]{3,2,1,0:T(8,128)(2,1)S(1)}, bf16[2,4,48,384]{3,2,1,0:T(8,128)(2,1)S(1)}, u32[]{:S(2)}, u32[]{:S(2)}) collective-permute-start(bf16[2,4,48,384]{3,2,1,0:T(8,128)(2,1)S(1)} %get-tuple-element.18), channel_id=1, source_target_pairs={{0,1},{3,2},{4,5},{7,6},{8,9},{11,10},{12,13},{15,14},{16,17},{19,... | collective-permute-start | bytes 884744 | tf_op jit(solution)/shard_map/ppermute | solution.py:333
  24.8 11.7 %collective-permute-start.2 = (bf16[2,4,48,384]{3,2,1,0:T(8,128)(2,1)S(1)}, bf16[2,4,48,384]{3,2,1,0:T(8,128)(2,1)S(1)}, u32[]{:S(2)}, u32[]{:S(2)}) collective-permute-start(bf16[2,4,48,384]{3,2,1,0:T(8,128)(2,1)S(1)} %shard_map.47), channel_id=1, source_target_pairs={{0,1},{1,0},{2,3},{3,2},{4,5},{5,4},{6,7},{7,6},{8,9},{9,8},{10,11... | collective-permute-start | bytes 884744 | tf_op jit(solution)/shard_map/ppermute | solution.py:335
  24.9 11.7 %collective-permute-start.1 = (bf16[2,4,48,384]{3,2,1,0:T(8,128)(2,1)S(1)}, bf16[2,4,48,384]{3,2,1,0:T(8,128)(2,1)S(1)}, u32[]{:S(2)}, u32[]{:S(2)}) collective-permute-start(bf16[2,4,48,384]{3,2,1,0:T(8,128)(2,1)S(1)} %get-tuple-element.18), channel_id=1, source_target_pairs={{1,2},{2,1},{5,6},{6,5},{9,10},{10,9},{13,14},{14,13},{17,18},{18,... | collective-permute-start | bytes 884744 | tf_op jit(solution)/shard_map/ppermute | solution.py:332
  30.0 19.0 %collective-permute-start.4 = (bf16[2,4,48,384]{3,2,1,0:T(8,128)(2,1)S(1)}, bf16[2,4,48,384]{3,2,1,0:T(8,128)(2,1)S(1)}, u32[]{:S(2)}, u32[]{:S(2)}) collective-permute-start(bf16[2,4,48,384]{3,2,1,0:T(8,128)(2,1)S(1)} %add.60), channel_id=1, source_target_pairs={{0,2},{1,3},{2,0},{3,1},{4,6},{5,7},{6,4},{7,5},{8,10},{9,11},{10,... | collective-permute-start | bytes 884744 | tf_op jit(solution)/shard_map/ppermute | solution.py:22

commit v7 on v6

--- a/solution.py
+++ b/solution.py
@@ -35,6 +35,18 @@
 
 def in_plane(shifts_ref, direction):
     return shifts_ref[jnp.where(direction == 3, 0, direction)]
+
+
+def middle_exchange(block):
+    lines, ring = lax.axis_size("ta"), lax.axis_size("site")
+    route = []
+    for line in range(lines):
+        beside = line ^ 1 if lines % 2 == 0 else line
+        for site in range(ring):
+            inner = 0 < site < ring - 1
+            target = line * ring + ring - 1 - site if inner else beside * ring + site
+            route.append((line * ring + site, target))
+    return lax.ppermute(block, ("ta", "site"), route)
 
 
 def mul(left, right):
@@ -128,9 +140,7 @@
     vectors, sites = plane_ref.shape[-2:]
     for color in range(COLORS):
         for part in range(2):
-            field = plane_ref[part, color]
-            if shift is not None:
-                field = jnp.dot(field, shift, preferred_element_type=jnp.float32)
+            field = jnp.dot(plane_ref[part, color], shift, preferred_element_type=jnp.float32)
             right_ref[
                 combo, part * vectors : (part + 1) * vectors, color * sites : (color + 1) * sites
             ] = field.astype(right_ref.dtype)
@@ -213,33 +223,60 @@
     return Moves(), Rows()
 
 
-def prepare(of_next, layout, meta, plane_ref, shifts_ref, joins_ref, right_ref, matrices_ref):
-    moves, rows = moves_of(meta, layout)
-    for combo in range(layout[1]):
-
-        @pl.when((moves[combo, 0] == 3) == of_next)
-        def _(combo=combo):
-            shift = None if of_next else in_plane(shifts_ref, moves[combo, 0])
-            site_matrices(combo, rows, plane_ref, shift, joins_ref, matrices_ref)
-
-        @pl.when((moves[combo, 2] == 3) == of_next)
-        def _(combo=combo):
-            shift = None if of_next else in_plane(shifts_ref, moves[combo, 2])
-            right_operand(combo, plane_ref, shift, right_ref)
-
-
 def early_kernel(layout, scale, meta, here_ref, links_ref, shifts_ref, right_ref, matrices_ref, copy_ref, joins_ref):
     copy_ref[...] = here_ref[...]
-    moves, _ = moves_of(meta, layout)
+    moves, rows = moves_of(meta, layout)
     for combo in range(layout[1]):
         join_links(combo, moves, links_ref, joins_ref, scale)
-    prepare(False, layout, meta, here_ref, shifts_ref, joins_ref, right_ref, matrices_ref)
+    for combo in range(layout[1]):
+
+        @pl.when(moves[combo, 0] != 3)
+        def _(combo=combo):
+            shift = in_plane(shifts_ref, moves[combo, 0])
+            site_matrices(combo, rows, here_ref, shift, joins_ref, matrices_ref)
+
+        @pl.when(moves[combo, 2] != 3)
+        def _(combo=combo):
+            right_operand(combo, here_ref, in_plane(shifts_ref, moves[combo, 2]), right_ref)
+
+
+def keep_right(combo, field, right_ref, turned_ref):
+    vectors, sites = right_ref.shape[1] // 2, right_ref.shape[2] // COLORS
+    for color in range(COLORS):
+        wide = slice(color * sites, (color + 1) * sites)
+        re, im = field(0, color), field(1, color)
+        right_ref[combo, :vectors, wide] = re
+        right_ref[combo, vectors:, wide] = im
+        turned_ref[combo, :vectors, wide] = -im
+        turned_ref[combo, vectors:, wide] = re
 
 
 def first_kernel(layout, meta, here_ref, next_ref, joins_ref, shifts_ref, right_in, matrices_in, right_ref, matrices_ref, out_ref, turned_ref, mid_ref, crossed_ref):
-    prepare(True, layout, meta, next_ref, shifts_ref, joins_ref, right_ref, matrices_ref)
-    turn(right_ref, turned_ref)
-    moves, _ = moves_of(meta, layout)
+    moves, rows = moves_of(meta, layout)
+    vectors, sites = here_ref.shape[-2:]
+    for combo in range(layout[1]):
+
+        @pl.when(moves[combo, 0] == 3)
+        def _(combo=combo):
+            site_matrices(combo, rows, next_ref, None, joins_ref, matrices_ref)
+
+        @pl.when(moves[combo, 0] != 3)
+        def _(combo=combo):
+            matrices_ref[combo] = matrices_in[combo]
+
+        @pl.when(moves[combo, 2] == 3)
+        def _(combo=combo):
+            keep_right(combo, lambda part, color: next_ref[part, color], right_ref, turned_ref)
+
+        @pl.when(moves[combo, 2] != 3)
+        def _(combo=combo):
+            def ready(part, color):
+                return right_in[
+                    combo, part * vectors : (part + 1) * vectors, color * sites : (color + 1) * sites
+                ]
+
+            keep_right(combo, ready, right_ref, turned_ref)
+
     for combo in range(layout[1]):
         row_block(combo, meta[0], moves, here_ref, next_ref, shifts_ref, matrices_ref, right_ref, turned_ref, mid_ref.at[combo], crossed_ref.at[combo], out_ref)
 
@@ -307,7 +344,6 @@
         ),
         in_specs=[smem, vmem, vmem, vmem, vmem, vmem, vmem],
         out_specs=(vmem, vmem, vmem),
-        input_output_aliases={5: 0, 6: 1},
         scratch_shapes=scratch,
         compiler_params=params,
         name="first",
@@ -329,7 +365,8 @@
     if not folded:
         arrived = [shifted(block, "site", offset + 1) for offset, block in enumerate(blocks)]
         return functools.reduce(lambda total, block: total + block.astype(jnp.float32), arrived, own)
-    near = lax.ppermute(blocks[0], "site", [(1, 2), (2, 1)])
+    near = middle_exchange(blocks[0])
+    near = jnp.where((me > 0) & (me < last), near, jnp.zeros_like(near))
     passed = lax.ppermute(blocks[0], "site", [(0, 1), (3, 2)])
     far = shifted(blocks[1] + passed, "site", 2)
     paired = lax.ppermute(blocks[2], "site", [(0, 1), (1, 0), (2, 3), (3, 2)])

time: 50.2 us -> 49.2 us (0.980)
  waiting for transfers between devices: 21.5 us -> 17.2 us
  other arithmetic: 2.83 us -> 4.79 us
  local copies, waits for them, and re-layouts: 1.86 us -> 2.8 us
    ppermute x2, waiting for transfers between devices: 19.4 us -> 16.2 us  [shifted(): lax.ppermute(block, axis, [(i, (i + distance) % count) for i in range(cou...]
    ppermute x1, waiting for transfers between devices: 2.08 us -> 1.03 us  [local_work(): passed = lax.ppermute(blocks[0], 'site', [(0, 1), (3, 2)])]
    add x1, other arithmetic: 0.08 us -> 1.08 us  [local_work(): held = own + near.astype(jnp.float32) + paired.astype(jnp.float32)]
    add x1, other arithmetic: 0.08 us -> 1.04 us  [local_work(): far = shifted(blocks[1] + passed, 'site', 2)]
    unnamed x2 -> x8, local copies, waits for them, and re-layouts: 1.06 us -> 2 us
    ppermute x1, starting transfers between devices: 2.28 us -> 2.97 us  [local_work(): passed = lax.ppermute(blocks[0], 'site', [(0, 1), (3, 2)])]
    ppermute x1, starting transfers between devices: 0.68 us -> 0.07 us  [middle_exchange(): return lax.ppermute(block, ('ta', 'site'), route)]
  transfers between devices with their start and end apart: 5 -> 5, of which waited for: 3 -> 3; matrix products, arithmetic and copies ran while one was open for 6% -> 10% of each run, Pallas kernels for 18% -> 18%
where the time goes in v7:
time: 49.2 us; the launch traced here: 48.9 us
  waiting for transfers between devices  17.2 us (35%)
  starting transfers between devices  12.6 us (26%)
  Pallas kernels  11.3 us (23%)
  other arithmetic  4.79 us (10%)
  local copies, waits for them, and re-layouts  2.8 us (6%)
    ppermute x2, waiting for transfers between devices, shifted(): lax.ppermute(block, axis, [(i, (i + distance) % count) for i in range(cou...  16.2 us
    ppermute x2, starting transfers between devices, shifted(): lax.ppermute(block, axis, [(i, (i + distance) % count) for i in range(cou...  9.47 us
    pallas_call x3, Pallas kernels, local_work(): pl.pallas_call(functools.partial(block_kernel, number, layout), out_shape...  6.77 us
    ppermute x1, starting transfers between devices, local_work(): passed = lax.ppermute(blocks[0], 'site', [(0, 1), (3, 2)])  2.97 us
    pallas_call x1, Pallas kernels, local_work(): pl.pallas_call(functools.partial(first_kernel, layout), out_shape=(jax.Sh...  2.39 us
    pallas_call x1, Pallas kernels, local_work(): pl.pallas_call(functools.partial(early_kernel, layout, scale), out_shape=...  2.17 us
    unnamed x8, local copies, waits for them, and re-layouts  2 us
    add x1, other arithmetic, local_work(): held = own + near.astype(jnp.float32) + paired.astype(jnp.float32)  1.08 us
  transfers between devices with their start and end apart: 5, of which 3 were waited for; matrix products, arithmetic and copies ran while one was open for 10% of the time, Pallas kernels for 18%

profile of v7, /device:TPU:0, one launch (start us, length us, event | category | flops | bytes accessed | tf_op | source)
XLA Modules:
  0.0 48.9 jit_solution(18189618579173946326)
XLA Ops:
  0.0 5.1 %collective-permute-start = (bf16[2,3,192,256]{3,2,1,0:T(8,128)(2,1)}, bf16[2,3,192,256]{3,2,1,0:T(8,128)(2,1)S(1)}, u32[]{:S(2)}, u32[]{:S(2)}) collective-permute-start(bf16[2,3,192,256]{3,2,1,0:T(8,128)(2,1)} %bitcast.13), channel_id=1, source_target_pairs={{0,3},{1,0},{2,1},{3,2},{4,7},{5,4},{6,5},{7,6},{8,11},{9,8},{10,9... | collective-permute-start | bytes 1769480 | tf_op jit(solution)/shard_map/ppermute | solution.py:22
  5.1 0.8 %reshape.11 = s32[6]{0:T(128)S(1)} reshape(s32[2,3]{1,0:T(2,128)} %param.6) | data formatting | bytes 48 | tf_op jit(solution)/shard_map/reshape | solution.py:311
  5.8 0.8 %convert_bitcast_fusion = f32[3,3,3,2,1,256]{5,3,4,2,1,0:T(2,128)S(1)} fusion(bf16[2,3,3,3,1,256]{5,0,4,3,2,1:T(2,128)(2,1)} %param.5), kind=kLoop, calls=%fused_computation.7 | loop fusion | flops 13824 | bytes 82944 | tf_op jit(solution)/shard_map/reshape | solution.py:302
  6.7 0.1 add_multiply_fusion
  6.7 0.7 %pad_add_fusion.meta = s32[14]{0:T(128)S(1)} fusion(s32[4]{0:T(128)} %param.7, s32[6]{0:T(128)S(1)} %reshape.11, s32[4]{0:T(128)S(1)} %add_multiply_fusion), kind=kLoop, calls=%fused_computation.19 | loop fusion | flops 28 | bytes 112 | tf_op jit(solution)/shard_map/concatenate | solution.py:310
  7.5 0.2 select_convert_fusion.shifts_ref
  7.7 0.0 copy-start
  7.7 1.1 %copy-done = bf16[2,192,3,1,256]{4,1,3,2,0:T(8,128)(2,1)S(1)} copy-done((bf16[2,192,3,1,256]{4,1,3,2,0:T(8,128)(2,1)S(1)}, bf16[2,192,3,1,256]{4,1,3,2,0:T(8,128)(2,1)}, u32[]{:S(2)}) %copy-start) | copy-done | bytes 589848
  8.8 2.2 %early.1 = (bf16[2,384,768]{2,1,0:T(8,128)(2,1)S(1)}, f32[2,27,4,256]{3,2,1,0:T(4,128)S(1)}, bf16[2,3,192,256]{3,2,1,0:T(8,128)(2,1)S(1)}, f32[2,72,256]{2,1,0:T(8,128)S(1)}) custom-call(s32[14]{0:T(128)S(1)} %pad_add_fusion.meta, bf16[2,3,192,256]{3,2,1,0:T(8,128)(2,1)S(1)} %bitcast.14, f32[3,18,256]{2,1,0:T(8,128)S(1)} %reshape.16.links_ref, ...), custom_call_target="tpu_custom_call" | custom-call | flops 500000000 | bytes 4000000 | tf_op jit(solution)/shard_map/early/pallas_call | solution.py:329
  10.9 7.0 %collective-permute-done.next_ref = bf16[2,3,192,256]{3,2,1,0:T(8,128)(2,1)S(1)} collective-permute-done((bf16[2,3,192,256]{3,2,1,0:T(8,128)(2,1)}, bf16[2,3,192,256]{3,2,1,0:T(8,128)(2,1)S(1)}, u32[]{:S(2)}, u32[]{:S(2)}) %collective-permute-start) | collective-permute-done | bytes 589856 | tf_op jit(solution)/shard_map/ppermute | solution.py:22
  18.0 2.4 %first.1 = (bf16[2,384,768]{2,1,0:T(8,128)(2,1)S(1)}, f32[2,27,4,256]{3,2,1,0:T(4,128)S(1)}, bf16[2,4,48,384]{3,2,1,0:T(8,128)(2,1)S(1)}) custom-call(s32[14]{0:T(128)S(1)} %pad_add_fusion.meta, bf16[2,3,192,256]{3,2,1,0:T(8,128)(2,1)S(1)} %get-tuple-element.12.here_ref, bf16[2,3,192,256]{3,2,1,0:T(8,128)(2,1)S(1)} %collective-permute-done.next_ref, ...), custom_call_target="tpu_custom_call" | custom-call | tf_op jit(solution)/shard_map/first/pallas_call | solution.py:338
  20.4 0.0 copy-start.1
  20.4 3.0 %collective-permute-start.3 = (bf16[2,4,48,384]{3,2,1,0:T(8,128)(2,1)S(1)}, bf16[2,4,48,384]{3,2,1,0:T(8,128)(2,1)}, u32[]{:S(2)}, u32[]{:S(2)}) collective-permute-start(bf16[2,4,48,384]{3,2,1,0:T(8,128)(2,1)S(1)} %get-tuple-element.18), channel_id=1, source_target_pairs={{0,1},{3,2},{4,5},{7,6},{8,9},{11,10},{12,13},{15,14},{16,17},{19,... | collective-permute-start | bytes 884744 | tf_op jit(solution)/shard_map/ppermute | solution.py:370
  23.4 2.3 %shard_map.47 = bf16[2,4,48,384]{3,2,1,0:T(8,128)(2,1)S(1)} custom-call(s32[14]{0:T(128)S(1)} %pad_add_fusion.meta, bf16[2,3,192,256]{3,2,1,0:T(8,128)(2,1)S(1)} %get-tuple-element.12.here_ref, bf16[2,3,192,256]{3,2,1,0:T(8,128)(2,1)S(1)} %collective-permute-done.next_ref, bf16[3,256,256]{2,1,0:T(8,128)(2,1)S(1)} %select_convert_fusion.shifts_ref, ...), custom_call_target="tpu_custom_call" | custom-call | flops 1000000000 | bytes 4000000 | tf_op jit(solution)/shard_map/pallas_call | solution.py:354
  25.6 0.0 copy-done.1
  25.6 0.1 collective-permute-start.2
  25.7 0.1 collective-permute-start.1
  25.8 0.0 copy-start.2
  25.8 0.9 %copy-done.2 = f32[2,27,4,256]{3,2,1,0:T(4,128)S(1)} copy-done((f32[2,27,4,256]{3,2,1,0:T(4,128)S(1)}, f32[2,27,4,256]{3,2,1,0:T(4,128)}, u32[]{:S(2)}) %copy-start.2) | copy-done | bytes 221208
  26.7 0.0 copy-start.3
  26.7 2.3 %shard_map.48 = bf16[2,4,48,384]{3,2,1,0:T(8,128)(2,1)S(1)} custom-call(s32[14]{0:T(128)S(1)} %pad_add_fusion.meta, bf16[2,3,192,256]{3,2,1,0:T(8,128)(2,1)S(1)} %get-tuple-element.12.here_ref, bf16[2,3,192,256]{3,2,1,0:T(8,128)(2,1)S(1)} %collective-permute-done.next_ref, bf16[3,256,256]{2,1,0:T(8,128)(2,1)S(1)} %select_convert_fusion.shifts_ref, ...), custom_call_target="tpu_custom_call" | custom-call | flops 1000000000 | bytes 4000000 | tf_op jit(solution)/shard_map/pallas_call | solution.py:354
  29.0 1.0 %collective-permute-done.3 = bf16[2,4,48,384]{3,2,1,0:T(8,128)(2,1)} collective-permute-done((bf16[2,4,48,384]{3,2,1,0:T(8,128)(2,1)S(1)}, bf16[2,4,48,384]{3,2,1,0:T(8,128)(2,1)}, u32[]{:S(2)}, u32[]{:S(2)}) %collective-permute-start.3) | collective-permute-done | bytes 294944 | tf_op jit(solution)/shard_map/ppermute | solution.py:370
  30.0 1.0 %add.60 = bf16[2,4,48,384]{3,2,1,0:T(8,128)(2,1)S(1)} add(bf16[2,4,48,384]{3,2,1,0:T(8,128)(2,1)S(1)} %shard_map.48, bf16[2,4,48,384]{3,2,1,0:T(8,128)(2,1)} %collective-permute-done.3) | non-fusion elementwise | flops 147456 | bytes 884736 | tf_op jit(solution)/shard_map/add | solution.py:371
  31.1 4.4 %collective-permute-start.4 = (bf16[2,4,48,384]{3,2,1,0:T(8,128)(2,1)S(1)}, bf16[2,4,48,384]{3,2,1,0:T(8,128)(2,1)S(1)}, u32[]{:S(2)}, u32[]{:S(2)}) collective-permute-start(bf16[2,4,48,384]{3,2,1,0:T(8,128)(2,1)S(1)} %add.60), channel_id=1, source_target_pairs={{0,2},{1,3},{2,0},{3,1},{4,6},{5,7},{6,4},{7,5},{8,10},{9,11},{10,... | collective-permute-start | bytes 884744 | tf_op jit(solution)/shard_map/ppermute | solution.py:22
  35.5 0.0 copy-done.3
  35.5 2.3 %shard_map.46 = f32[2,4,48,384]{3,2,1,0:T(8,128)S(1)} custom-call(s32[14]{0:T(128)S(1)} %pad_add_fusion.meta, bf16[2,3,192,256]{3,2,1,0:T(8,128)(2,1)S(1)} %get-tuple-element.12.here_ref, bf16[2,3,192,256]{3,2,1,0:T(8,128)(2,1)S(1)} %collective-permute-done.next_ref, bf16[3,256,256]{2,1,0:T(8,128)(2,1)S(1)} %select_convert_fusion.shifts_ref, ...), custom_call_target="tpu_custom_call" | custom-call | flops 1000000000 | bytes 4000000 | tf_op jit(solution)/shard_map/pallas_call | solution.py:354
  37.7 0.0 collective-permute-done.2
  37.8 0.0 collective-permute-done.1
  37.8 1.1 %convert_add_fusion.1 = f32[2,4,48,384]{3,2,1,0:T(8,128)S(1)} fusion(bf16[2,4,48,384]{3,2,1,0:T(8,128)(2,1)} %collective-permute-done.2, f32[2,4,48,384]{3,2,1,0:T(8,128)S(1)} %shard_map.46, bf16[2,4,48,384]{3,2,1,0:T(8,128)(2,1)} %collective-permute-done.1, pred[]{:T(512)S(6)} %and.11), kind=kLoop, calls=%fused_computation.6 | loop fusion | flops 737280 | bytes 1769473 | tf_op jit(solution)/shard_map/add | solution.py:373
  38.9 9.1 %collective-permute-done.4 = bf16[2,4,48,384]{3,2,1,0:T(8,128)(2,1)S(1)} collective-permute-done((bf16[2,4,48,384]{3,2,1,0:T(8,128)(2,1)S(1)}, bf16[2,4,48,384]{3,2,1,0:T(8,128)(2,1)S(1)}, u32[]{:S(2)}, u32[]{:S(2)}) %collective-permute-start.4) | collective-permute-done | bytes 294944 | tf_op jit(solution)/shard_map/ppermute | solution.py:22
  48.0 0.9 %convert_add_fusion = f32[2,4,48,384]{3,2,1,0:T(8,128)} fusion(f32[2,4,48,384]{3,2,1,0:T(8,128)S(1)} %convert_add_fusion.1, bf16[2,4,48,384]{3,2,1,0:T(8,128)(2,1)S(1)} %collective-permute-done.4), kind=kLoop, calls=%fused_computation.5 | loop fusion | flops 294912 | bytes 1474560 | tf_op jit(solution)/shard_map/add | solution.py:375
  (5 shorter events, 0.1 us)
Async XLA Ops:
  0.0 18.0 %collective-permute-start = (bf16[2,3,192,256]{3,2,1,0:T(8,128)(2,1)}, bf16[2,3,192,256]{3,2,1,0:T(8,128)(2,1)S(1)}, u32[]{:S(2)}, u32[]{:S(2)}) collective-permute-start(bf16[2,3,192,256]{3,2,1,0:T(8,128)(2,1)} %bitcast.13), channel_id=1, source_target_pairs={{0,3},{1,0},{2,1},{3,2},{4,7},{5,4},{6,5},{7,6},{8,11},{9,8},{10,9... | collective-permute-start | bytes 1769480 | tf_op jit(solution)/shard_map/ppermute | solution.py:22
  7.7 1.1 %copy-start = (bf16[2,192,3,1,256]{4,1,3,2,0:T(8,128)(2,1)S(1)}, bf16[2,192,3,1,256]{4,1,3,2,0:T(8,128)(2,1)}, u32[]{:S(2)}) copy-start(bf16[2,192,3,1,256]{4,1,3,2,0:T(8,128)(2,1)} %param.4) | copy-start | bytes 1769476
  20.4 5.2 %copy-start.1 = (f32[2,27,4,256]{3,2,1,0:T(4,128)}, f32[2,27,4,256]{3,2,1,0:T(4,128)S(1)}, u32[]{:S(2)}) copy-start(f32[2,27,4,256]{3,2,1,0:T(4,128)S(1)} %get-tuple-element.17.matrices_ref) | copy-start | bytes 663556
  20.4 9.7 %collective-permute-start.3 = (bf16[2,4,48,384]{3,2,1,0:T(8,128)(2,1)S(1)}, bf16[2,4,48,384]{3,2,1,0:T(8,128)(2,1)}, u32[]{:S(2)}, u32[]{:S(2)}) collective-permute-start(bf16[2,4,48,384]{3,2,1,0:T(8,128)(2,1)S(1)} %get-tuple-element.18), channel_id=1, source_target_pairs={{0,1},{3,2},{4,5},{7,6},{8,9},{11,10},{12,13},{15,14},{16,17},{19,... | collective-permute-start | bytes 884744 | tf_op jit(solution)/shard_map/ppermute | solution.py:370
  25.6 12.1 %collective-permute-start.2 = (bf16[2,4,48,384]{3,2,1,0:T(8,128)(2,1)S(1)}, bf16[2,4,48,384]{3,2,1,0:T(8,128)(2,1)}, u32[]{:S(2)}, u32[]{:S(2)}) collective-permute-start(bf16[2,4,48,384]{3,2,1,0:T(8,128)(2,1)S(1)} %shard_map.47), channel_id=1, source_target_pairs={{0,1},{1,0},{2,3},{3,2},{4,5},{5,4},{6,7},{7,6},{8,9},{9,8},{10,11... | collective-permute-start | bytes 884744 | tf_op jit(solution)/shard_map/ppermute | solution.py:372
  25.7 12.0 %collective-permute-start.1 = (bf16[2,4,48,384]{3,2,1,0:T(8,128)(2,1)S(1)}, bf16[2,4,48,384]{3,2,1,0:T(8,128)(2,1)}, u32[]{:S(2)}, u32[]{:S(2)}) collective-permute-start(bf16[2,4,48,384]{3,2,1,0:T(8,128)(2,1)S(1)} %get-tuple-element.18), channel_id=1, source_target_pairs={{0,4},{1,2},{2,1},{3,7},{4,0},{5,6},{6,5},{7,3},{8,12},{9,10},{10,... | collective-permute-start | bytes 884744 | tf_op jit(solution)/shard_map/ppermute | solution.py:49
  25.8 0.9 %copy-start.2 = (f32[2,27,4,256]{3,2,1,0:T(4,128)S(1)}, f32[2,27,4,256]{3,2,1,0:T(4,128)}, u32[]{:S(2)}) copy-start(f32[2,27,4,256]{3,2,1,0:T(4,128)} %copy-done.1) | copy-start | bytes 663556
  26.7 8.7 %copy-start.3 = (f32[2,27,4,256]{3,2,1,0:T(4,128)S(1)}, f32[2,27,4,256]{3,2,1,0:T(4,128)}, u32[]{:S(2)}) copy-start(f32[2,27,4,256]{3,2,1,0:T(4,128)} %copy-done.1) | copy-start | bytes 663556
  31.1 16.9 %collective-permute-start.4 = (bf16[2,4,48,384]{3,2,1,0:T(8,128)(2,1)S(1)}, bf16[2,4,48,384]{3,2,1,0:T(8,128)(2,1)S(1)}, u32[]{:S(2)}, u32[]{:S(2)}) collective-permute-start(bf16[2,4,48,384]{3,2,1,0:T(8,128)(2,1)S(1)} %add.60), channel_id=1, source_target_pairs={{0,2},{1,3},{2,0},{3,1},{4,6},{5,7},{6,4},{7,5},{8,10},{9,11},{10,... | collective-permute-start | bytes 884744 | tf_op jit(solution)/shard_map/ppermute | solution.py:22

commit v8 on v7

--- a/solution.py
+++ b/solution.py
@@ -55,10 +55,6 @@
 
 def add(left, right):
     return left[0] + right[0], left[1] + right[1]
-
-
-def plane_of(here_ref, next_ref, direction, index):
-    return jnp.where(direction == 3, next_ref[index], here_ref[index])
 
 
 def chosen_link(links_ref, direction):
@@ -153,16 +149,12 @@
         turned_ref[combo, vectors:] = right_ref[combo, :vectors]
 
 
-def row_block(combo, start, moves, here_ref, next_ref, shifts_ref, matrices_ref, right_ref, turned_ref, mid_ref, crossed_ref, out_ref):
-    sites = here_ref.shape[-1]
+def row_block(combo, start, mids_ref, matrices_ref, right_ref, turned_ref, mid_ref, crossed_ref, out_ref):
+    sites = mids_ref.shape[-1]
     picks, count = out_ref.shape[1:3]
-    direction = moves[combo, 1]
+    half = COLORS * count
     rows = pl.ds(pl.multiple_of(start, TILE), count)
-    block = plane_of(here_ref, next_ref, direction, (slice(None), slice(None), rows))
-    half = COLORS * count
-    both = jnp.dot(
-        block.reshape(2 * half, sites), in_plane(shifts_ref, direction), preferred_element_type=jnp.float32
-    )
+    both = mids_ref[combo, :, :, rows].reshape(2 * half, sites).astype(jnp.float32)
     re, im = both[:half], both[half:]
     mid_ref[:half] = re
     mid_ref[half : 2 * half] = im - re
@@ -223,8 +215,7 @@
     return Moves(), Rows()
 
 
-def early_kernel(layout, scale, meta, here_ref, links_ref, shifts_ref, right_ref, matrices_ref, copy_ref, joins_ref):
-    copy_ref[...] = here_ref[...]
+def early_kernel(layout, scale, meta, here_ref, links_ref, shifts_ref, right_ref, matrices_ref, mids_ref, joins_ref):
     moves, rows = moves_of(meta, layout)
     for combo in range(layout[1]):
         join_links(combo, moves, links_ref, joins_ref, scale)
@@ -238,6 +229,14 @@
         @pl.when(moves[combo, 2] != 3)
         def _(combo=combo):
             right_operand(combo, here_ref, in_plane(shifts_ref, moves[combo, 2]), right_ref)
+
+        @pl.when(moves[combo, 1] != 3)
+        def _(combo=combo):
+            shift = in_plane(shifts_ref, moves[combo, 1])
+            for part in range(2):
+                for color in range(COLORS):
+                    field = jnp.dot(here_ref[part, color], shift, preferred_element_type=jnp.float32)
+                    mids_ref[combo, part, color] = field.astype(mids_ref.dtype)
 
 
 def keep_right(combo, field, right_ref, turned_ref):
@@ -251,10 +250,18 @@
         turned_ref[combo, vectors:, wide] = re
 
 
-def first_kernel(layout, meta, here_ref, next_ref, joins_ref, shifts_ref, right_in, matrices_in, right_ref, matrices_ref, out_ref, turned_ref, mid_ref, crossed_ref):
+def first_kernel(layout, meta, next_ref, joins_ref, right_in, matrices_in, mids_in, right_ref, matrices_ref, mids_ref, out_ref, turned_ref, mid_ref, crossed_ref):
     moves, rows = moves_of(meta, layout)
-    vectors, sites = here_ref.shape[-2:]
+    vectors, sites = next_ref.shape[-2:]
     for combo in range(layout[1]):
+
+        @pl.when(moves[combo, 1] == 3)
+        def _(combo=combo):
+            mids_ref[combo] = next_ref[...]
+
+        @pl.when(moves[combo, 1] != 3)
+        def _(combo=combo):
+            mids_ref[combo] = mids_in[combo]
 
         @pl.when(moves[combo, 0] == 3)
         def _(combo=combo):
@@ -278,14 +285,13 @@
             keep_right(combo, ready, right_ref, turned_ref)
 
     for combo in range(layout[1]):
-        row_block(combo, meta[0], moves, here_ref, next_ref, shifts_ref, matrices_ref, right_ref, turned_ref, mid_ref.at[combo], crossed_ref.at[combo], out_ref)
-
-
-def block_kernel(number, layout, meta, here_ref, next_ref, shifts_ref, right_ref, matrices_ref, out_ref, turned_ref, mid_ref, crossed_ref):
+        row_block(combo, meta[0], mids_ref, matrices_ref, right_ref, turned_ref, mid_ref.at[combo], crossed_ref.at[combo], out_ref)
+
+
+def block_kernel(number, layout, meta, mids_ref, right_ref, matrices_ref, out_ref, turned_ref, mid_ref, crossed_ref):
     turn(right_ref, turned_ref)
-    moves, _ = moves_of(meta, layout)
     for combo in range(layout[1]):
-        row_block(combo, meta[number], moves, here_ref, next_ref, shifts_ref, matrices_ref, right_ref, turned_ref, mid_ref.at[combo], crossed_ref.at[combo], out_ref)
+        row_block(combo, meta[number], mids_ref, matrices_ref, right_ref, turned_ref, mid_ref.at[combo], crossed_ref.at[combo], out_ref)
 
 
 def local_work(eigenvectors, gauge_links, displacements, block_rows):
@@ -326,40 +332,42 @@
     def chunk(kind):
         return jax.ShapeDtypeStruct((combos, picks, count, 2 * vectors), kind)
 
-    right, matrices, here, joins = pl.pallas_call(
+    right, matrices, mids, joins = pl.pallas_call(
         functools.partial(early_kernel, layout, scale),
-        out_shape=(right, matrices, jax.ShapeDtypeStruct(here.shape, here.dtype), joins),
+        out_shape=(right, matrices, jax.ShapeDtypeStruct((combos, *here.shape), here.dtype), joins),
         in_specs=[smem, vmem, vmem, vmem],
         out_specs=(vmem, vmem, vmem, vmem),
         compiler_params=params,
         cost_estimate=pl.CostEstimate(flops=500_000_000, bytes_accessed=4_000_000, transcendentals=0),
         name="early",
     )(meta, here, links, shifts)
-    right, matrices, sent = pl.pallas_call(
+    right, matrices, mids, sent = pl.pallas_call(
         functools.partial(first_kernel, layout),
         out_shape=(
             jax.ShapeDtypeStruct(right.shape, right.dtype),
             jax.ShapeDtypeStruct(matrices.shape, matrices.dtype),
+            jax.ShapeDtypeStruct(mids.shape, mids.dtype),
             chunk(jnp.bfloat16),
         ),
-        in_specs=[smem, vmem, vmem, vmem, vmem, vmem, vmem],
-        out_specs=(vmem, vmem, vmem),
+        in_specs=[smem, vmem, vmem, vmem, vmem, vmem],
+        out_specs=(vmem, vmem, vmem, vmem),
+        input_output_aliases={3: 0, 4: 1, 5: 2},
         scratch_shapes=scratch,
         compiler_params=params,
         name="first",
-    )(meta, here, after, joins, shifts, right, matrices)
+    )(meta, after, joins, right, matrices, mids)
     blocks = [sent]
     for number in range(1, ring):
         blocks.append(
             pl.pallas_call(
                 functools.partial(block_kernel, number, layout),
                 out_shape=chunk(jnp.float32 if number == last else jnp.bfloat16),
-                in_specs=[smem, vmem, vmem, vmem, vmem, vmem],
+                in_specs=[smem, vmem, vmem, vmem],
                 out_specs=vmem,
                 scratch_shapes=scratch,
                 compiler_params=params,
                 cost_estimate=pl.CostEstimate(flops=1_000_000_000, bytes_accessed=4_000_000, transcendentals=0),
-            )(meta, here, after, shifts, right, matrices)
+            )(meta, mids, right, matrices)
         )
     own = blocks.pop()
     if not folded:

time: 49.2 us -> 48.5 us (0.986)
  waiting for transfers between devices: 17.2 us -> 19.1 us
  Pallas kernels: 11.3 us -> 9.77 us
  local copies, waits for them, and re-layouts: 2.8 us -> 1.86 us
    ppermute x1, waiting for transfers between devices: 1.03 us -> 2.84 us  [local_work(): passed = lax.ppermute(blocks[0], 'site', [(0, 1), (3, 2)])]
    pallas_call x3, Pallas kernels: 6.77 us -> 5.46 us  [local_work(): pl.pallas_call(functools.partial(block_kernel, number, layout), out_shape...]
    unnamed x8 -> x2, local copies, waits for them, and re-layouts: 2 us -> 1.06 us
  transfers between devices with their start and end apart: 5 -> 5, of which waited for: 3 -> 3; matrix products, arithmetic and copies ran while one was open for 10% -> 10% of each run, Pallas kernels for 18% -> 16%
where the time goes in v8:
time: 48.5 us; the launch traced here: 48.2 us
  waiting for transfers between devices  19.1 us (39%)
  starting transfers between devices  12.6 us (26%)
  Pallas kernels  9.77 us (20%)
  other arithmetic  4.79 us (10%)
  local copies, waits for them, and re-layouts  1.86 us (4%)
    ppermute x2, waiting for transfers between devices, shifted(): lax.ppermute(block, axis, [(i, (i + distance) % count) for i in range(cou...  16.2 us
    ppermute x2, starting transfers between devices, shifted(): lax.ppermute(block, axis, [(i, (i + distance) % count) for i in range(cou...  9.48 us
    pallas_call x3, Pallas kernels, local_work(): pl.pallas_call(functools.partial(block_kernel, number, layout), out_shape...  5.46 us
    ppermute x1, starting transfers between devices, local_work(): passed = lax.ppermute(blocks[0], 'site', [(0, 1), (3, 2)])  2.98 us
    ppermute x1, waiting for transfers between devices, local_work(): passed = lax.ppermute(blocks[0], 'site', [(0, 1), (3, 2)])  2.84 us
    pallas_call x1, Pallas kernels, local_work(): pl.pallas_call(functools.partial(first_kernel, layout), out_shape=(jax.Sh...  2.17 us
    pallas_call x1, Pallas kernels, local_work(): pl.pallas_call(functools.partial(early_kernel, layout, scale), out_shape=...  2.14 us
    add x1, other arithmetic, local_work(): held = own + near.astype(jnp.float32) + paired.astype(jnp.float32)  1.08 us
  transfers between devices with their start and end apart: 5, of which 3 were waited for; matrix products, arithmetic and copies ran while one was open for 10% of the time, Pallas kernels for 16%

profile of v8, /device:TPU:0, one launch (start us, length us, event | category | flops | bytes accessed | tf_op | source)
XLA Modules:
  0.0 48.2 jit_solution(17460535788508584019)
XLA Ops:
  0.0 5.1 %collective-permute-start = (bf16[2,3,192,256]{3,2,1,0:T(8,128)(2,1)}, bf16[2,3,192,256]{3,2,1,0:T(8,128)(2,1)S(1)}, u32[]{:S(2)}, u32[]{:S(2)}) collective-permute-start(bf16[2,3,192,256]{3,2,1,0:T(8,128)(2,1)} %bitcast.13), channel_id=1, source_target_pairs={{0,3},{1,0},{2,1},{3,2},{4,7},{5,4},{6,5},{7,6},{8,11},{9,8},{10,9... | collective-permute-start | bytes 1769480 | tf_op jit(solution)/shard_map/ppermute | solution.py:22
  5.1 0.8 %reshape.11 = s32[6]{0:T(128)S(1)} reshape(s32[2,3]{1,0:T(2,128)} %param.6) | data formatting | bytes 48 | tf_op jit(solution)/shard_map/reshape | solution.py:317
  5.8 0.8 %convert_bitcast_fusion = f32[3,3,3,2,1,256]{5,3,4,2,1,0:T(2,128)S(1)} fusion(bf16[2,3,3,3,1,256]{5,0,4,3,2,1:T(2,128)(2,1)} %param.5), kind=kLoop, calls=%fused_computation.7 | loop fusion | flops 13824 | bytes 82944 | tf_op jit(solution)/shard_map/reshape | solution.py:308
  6.7 0.1 add_multiply_fusion
  6.7 0.7 %pad_add_fusion.meta = s32[14]{0:T(128)S(1)} fusion(s32[4]{0:T(128)} %param.7, s32[6]{0:T(128)S(1)} %reshape.11, s32[4]{0:T(128)S(1)} %add_multiply_fusion), kind=kLoop, calls=%fused_computation.19 | loop fusion | flops 28 | bytes 112 | tf_op jit(solution)/shard_map/concatenate | solution.py:316
  7.5 0.2 select_convert_fusion.shifts_ref
  7.7 0.0 copy-start
  7.7 1.1 %copy-done = bf16[2,192,3,1,256]{4,1,3,2,0:T(8,128)(2,1)S(1)} copy-done((bf16[2,192,3,1,256]{4,1,3,2,0:T(8,128)(2,1)S(1)}, bf16[2,192,3,1,256]{4,1,3,2,0:T(8,128)(2,1)}, u32[]{:S(2)}) %copy-start) | copy-done | bytes 589848
  8.8 2.1 %early.1 = (bf16[2,384,768]{2,1,0:T(8,128)(2,1)S(1)}, f32[2,27,4,256]{3,2,1,0:T(4,128)S(1)}, bf16[2,2,3,192,256]{4,3,2,1,0:T(8,128)(2,1)S(1)}, f32[2,72,256]{2,1,0:T(8,128)S(1)}) custom-call(s32[14]{0:T(128)S(1)} %pad_add_fusion.meta, bf16[2,3,192,256]{3,2,1,0:T(8,128)(2,1)S(1)} %bitcast.14, f32[3,18,256]{2,1,0:T(8,128)S(1)} %reshape.16.links_ref, ...), custom_call_target="tpu_custom_call" | custom-call | flops 500000000 | bytes 4000000 | tf_op jit(solution)/shard_map/early/pallas_call | solution.py:335
  10.9 7.1 %collective-permute-done.next_ref = bf16[2,3,192,256]{3,2,1,0:T(8,128)(2,1)S(1)} collective-permute-done((bf16[2,3,192,256]{3,2,1,0:T(8,128)(2,1)}, bf16[2,3,192,256]{3,2,1,0:T(8,128)(2,1)S(1)}, u32[]{:S(2)}, u32[]{:S(2)}) %collective-permute-start) | collective-permute-done | bytes 589856 | tf_op jit(solution)/shard_map/ppermute | solution.py:22
  18.0 2.2 %first.1 = (bf16[2,384,768]{2,1,0:T(8,128)(2,1)S(1)}, f32[2,27,4,256]{3,2,1,0:T(4,128)S(1)}, bf16[2,2,3,192,256]{4,3,2,1,0:T(8,128)(2,1)S(1)}, bf16[2,4,48,384]{3,2,1,0:T(8,128)(2,1)S(1)}) custom-call(s32[14]{0:T(128)S(1)} %pad_add_fusion.meta, ...), custom_call_target="tpu_custom_call", output_to_operand_aliasing={{0}: (3, {}), {1}: (4, {}), {2}: (5, {})} | custom-call | tf_op jit(solution)/shard_map/first/pallas_call | solution.py:344
  20.2 3.0 %collective-permute-start.3 = (bf16[2,4,48,384]{3,2,1,0:T(8,128)(2,1)S(1)}, bf16[2,4,48,384]{3,2,1,0:T(8,128)(2,1)}, u32[]{:S(2)}, u32[]{:S(2)}) collective-permute-start(bf16[2,4,48,384]{3,2,1,0:T(8,128)(2,1)S(1)} %get-tuple-element.20), channel_id=1, source_target_pairs={{0,1},{3,2},{4,5},{7,6},{8,9},{11,10},{12,13},{15,14},{16,17},{19,... | collective-permute-start | bytes 884744 | tf_op jit(solution)/shard_map/ppermute | solution.py:378
  23.1 1.8 %shard_map.47 = bf16[2,4,48,384]{3,2,1,0:T(8,128)(2,1)S(1)} custom-call(s32[14]{0:T(128)S(1)} %pad_add_fusion.meta, bf16[2,2,3,192,256]{4,3,2,1,0:T(8,128)(2,1)S(1)} %get-tuple-element.17.mids_ref, bf16[2,384,768]{2,1,0:T(8,128)(2,1)S(1)} %get-tuple-element.18.right_ref, f32[2,27,4,256]{3,2,1,0:T(4,128)S(1)} %get-tuple-element.19.matrices_ref), custom_call_target="tpu_custom_call" | custom-call | flops 1000000000 | bytes 4000000 | tf_op jit(solution)/shard_map/pallas_call | solution.py:362
  25.0 0.1 collective-permute-start.2
  25.0 0.1 collective-permute-start.1
  25.1 1.8 %shard_map.48 = bf16[2,4,48,384]{3,2,1,0:T(8,128)(2,1)S(1)} custom-call(s32[14]{0:T(128)S(1)} %pad_add_fusion.meta, bf16[2,2,3,192,256]{4,3,2,1,0:T(8,128)(2,1)S(1)} %get-tuple-element.17.mids_ref, bf16[2,384,768]{2,1,0:T(8,128)(2,1)S(1)} %get-tuple-element.18.right_ref, f32[2,27,4,256]{3,2,1,0:T(4,128)S(1)} %get-tuple-element.19.matrices_ref), custom_call_target="tpu_custom_call" | custom-call | flops 1000000000 | bytes 4000000 | tf_op jit(solution)/shard_map/pallas_call | solution.py:362
  27.0 2.8 %collective-permute-done.3 = bf16[2,4,48,384]{3,2,1,0:T(8,128)(2,1)} collective-permute-done((bf16[2,4,48,384]{3,2,1,0:T(8,128)(2,1)S(1)}, bf16[2,4,48,384]{3,2,1,0:T(8,128)(2,1)}, u32[]{:S(2)}, u32[]{:S(2)}) %collective-permute-start.3) | collective-permute-done | bytes 294944 | tf_op jit(solution)/shard_map/ppermute | solution.py:378
  29.8 1.0 %add.36 = bf16[2,4,48,384]{3,2,1,0:T(8,128)(2,1)S(1)} add(bf16[2,4,48,384]{3,2,1,0:T(8,128)(2,1)S(1)} %shard_map.48, bf16[2,4,48,384]{3,2,1,0:T(8,128)(2,1)} %collective-permute-done.3) | non-fusion elementwise | flops 147456 | bytes 884736 | tf_op jit(solution)/shard_map/add | solution.py:379
  30.8 4.4 %collective-permute-start.4 = (bf16[2,4,48,384]{3,2,1,0:T(8,128)(2,1)S(1)}, bf16[2,4,48,384]{3,2,1,0:T(8,128)(2,1)S(1)}, u32[]{:S(2)}, u32[]{:S(2)}) collective-permute-start(bf16[2,4,48,384]{3,2,1,0:T(8,128)(2,1)S(1)} %add.36), channel_id=1, source_target_pairs={{0,2},{1,3},{2,0},{3,1},{4,6},{5,7},{6,4},{7,5},{8,10},{9,11},{10,... | collective-permute-start | bytes 884744 | tf_op jit(solution)/shard_map/ppermute | solution.py:22
  35.2 1.8 %shard_map.46 = f32[2,4,48,384]{3,2,1,0:T(8,128)S(1)} custom-call(s32[14]{0:T(128)S(1)} %pad_add_fusion.meta, bf16[2,2,3,192,256]{4,3,2,1,0:T(8,128)(2,1)S(1)} %get-tuple-element.17.mids_ref, bf16[2,384,768]{2,1,0:T(8,128)(2,1)S(1)} %get-tuple-element.18.right_ref, f32[2,27,4,256]{3,2,1,0:T(4,128)S(1)} %get-tuple-element.19.matrices_ref), custom_call_target="tpu_custom_call" | custom-call | flops 1000000000 | bytes 4000000 | tf_op jit(solution)/shard_map/pallas_call | solution.py:362
  37.1 0.0 collective-permute-done.2
  37.1 0.0 collective-permute-done.1
  37.1 1.1 %convert_add_fusion.1 = f32[2,4,48,384]{3,2,1,0:T(8,128)S(1)} fusion(bf16[2,4,48,384]{3,2,1,0:T(8,128)(2,1)} %collective-permute-done.2, f32[2,4,48,384]{3,2,1,0:T(8,128)S(1)} %shard_map.46, bf16[2,4,48,384]{3,2,1,0:T(8,128)(2,1)} %collective-permute-done.1, pred[]{:T(512)S(6)} %and.11), kind=kLoop, calls=%fused_computation.6 | loop fusion | flops 737280 | bytes 1769473 | tf_op jit(solution)/shard_map/add | solution.py:381
  38.2 9.1 %collective-permute-done.4 = bf16[2,4,48,384]{3,2,1,0:T(8,128)(2,1)S(1)} collective-permute-done((bf16[2,4,48,384]{3,2,1,0:T(8,128)(2,1)S(1)}, bf16[2,4,48,384]{3,2,1,0:T(8,128)(2,1)S(1)}, u32[]{:S(2)}, u32[]{:S(2)}) %collective-permute-start.4) | collective-permute-done | bytes 294944 | tf_op jit(solution)/shard_map/ppermute | solution.py:22
  47.3 0.9 %convert_add_fusion = f32[2,4,48,384]{3,2,1,0:T(8,128)} fusion(f32[2,4,48,384]{3,2,1,0:T(8,128)S(1)} %convert_add_fusion.1, bf16[2,4,48,384]{3,2,1,0:T(8,128)(2,1)S(1)} %collective-permute-done.4), kind=kLoop, calls=%fused_computation.5 | loop fusion | flops 294912 | bytes 1474560 | tf_op jit(solution)/shard_map/add | solution.py:383
  (5 shorter events, 0.1 us)
Async XLA Ops:
  0.0 18.0 %collective-permute-start = (bf16[2,3,192,256]{3,2,1,0:T(8,128)(2,1)}, bf16[2,3,192,256]{3,2,1,0:T(8,128)(2,1)S(1)}, u32[]{:S(2)}, u32[]{:S(2)}) collective-permute-start(bf16[2,3,192,256]{3,2,1,0:T(8,128)(2,1)} %bitcast.13), channel_id=1, source_target_pairs={{0,3},{1,0},{2,1},{3,2},{4,7},{5,4},{6,5},{7,6},{8,11},{9,8},{10,9... | collective-permute-start | bytes 1769480 | tf_op jit(solution)/shard_map/ppermute | solution.py:22
  7.7 1.1 %copy-start = (bf16[2,192,3,1,256]{4,1,3,2,0:T(8,128)(2,1)S(1)}, bf16[2,192,3,1,256]{4,1,3,2,0:T(8,128)(2,1)}, u32[]{:S(2)}) copy-start(bf16[2,192,3,1,256]{4,1,3,2,0:T(8,128)(2,1)} %param.4) | copy-start | bytes 1769476
  20.2 9.6 %collective-permute-start.3 = (bf16[2,4,48,384]{3,2,1,0:T(8,128)(2,1)S(1)}, bf16[2,4,48,384]{3,2,1,0:T(8,128)(2,1)}, u32[]{:S(2)}, u32[]{:S(2)}) collective-permute-start(bf16[2,4,48,384]{3,2,1,0:T(8,128)(2,1)S(1)} %get-tuple-element.20), channel_id=1, source_target_pairs={{0,1},{3,2},{4,5},{7,6},{8,9},{11,10},{12,13},{15,14},{16,17},{19,... | collective-permute-start | bytes 884744 | tf_op jit(solution)/shard_map/ppermute | solution.py:378
  25.0 12.1 %collective-permute-start.2 = (bf16[2,4,48,384]{3,2,1,0:T(8,128)(2,1)S(1)}, bf16[2,4,48,384]{3,2,1,0:T(8,128)(2,1)}, u32[]{:S(2)}, u32[]{:S(2)}) collective-permute-start(bf16[2,4,48,384]{3,2,1,0:T(8,128)(2,1)S(1)} %shard_map.47), channel_id=1, source_target_pairs={{0,1},{1,0},{2,3},{3,2},{4,5},{5,4},{6,7},{7,6},{8,9},{9,8},{10,11... | collective-permute-start | bytes 884744 | tf_op jit(solution)/shard_map/ppermute | solution.py:380
  25.0 12.0 %collective-permute-start.1 = (bf16[2,4,48,384]{3,2,1,0:T(8,128)(2,1)S(1)}, bf16[2,4,48,384]{3,2,1,0:T(8,128)(2,1)}, u32[]{:S(2)}, u32[]{:S(2)}) collective-permute-start(bf16[2,4,48,384]{3,2,1,0:T(8,128)(2,1)S(1)} %get-tuple-element.20), channel_id=1, source_target_pairs={{0,4},{1,2},{2,1},{3,7},{4,0},{5,6},{6,5},{7,3},{8,12},{9,10},{10,... | collective-permute-start | bytes 884744 | tf_op jit(solution)/shard_map/ppermute | solution.py:49
  30.8 16.5 %collective-permute-start.4 = (bf16[2,4,48,384]{3,2,1,0:T(8,128)(2,1)S(1)}, bf16[2,4,48,384]{3,2,1,0:T(8,128)(2,1)S(1)}, u32[]{:S(2)}, u32[]{:S(2)}) collective-permute-start(bf16[2,4,48,384]{3,2,1,0:T(8,128)(2,1)S(1)} %add.36), channel_id=1, source_target_pairs={{0,2},{1,3},{2,0},{3,1},{4,6},{5,7},{6,4},{7,5},{8,10},{9,11},{10,... | collective-permute-start | bytes 884744 | tf_op jit(solution)/shard_map/ppermute | solution.py:22

commit v9 on v8

--- a/solution.py
+++ b/solution.py
@@ -35,18 +35,6 @@
 
 def in_plane(shifts_ref, direction):
     return shifts_ref[jnp.where(direction == 3, 0, direction)]
-
-
-def middle_exchange(block):
-    lines, ring = lax.axis_size("ta"), lax.axis_size("site")
-    route = []
-    for line in range(lines):
-        beside = line ^ 1 if lines % 2 == 0 else line
-        for site in range(ring):
-            inner = 0 < site < ring - 1
-            target = line * ring + ring - 1 - site if inner else beside * ring + site
-            route.append((line * ring + site, target))
-    return lax.ppermute(block, ("ta", "site"), route)
 
 
 def mul(left, right):
@@ -373,8 +361,7 @@
     if not folded:
         arrived = [shifted(block, "site", offset + 1) for offset, block in enumerate(blocks)]
         return functools.reduce(lambda total, block: total + block.astype(jnp.float32), arrived, own)
-    near = middle_exchange(blocks[0])
-    near = jnp.where((me > 0) & (me < last), near, jnp.zeros_like(near))
+    near = lax.ppermute(blocks[0], "site", [(1, 2), (2, 1)])
     passed = lax.ppermute(blocks[0], "site", [(0, 1), (3, 2)])
     far = shifted(blocks[1] + passed, "site", 2)
     paired = lax.ppermute(blocks[2], "site", [(0, 1), (1, 0), (2, 3), (3, 2)])

time: 48.5 us -> 49.8 us (1.027)
  waiting for transfers between devices: 19.1 us -> 22.3 us
  other arithmetic: 4.79 us -> 2.82 us
    ppermute x2, waiting for transfers between devices: 16.2 us -> 19.4 us  [shifted(): lax.ppermute(block, axis, [(i, (i + distance) % count) for i in range(cou...]
    add x1, other arithmetic: 1.08 us -> 0.08 us  [local_work(): held = own + near.astype(jnp.float32) + paired.astype(jnp.float32)]
    add x1, other arithmetic: 1.04 us -> 0.07 us  [local_work(): far = shifted(blocks[1] + passed, 'site', 2)]
    ppermute x1, starting transfers between devices: 2.98 us -> 2.27 us  [local_work(): passed = lax.ppermute(blocks[0], 'site', [(0, 1), (3, 2)])]
    ppermute x1, starting transfers between devices: 0.07 us -> 0.68 us  [local_work(): near = lax.ppermute(blocks[0], 'site', [(1, 2), (2, 1)])]
  transfers between devices with their start and end apart: 5 -> 5, of which waited for: 3 -> 4; matrix products, arithmetic and copies ran while one was open for 10% -> 6% of each run, Pallas kernels for 16% -> 16%
where the time goes in v9:
time: 49.8 us; the launch traced here: 49.5 us
  waiting for transfers between devices  22.3 us (45%)
  starting transfers between devices  12.4 us (25%)
  Pallas kernels  10 us (20%)
  other arithmetic  2.82 us (6%)
  local copies, waits for them, and re-layouts  1.86 us (4%)
    ppermute x2, waiting for transfers between devices, shifted(): lax.ppermute(block, axis, [(i, (i + distance) % count) for i in range(cou...  19.4 us
    ppermute x2, starting transfers between devices, shifted(): lax.ppermute(block, axis, [(i, (i + distance) % count) for i in range(cou...  9.37 us
    pallas_call x3, Pallas kernels, local_work(): pl.pallas_call(functools.partial(block_kernel, number, layout), out_shape...  5.66 us
    ppermute x1, waiting for transfers between devices, local_work(): passed = lax.ppermute(blocks[0], 'site', [(0, 1), (3, 2)])  2.81 us
    ppermute x1, starting transfers between devices, local_work(): passed = lax.ppermute(blocks[0], 'site', [(0, 1), (3, 2)])  2.27 us
    pallas_call x1, Pallas kernels, local_work(): pl.pallas_call(functools.partial(first_kernel, layout), out_shape=(jax.Sh...  2.23 us
    pallas_call x1, Pallas kernels, local_work(): pl.pallas_call(functools.partial(early_kernel, layout, scale), out_shape=...  2.14 us
    unnamed x2, local copies, waits for them, and re-layouts  1.06 us
  transfers between devices with their start and end apart: 5, of which 4 were waited for; matrix products, arithmetic and copies ran while one was open for 6% of the time, Pallas kernels for 16%

profile of v9, /device:TPU:0, one launch (start us, length us, event | category | flops | bytes accessed | tf_op | source)
XLA Modules:
  0.0 49.5 jit_solution(7865032893956472709)
XLA Ops:
  0.0 5.1 %collective-permute-start = (bf16[2,3,192,256]{3,2,1,0:T(8,128)(2,1)}, bf16[2,3,192,256]{3,2,1,0:T(8,128)(2,1)S(1)}, u32[]{:S(2)}, u32[]{:S(2)}) collective-permute-start(bf16[2,3,192,256]{3,2,1,0:T(8,128)(2,1)} %bitcast.13), channel_id=1, source_target_pairs={{0,3},{1,0},{2,1},{3,2},{4,7},{5,4},{6,5},{7,6},{8,11},{9,8},{10,9... | collective-permute-start | bytes 1769480 | tf_op jit(solution)/shard_map/ppermute | solution.py:22
  5.1 0.8 %reshape.11 = s32[6]{0:T(128)S(1)} reshape(s32[2,3]{1,0:T(2,128)} %param.6) | data formatting | bytes 48 | tf_op jit(solution)/shard_map/reshape | solution.py:305
  5.8 0.8 %convert_bitcast_fusion = f32[3,3,3,2,1,256]{5,3,4,2,1,0:T(2,128)S(1)} fusion(bf16[2,3,3,3,1,256]{5,0,4,3,2,1:T(2,128)(2,1)} %param.5), kind=kLoop, calls=%fused_computation.7 | loop fusion | flops 13824 | bytes 82944 | tf_op jit(solution)/shard_map/reshape | solution.py:296
  6.7 0.1 add_multiply_fusion
  6.7 0.7 %pad_add_fusion.meta = s32[14]{0:T(128)S(1)} fusion(s32[4]{0:T(128)} %param.7, s32[6]{0:T(128)S(1)} %reshape.11, s32[4]{0:T(128)S(1)} %add_multiply_fusion), kind=kLoop, calls=%fused_computation.19 | loop fusion | flops 28 | bytes 112 | tf_op jit(solution)/shard_map/concatenate | solution.py:304
  7.5 0.2 select_convert_fusion.shifts_ref
  7.7 0.0 copy-start
  7.7 1.1 %copy-done = bf16[2,192,3,1,256]{4,1,3,2,0:T(8,128)(2,1)S(1)} copy-done((bf16[2,192,3,1,256]{4,1,3,2,0:T(8,128)(2,1)S(1)}, bf16[2,192,3,1,256]{4,1,3,2,0:T(8,128)(2,1)}, u32[]{:S(2)}) %copy-start) | copy-done | bytes 589848
  8.8 2.1 %early.1 = (bf16[2,384,768]{2,1,0:T(8,128)(2,1)S(1)}, f32[2,27,4,256]{3,2,1,0:T(4,128)S(1)}, bf16[2,2,3,192,256]{4,3,2,1,0:T(8,128)(2,1)S(1)}, f32[2,72,256]{2,1,0:T(8,128)S(1)}) custom-call(s32[14]{0:T(128)S(1)} %pad_add_fusion.meta, bf16[2,3,192,256]{3,2,1,0:T(8,128)(2,1)S(1)} %bitcast.14, f32[3,18,256]{2,1,0:T(8,128)S(1)} %reshape.16.links_ref, ...), custom_call_target="tpu_custom_call" | custom-call | flops 500000000 | bytes 4000000 | tf_op jit(solution)/shard_map/early/pallas_call | solution.py:323
  10.9 7.1 %collective-permute-done.next_ref = bf16[2,3,192,256]{3,2,1,0:T(8,128)(2,1)S(1)} collective-permute-done((bf16[2,3,192,256]{3,2,1,0:T(8,128)(2,1)}, bf16[2,3,192,256]{3,2,1,0:T(8,128)(2,1)S(1)}, u32[]{:S(2)}, u32[]{:S(2)}) %collective-permute-start) | collective-permute-done | bytes 589856 | tf_op jit(solution)/shard_map/ppermute | solution.py:22
  18.0 2.2 %first.1 = (bf16[2,384,768]{2,1,0:T(8,128)(2,1)S(1)}, f32[2,27,4,256]{3,2,1,0:T(4,128)S(1)}, bf16[2,2,3,192,256]{4,3,2,1,0:T(8,128)(2,1)S(1)}, bf16[2,4,48,384]{3,2,1,0:T(8,128)(2,1)S(1)}) custom-call(s32[14]{0:T(128)S(1)} %pad_add_fusion.meta, ...), custom_call_target="tpu_custom_call", output_to_operand_aliasing={{0}: (3, {}), {1}: (4, {}), {2}: (5, {})} | custom-call | tf_op jit(solution)/shard_map/first/pallas_call | solution.py:332
  20.2 2.3 %collective-permute-start.3 = (bf16[2,4,48,384]{3,2,1,0:T(8,128)(2,1)S(1)}, bf16[2,4,48,384]{3,2,1,0:T(8,128)(2,1)S(1)}, u32[]{:S(2)}, u32[]{:S(2)}) collective-permute-start(bf16[2,4,48,384]{3,2,1,0:T(8,128)(2,1)S(1)} %get-tuple-element.20), channel_id=1, source_target_pairs={{0,1},{3,2},{4,5},{7,6},{8,9},{11,10},{12,13},{15,14},{16,17},{19,... | collective-permute-start | bytes 884744 | tf_op jit(solution)/shard_map/ppermute | solution.py:365
  22.5 1.9 %shard_map.47 = bf16[2,4,48,384]{3,2,1,0:T(8,128)(2,1)S(1)} custom-call(s32[14]{0:T(128)S(1)} %pad_add_fusion.meta, bf16[2,2,3,192,256]{4,3,2,1,0:T(8,128)(2,1)S(1)} %get-tuple-element.17.mids_ref, bf16[2,384,768]{2,1,0:T(8,128)(2,1)S(1)} %get-tuple-element.18.right_ref, f32[2,27,4,256]{3,2,1,0:T(4,128)S(1)} %get-tuple-element.19.matrices_ref), custom_call_target="tpu_custom_call" | custom-call | flops 1000000000 | bytes 4000000 | tf_op jit(solution)/shard_map/pallas_call | solution.py:350
  24.4 0.1 collective-permute-start.2
  24.5 0.7 %collective-permute-start.1 = (bf16[2,4,48,384]{3,2,1,0:T(8,128)(2,1)S(1)}, bf16[2,4,48,384]{3,2,1,0:T(8,128)(2,1)S(1)}, u32[]{:S(2)}, u32[]{:S(2)}) collective-permute-start(bf16[2,4,48,384]{3,2,1,0:T(8,128)(2,1)S(1)} %get-tuple-element.20), channel_id=1, source_target_pairs={{1,2},{2,1},{5,6},{6,5},{9,10},{10,9},{13,14},{14,13},{17,18},{18,... | collective-permute-start | bytes 884744 | tf_op jit(solution)/shard_map/ppermute | solution.py:364
  25.2 1.9 %shard_map.48 = bf16[2,4,48,384]{3,2,1,0:T(8,128)(2,1)S(1)} custom-call(s32[14]{0:T(128)S(1)} %pad_add_fusion.meta, bf16[2,2,3,192,256]{4,3,2,1,0:T(8,128)(2,1)S(1)} %get-tuple-element.17.mids_ref, bf16[2,384,768]{2,1,0:T(8,128)(2,1)S(1)} %get-tuple-element.18.right_ref, f32[2,27,4,256]{3,2,1,0:T(4,128)S(1)} %get-tuple-element.19.matrices_ref), custom_call_target="tpu_custom_call" | custom-call | flops 1000000000 | bytes 4000000 | tf_op jit(solution)/shard_map/pallas_call | solution.py:350
  27.1 2.8 %collective-permute-done.3 = bf16[2,4,48,384]{3,2,1,0:T(8,128)(2,1)S(1)} collective-permute-done((bf16[2,4,48,384]{3,2,1,0:T(8,128)(2,1)S(1)}, bf16[2,4,48,384]{3,2,1,0:T(8,128)(2,1)S(1)}, u32[]{:S(2)}, u32[]{:S(2)}) %collective-permute-start.3) | collective-permute-done | bytes 294944 | tf_op jit(solution)/shard_map/ppermute | solution.py:365
  29.9 0.1 add.36
  29.9 4.3 %collective-permute-start.4 = (bf16[2,4,48,384]{3,2,1,0:T(8,128)(2,1)S(1)}, bf16[2,4,48,384]{3,2,1,0:T(8,128)(2,1)S(1)}, u32[]{:S(2)}, u32[]{:S(2)}) collective-permute-start(bf16[2,4,48,384]{3,2,1,0:T(8,128)(2,1)S(1)} %add.36), channel_id=1, source_target_pairs={{0,2},{1,3},{2,0},{3,1},{4,6},{5,7},{6,4},{7,5},{8,10},{9,11},{10,... | collective-permute-start | bytes 884744 | tf_op jit(solution)/shard_map/ppermute | solution.py:22
  34.2 1.9 %shard_map.46 = f32[2,4,48,384]{3,2,1,0:T(8,128)S(1)} custom-call(s32[14]{0:T(128)S(1)} %pad_add_fusion.meta, bf16[2,2,3,192,256]{4,3,2,1,0:T(8,128)(2,1)S(1)} %get-tuple-element.17.mids_ref, bf16[2,384,768]{2,1,0:T(8,128)(2,1)S(1)} %get-tuple-element.18.right_ref, f32[2,27,4,256]{3,2,1,0:T(4,128)S(1)} %get-tuple-element.19.matrices_ref), custom_call_target="tpu_custom_call" | custom-call | flops 1000000000 | bytes 4000000 | tf_op jit(solution)/shard_map/pallas_call | solution.py:350
  36.1 0.1 collective-permute-done.2
  36.2 0.0 collective-permute-done.1
  36.2 0.1 convert_add_fusion.1
  36.3 12.4 %collective-permute-done.4 = bf16[2,4,48,384]{3,2,1,0:T(8,128)(2,1)S(1)} collective-permute-done((bf16[2,4,48,384]{3,2,1,0:T(8,128)(2,1)S(1)}, bf16[2,4,48,384]{3,2,1,0:T(8,128)(2,1)S(1)}, u32[]{:S(2)}, u32[]{:S(2)}) %collective-permute-start.4) | collective-permute-done | bytes 294944 | tf_op jit(solution)/shard_map/ppermute | solution.py:22
  48.6 0.9 %convert_add_fusion = f32[2,4,48,384]{3,2,1,0:T(8,128)} fusion(f32[2,4,48,384]{3,2,1,0:T(8,128)S(1)} %convert_add_fusion.1, bf16[2,4,48,384]{3,2,1,0:T(8,128)(2,1)S(1)} %collective-permute-done.4), kind=kLoop, calls=%fused_computation.5 | loop fusion | flops 294912 | bytes 1474560 | tf_op jit(solution)/shard_map/add | solution.py:370
  (5 shorter events, 0.1 us)
Async XLA Ops:
  0.0 18.0 %collective-permute-start = (bf16[2,3,192,256]{3,2,1,0:T(8,128)(2,1)}, bf16[2,3,192,256]{3,2,1,0:T(8,128)(2,1)S(1)}, u32[]{:S(2)}, u32[]{:S(2)}) collective-permute-start(bf16[2,3,192,256]{3,2,1,0:T(8,128)(2,1)} %bitcast.13), channel_id=1, source_target_pairs={{0,3},{1,0},{2,1},{3,2},{4,7},{5,4},{6,5},{7,6},{8,11},{9,8},{10,9... | collective-permute-start | bytes 1769480 | tf_op jit(solution)/shard_map/ppermute | solution.py:22
  7.7 1.1 %copy-start = (bf16[2,192,3,1,256]{4,1,3,2,0:T(8,128)(2,1)S(1)}, bf16[2,192,3,1,256]{4,1,3,2,0:T(8,128)(2,1)}, u32[]{:S(2)}) copy-start(bf16[2,192,3,1,256]{4,1,3,2,0:T(8,128)(2,1)} %param.4) | copy-start | bytes 1769476
  20.2 9.6 %collective-permute-start.3 = (bf16[2,4,48,384]{3,2,1,0:T(8,128)(2,1)S(1)}, bf16[2,4,48,384]{3,2,1,0:T(8,128)(2,1)S(1)}, u32[]{:S(2)}, u32[]{:S(2)}) collective-permute-start(bf16[2,4,48,384]{3,2,1,0:T(8,128)(2,1)S(1)} %get-tuple-element.20), channel_id=1, source_target_pairs={{0,1},{3,2},{4,5},{7,6},{8,9},{11,10},{12,13},{15,14},{16,17},{19,... | collective-permute-start | bytes 884744 | tf_op jit(solution)/shard_map/ppermute | solution.py:365
  24.4 11.8 %collective-permute-start.2 = (bf16[2,4,48,384]{3,2,1,0:T(8,128)(2,1)S(1)}, bf16[2,4,48,384]{3,2,1,0:T(8,128)(2,1)S(1)}, u32[]{:S(2)}, u32[]{:S(2)}) collective-permute-start(bf16[2,4,48,384]{3,2,1,0:T(8,128)(2,1)S(1)} %shard_map.47), channel_id=1, source_target_pairs={{0,1},{1,0},{2,3},{3,2},{4,5},{5,4},{6,7},{7,6},{8,9},{9,8},{10,11... | collective-permute-start | bytes 884744 | tf_op jit(solution)/shard_map/ppermute | solution.py:367
  24.5 11.7 %collective-permute-start.1 = (bf16[2,4,48,384]{3,2,1,0:T(8,128)(2,1)S(1)}, bf16[2,4,48,384]{3,2,1,0:T(8,128)(2,1)S(1)}, u32[]{:S(2)}, u32[]{:S(2)}) collective-permute-start(bf16[2,4,48,384]{3,2,1,0:T(8,128)(2,1)S(1)} %get-tuple-element.20), channel_id=1, source_target_pairs={{1,2},{2,1},{5,6},{6,5},{9,10},{10,9},{13,14},{14,13},{17,18},{18,... | collective-permute-start | bytes 884744 | tf_op jit(solution)/shard_map/ppermute | solution.py:364
  29.9 18.7 %collective-permute-start.4 = (bf16[2,4,48,384]{3,2,1,0:T(8,128)(2,1)S(1)}, bf16[2,4,48,384]{3,2,1,0:T(8,128)(2,1)S(1)}, u32[]{:S(2)}, u32[]{:S(2)}) collective-permute-start(bf16[2,4,48,384]{3,2,1,0:T(8,128)(2,1)S(1)} %add.36), channel_id=1, source_target_pairs={{0,2},{1,3},{2,0},{3,1},{4,6},{5,7},{6,4},{7,5},{8,10},{9,11},{10,... | collective-permute-start | bytes 884744 | tf_op jit(solution)/shard_map/ppermute | solution.py:22
